TPU v7x, 32 devices: a whole 2x2x4 slice. The times are simulated.
32 devices in a mesh: dp: 16 (over z, y, x), tensor: 2 (over core).
Axes of the slice: x: 2, y: 2, z: 4, core: 2. Of those that a mesh axis runs over, the one named last changes fastest.
Arguments:
- inputs: bfloat16 [4096, 768], P(('dp', 'tensor')), may hold values from -6 to 6
- neighbours: bfloat16 [96, 128, 768], P(('dp', 'tensor')), may hold values from -6 to 6
- nbr_index: int32 [64, 2], P('dp'), may hold values from 0 to 5
- ln1_gain: float32 [768], P('dp'), may hold values from 0.25 to 1.75
- ln1_bias: float32 [768], P('dp'), may hold values from -1.5 to 1.5
- ln2_gain: float32 [768], P('dp'), may hold values from 0.25 to 1.75
- ln2_bias: float32 [768], P('dp'), may hold values from -1.5 to 1.5
- ln3_gain: float32 [768], P('dp'), may hold values from 0.25 to 1.75
- ln3_bias: float32 [768], P('dp'), may hold values from -1.5 to 1.5
- w_query: float32 [768, 768], P('dp', 'tensor'), may hold values from -0.21875 to 0.21875
- w_key: float32 [768, 768], P('dp', 'tensor'), may hold values from -0.21875 to 0.21875
- w_value: float32 [768, 768], P('dp', 'tensor'), may hold values from -0.21875 to 0.21875
- c_query: float32 [768, 768], P('dp', 'tensor'), may hold values from -0.21875 to 0.21875
- c_key: float32 [768, 768], P('dp', 'tensor'), may hold values from -0.21875 to 0.21875
- c_value: float32 [768, 768], P('dp', 'tensor'), may hold values from -0.21875 to 0.21875
- w_up: float32 [768, 3072], P('dp', 'tensor'), may hold values from -0.21875 to 0.21875
- w_out: float32 [768, 768], P('tensor', 'dp'), may hold values from -0.875 to 0.875
- c_out: float32 [768, 768], P('tensor', 'dp'), may hold values from -0.875 to 0.875
- w_down: float32 [3072, 768], P('tensor', 'dp'), may hold values from -0.109375 to 0.109375
- cotangent: bfloat16 [4096, 768], P(('dp', 'tensor')), may hold values from -6 to 6
Outputs:
- result: bfloat16 [4096, 768], P(('dp', 'tensor'))
- d_inputs: float32 [4096, 768], P(('dp', 'tensor'))
- d_neighbours: float32 [96, 128, 768], P(('dp', 'tensor'))
- d_ln1_gain: float32 [768], P('dp')
- d_ln1_bias: float32 [768], P('dp')
- d_ln2_gain: float32 [768], P('dp')
- d_ln2_bias: float32 [768], P('dp')
- d_ln3_gain: float32 [768], P('dp')
- d_ln3_bias: float32 [768], P('dp')
- d_w_query: float32 [768, 768], P('dp', 'tensor')
- d_w_key: float32 [768, 768], P('dp', 'tensor')
- d_w_value: float32 [768, 768], P('dp', 'tensor')
- d_c_query: float32 [768, 768], P('dp', 'tensor')
- d_c_key: float32 [768, 768], P('dp', 'tensor')
- d_c_value: float32 [768, 768], P('dp', 'tensor')
- d_w_up: float32 [768, 3072], P('dp', 'tensor')
- d_w_out: float32 [768, 768], P('tensor', 'dp')
- d_c_out: float32 [768, 768], P('tensor', 'dp')
- d_w_down: float32 [3072, 768], P('tensor', 'dp')
Inputs may be any that keep to these rules, and one draw needn't show every extreme that they name: `nbr_index`: row s * 4 + c names two neighbours (they may coincide) of sequence s, counted from 0 within that sequence's 6.
All inputs are finite; a program needn't handle non-finite values.
Results may differ from a plain program's by a relative error of at most 0.03.
Values may be sent and summed in bfloat16 or wider, within the bound.
No kernel may reach another device: no remote copies, remote signals or barrier semaphores. Data moves between devices by JAX's collectives and lax.ppermute only.
A program may use at most 128 MiB of HBM per device.

v0:
```python
import jax
import jax.numpy as jnp
from jax import lax
from jax.sharding import PartitionSpec as P

D = 768
HEAD_DIM = 64
GROUP = 64
NBR_LEN = 128
NBRS = 2


HIGHEST_MODE = lax.Precision.HIGHEST
NEG_FILL = -1e30


def product(left, right):
    return jnp.dot(left, right, preferred_element_type=jnp.float32)


def outer_sum(left, right):
    return lax.dot_general(
        left, right, (((0,), (0,)), ((), ())), preferred_element_type=jnp.float32
    )


def back_product(left, right):
    return lax.dot_general(
        left, right, (((1,), (1,)), ((), ())), preferred_element_type=jnp.float32
    )


def layer_norm(stream, gain, shift):
    center = stream - jnp.mean(stream, axis=-1, keepdims=True)
    spread = jnp.mean(center * center, axis=-1, keepdims=True)
    return center * lax.rsqrt(spread + 1e-05) * gain + shift


def rotate(heads_in, direction):
    count_rows = heads_in.shape[0]
    halfway = heads_in.shape[-1] // 2
    frequency = jnp.power(10000.0, -jnp.arange(halfway, dtype=jnp.float32) / halfway)
    angles = jnp.arange(count_rows, dtype=jnp.float32)[:, None] * frequency[None, :]
    cosine = jnp.cos(angles)[:, None, :]
    sine_part = direction * jnp.sin(angles)[:, None, :]
    leading = heads_in[..., :halfway]
    trailing = heads_in[..., halfway:]
    return jnp.concatenate(
        [leading * cosine - trailing * sine_part, trailing * cosine + leading * sine_part], axis=-1
    )


def gelu_tanh(pre_act):
    return (
        0.5
        * pre_act
        * (1.0 + jnp.tanh(0.7978845608028654 * (pre_act + 0.044715 * pre_act * pre_act * pre_act)))
    )


def spread_rows(normed):
    return lax.all_gather(normed.astype(jnp.bfloat16), "tensor", axis=0, tiled=True)


def gather_grad(grad_in):
    return lax.all_gather(grad_in.astype(jnp.bfloat16), "tensor", axis=0, tiled=True)


def branch_total(partial_out):
    return lax.psum_scatter(
        partial_out.astype(jnp.bfloat16), "tensor", scatter_dimension=0, tiled=True
    ).astype(jnp.float32)


def grad_total(partial_grad):
    return lax.psum_scatter(
        partial_grad.astype(jnp.bfloat16), "tensor", scatter_dimension=0, tiled=True
    ).astype(jnp.float32)


def block_bounds(count_rows):
    block_rows = min(512, count_rows)
    return [(0, min(block_rows, count_rows))]


def masked_scores(block_queries, keys_part, first_row, score_scale):
    block_rows = block_queries.shape[0]
    scores = (
        jnp.einsum("qhd,khd->hqk", block_queries, keys_part, preferred_element_type=jnp.float32)
        * score_scale
    )
    query_pos = first_row + jnp.arange(block_rows, dtype=jnp.int32)
    key_pos = jnp.arange(keys_part.shape[0], dtype=jnp.int32)
    allowed = query_pos[:, None] >= key_pos[None, :]
    return jnp.where(allowed[None], scores, NEG_FILL)


def causal_forward(queries, keys_all, values_all, score_scale):
    count_rows, heads_local, head_width = queries.shape
    mixtures = []
    logsums = []
    for start, stop in block_bounds(count_rows):
        scores = masked_scores(queries, keys_all, start, score_scale)
        highest = jnp.max(scores, axis=-1, keepdims=True)
        raised = jnp.exp(scores - highest)
        totals = jnp.sum(raised, axis=-1, keepdims=True)
        attend = (raised / totals).astype(jnp.bfloat16)
        mixture = jnp.einsum("hqk,khd->qhd", attend, values_all, preferred_element_type=jnp.float32)
        mixtures.append(mixture.astype(jnp.bfloat16))
        logsums.append(highest + jnp.log(totals))
    mixture = mixtures[0]
    return (mixture.reshape(count_rows, heads_local * head_width), logsums)


def causal_backward(queries, keys_all, values_all, logsums, grad_mixture, score_scale):
    count_rows, heads_local, head_width = queries.shape
    grad_keys = jnp.zeros(keys_all.shape, jnp.float32)
    grad_values = jnp.zeros(keys_all.shape, jnp.float32)
    grad_pieces = []
    for turn, (start, stop) in enumerate(block_bounds(count_rows)):
        scores = masked_scores(queries, keys_all, start, score_scale)
        attend = jnp.exp(scores - logsums[turn])
        attend_low = attend.astype(jnp.bfloat16)
        grad_values = grad_values.at[:stop].add(
            jnp.einsum("hqk,qhd->khd", attend_low, grad_mixture, preferred_element_type=jnp.float32)
        )
        grad_attend = jnp.einsum(
            "qhd,khd->hqk", grad_mixture, values_all, preferred_element_type=jnp.float32
        )
        inner = jnp.sum(attend * grad_attend, axis=-1, keepdims=True)
        grad_scores = (attend * (grad_attend - inner)).astype(jnp.bfloat16)
        grad_pieces.append(
            jnp.einsum("hqk,khd->qhd", grad_scores, keys_all, preferred_element_type=jnp.float32)
            * score_scale
        )
        grad_keys = grad_keys.at[:stop].add(
            jnp.einsum("hqk,qhd->khd", grad_scores, queries, preferred_element_type=jnp.float32)
            * score_scale
        )
    grad_queries = grad_pieces[0]
    return (grad_queries, grad_keys, grad_values)


def cross_forward(cqueries, ckeys, cvalues, score_scale):
    scores = (
        jnp.einsum("cqhd,ckhd->chqk", cqueries, ckeys, preferred_element_type=jnp.float32)
        * score_scale
    )
    highest = jnp.max(scores, axis=-1, keepdims=True)
    raised = jnp.exp(scores - highest)
    totals = jnp.sum(raised, axis=-1, keepdims=True)
    attend = (raised / totals).astype(jnp.bfloat16)
    mixture = jnp.einsum("chqk,ckhd->cqhd", attend, cvalues, preferred_element_type=jnp.float32)
    return (mixture.astype(jnp.bfloat16), highest + jnp.log(totals))


def cross_backward(cqueries, ckeys, cvalues, logsum, grad_mixture, score_scale):
    scores = (
        jnp.einsum("cqhd,ckhd->chqk", cqueries, ckeys, preferred_element_type=jnp.float32)
        * score_scale
    )
    attend = jnp.exp(scores - logsum)
    attend_low = attend.astype(jnp.bfloat16)
    grad_values = jnp.einsum(
        "chqk,cqhd->ckhd", attend_low, grad_mixture, preferred_element_type=jnp.float32
    )
    grad_attend = jnp.einsum(
        "cqhd,ckhd->chqk", grad_mixture, cvalues, preferred_element_type=jnp.float32
    )
    inner = jnp.sum(attend * grad_attend, axis=-1, keepdims=True)
    grad_scores = (attend * (grad_attend - inner)).astype(jnp.bfloat16)
    grad_queries = (
        jnp.einsum("chqk,ckhd->cqhd", grad_scores, ckeys, preferred_element_type=jnp.float32)
        * score_scale
    )
    grad_keys = (
        jnp.einsum("chqk,cqhd->ckhd", grad_scores, cqueries, preferred_element_type=jnp.float32)
        * score_scale
    )
    return (grad_queries, grad_keys, grad_values)


def on_device(
    inputs,
    neighbours,
    nbr_index,
    ln1_gain,
    ln1_bias,
    ln2_gain,
    ln2_bias,
    ln3_gain,
    ln3_bias,
    w_query,
    w_key,
    w_value,
    c_query,
    c_key,
    c_value,
    w_up,
    w_out,
    c_out,
    w_down,
    cotangent,
):
    masters = (
        ln1_gain,
        ln1_bias,
        ln2_gain,
        ln2_bias,
        ln3_gain,
        ln3_bias,
        w_query,
        w_key,
        w_value,
        c_query,
        c_key,
        c_value,
        w_up,
        w_out,
        c_out,
        w_down,
    )
    shards = tuple((master.astype(jnp.bfloat16) for master in masters))
    fetched = (
        lax.all_gather(shards[0], "dp", axis=0, tiled=True),
        lax.all_gather(shards[1], "dp", axis=0, tiled=True),
        lax.all_gather(shards[2], "dp", axis=0, tiled=True),
        lax.all_gather(shards[3], "dp", axis=0, tiled=True),
        lax.all_gather(shards[4], "dp", axis=0, tiled=True),
        lax.all_gather(shards[5], "dp", axis=0, tiled=True),
        lax.all_gather(shards[6], "dp", axis=0, tiled=True),
        lax.all_gather(shards[7], "dp", axis=0, tiled=True),
        lax.all_gather(shards[8], "dp", axis=0, tiled=True),
        lax.all_gather(shards[9], "dp", axis=0, tiled=True),
        lax.all_gather(shards[10], "dp", axis=0, tiled=True),
        lax.all_gather(shards[11], "dp", axis=0, tiled=True),
        lax.all_gather(shards[12], "dp", axis=0, tiled=True),
        lax.all_gather(shards[13], "dp", axis=1, tiled=True),
        lax.all_gather(shards[14], "dp", axis=1, tiled=True),
        lax.all_gather(shards[15], "dp", axis=1, tiled=True),
    )
    (
        gain_one,
        shift_one,
        gain_two,
        shift_two,
        gain_three,
        shift_three,
        query_w,
        key_w,
        value_w,
        cquery_w,
        ckey_w,
        cvalue_w,
        up_w,
        out_w,
        cout_w,
        down_w,
    ) = fetched
    score_scale = HEAD_DIM ** (-0.5)
    stream = inputs.astype(jnp.float32)
    normed_one, norm_back_one = jax.vjp(
        layer_norm, stream, gain_one.astype(jnp.float32), shift_one.astype(jnp.float32)
    )
    self_rows = spread_rows(normed_one)
    seq_rows = self_rows.shape[0]
    heads_local = query_w.shape[1] // HEAD_DIM
    queries = rotate(
        product(self_rows, query_w).reshape(seq_rows, heads_local, HEAD_DIM), 1.0
    ).astype(jnp.bfloat16)
    keys_all = rotate(
        product(self_rows, key_w).reshape(seq_rows, heads_local, HEAD_DIM), 1.0
    ).astype(jnp.bfloat16)
    values_all = (
        product(self_rows, value_w).astype(jnp.bfloat16).reshape(seq_rows, heads_local, HEAD_DIM)
    )
    mixture, logsums = causal_forward(queries, keys_all, values_all, score_scale)
    after_self = stream + branch_total(product(mixture, out_w))
    normed_two, norm_back_two = jax.vjp(
        layer_norm, after_self, gain_two.astype(jnp.float32), shift_two.astype(jnp.float32)
    )
    cross_rows = spread_rows(normed_two)
    group_count = seq_rows // GROUP
    cqueries = (
        product(cross_rows, cquery_w)
        .astype(jnp.bfloat16)
        .reshape(group_count, GROUP, heads_local, HEAD_DIM)
    )
    pool_all = lax.all_gather(neighbours, "tensor", axis=0, tiled=True)
    pool_count = pool_all.shape[0]
    pool_flat = pool_all.reshape(pool_count * NBR_LEN, D)
    ckeys = product(pool_flat, ckey_w).astype(jnp.bfloat16)
    cvalues = product(pool_flat, cvalue_w).astype(jnp.bfloat16)
    chosen = nbr_index.reshape(-1)
    chosen_keys = ckeys.reshape(pool_count, -1)[chosen].reshape(
        group_count, NBRS * NBR_LEN, heads_local, HEAD_DIM
    )
    chosen_values = cvalues.reshape(pool_count, -1)[chosen].reshape(
        group_count, NBRS * NBR_LEN, heads_local, HEAD_DIM
    )
    cmixture, clogsum = cross_forward(cqueries, chosen_keys, chosen_values, score_scale)
    cmixture = cmixture.reshape(seq_rows, heads_local * HEAD_DIM)
    after_cross = after_self + branch_total(product(cmixture, cout_w))
    normed_three, norm_back_three = jax.vjp(
        layer_norm, after_cross, gain_three.astype(jnp.float32), shift_three.astype(jnp.float32)
    )
    mlp_rows = spread_rows(normed_three)
    pre_act = product(mlp_rows, up_w)
    activated, gelu_back = jax.vjp(gelu_tanh, pre_act)
    act_low = activated.astype(jnp.bfloat16)
    result = after_cross + branch_total(product(act_low, down_w))
    refetched = (
        lax.all_gather(shards[0], "dp", axis=0, tiled=True),
        lax.all_gather(shards[1], "dp", axis=0, tiled=True),
        lax.all_gather(shards[2], "dp", axis=0, tiled=True),
        lax.all_gather(shards[3], "dp", axis=0, tiled=True),
        lax.all_gather(shards[4], "dp", axis=0, tiled=True),
        lax.all_gather(shards[5], "dp", axis=0, tiled=True),
        lax.all_gather(shards[6], "dp", axis=0, tiled=True),
        lax.all_gather(shards[7], "dp", axis=0, tiled=True),
        lax.all_gather(shards[8], "dp", axis=0, tiled=True),
        lax.all_gather(shards[9], "dp", axis=0, tiled=True),
        lax.all_gather(shards[10], "dp", axis=0, tiled=True),
        lax.all_gather(shards[11], "dp", axis=0, tiled=True),
        lax.all_gather(shards[12], "dp", axis=0, tiled=True),
        lax.all_gather(shards[13], "dp", axis=1, tiled=True),
        lax.all_gather(shards[14], "dp", axis=1, tiled=True),
        lax.all_gather(shards[15], "dp", axis=1, tiled=True),
    )
    query_w, key_w, value_w = (refetched[6], refetched[7], refetched[8])
    cquery_w, ckey_w, cvalue_w = (refetched[9], refetched[10], refetched[11])
    up_w, out_w, cout_w, down_w = (refetched[12], refetched[13], refetched[14], refetched[15])
    grad_out = cotangent.astype(jnp.float32)
    grad_full = gather_grad(grad_out)
    grad_down = outer_sum(act_low, grad_full)
    grad_act = back_product(grad_full, down_w)
    grad_pre = gelu_back(grad_act)[0].astype(jnp.bfloat16)
    grad_up = outer_sum(mlp_rows, grad_pre)
    grad_stream, grad_gain_three, grad_shift_three = norm_back_three(
        grad_total(back_product(grad_pre, up_w))
    )
    grad_cross_out = grad_out + grad_stream
    grad_full = gather_grad(grad_cross_out)
    grad_cout = outer_sum(cmixture, grad_full)
    grad_cmix = (
        back_product(grad_full, cout_w)
        .astype(jnp.bfloat16)
        .reshape(group_count, GROUP, heads_local, HEAD_DIM)
    )
    grad_cq, grad_ck, grad_cv = cross_backward(
        cqueries, chosen_keys, chosen_values, clogsum, grad_cmix, score_scale
    )
    grad_cq_low = grad_cq.reshape(seq_rows, heads_local * HEAD_DIM).astype(jnp.bfloat16)
    grad_cquery = outer_sum(cross_rows, grad_cq_low)
    picks = (jnp.arange(pool_count, dtype=jnp.int32)[:, None] == chosen[None, :]).astype(
        jnp.float32
    )
    pool_dkey = (
        jnp.dot(
            picks,
            grad_ck.reshape(group_count * NBRS, -1),
            precision=HIGHEST_MODE,
            preferred_element_type=jnp.float32,
        )
        .reshape(pool_count * NBR_LEN, -1)
        .astype(jnp.bfloat16)
    )
    pool_dvalue = (
        jnp.dot(
            picks,
            grad_cv.reshape(group_count * NBRS, -1),
            precision=HIGHEST_MODE,
            preferred_element_type=jnp.float32,
        )
        .reshape(pool_count * NBR_LEN, -1)
        .astype(jnp.bfloat16)
    )
    grad_ckey = outer_sum(pool_flat, pool_dkey)
    grad_cvalue = outer_sum(pool_flat, pool_dvalue)
    pool_partial = back_product(pool_dkey, ckey_w) + back_product(pool_dvalue, cvalue_w)
    grad_pool = lax.psum_scatter(
        pool_partial.reshape(pool_count, NBR_LEN, D).astype(jnp.bfloat16),
        "tensor",
        scatter_dimension=0,
        tiled=True,
    ).astype(jnp.float32)
    grad_stream, grad_gain_two, grad_shift_two = norm_back_two(
        grad_total(back_product(grad_cq_low, cquery_w))
    )
    grad_self_out = grad_cross_out + grad_stream
    grad_full = gather_grad(grad_self_out)
    grad_wout = outer_sum(mixture, grad_full)
    grad_mix = (
        back_product(grad_full, out_w).astype(jnp.bfloat16).reshape(seq_rows, heads_local, HEAD_DIM)
    )
    grad_queries, grad_keys, grad_values = causal_backward(
        queries, keys_all, values_all, logsums, grad_mix, score_scale
    )
    query_low = rotate(grad_queries, -1.0).reshape(seq_rows, -1).astype(jnp.bfloat16)
    key_low = rotate(grad_keys, -1.0).reshape(seq_rows, -1).astype(jnp.bfloat16)
    value_low = grad_values.reshape(seq_rows, -1).astype(jnp.bfloat16)
    grad_query = outer_sum(self_rows, query_low)
    grad_key = outer_sum(self_rows, key_low)
    grad_value = outer_sum(self_rows, value_low)
    partial_grad = (
        back_product(query_low, query_w)
        + back_product(key_low, key_w)
        + back_product(value_low, value_w)
    )
    grad_stream, grad_gain_one, grad_shift_one = norm_back_one(grad_total(partial_grad))
    grad_input = grad_self_out + grad_stream
    norm_sums = lax.psum(
        (
            grad_gain_one,
            grad_shift_one,
            grad_gain_two,
            grad_shift_two,
            grad_gain_three,
            grad_shift_three,
        ),
        "tensor",
    )
    summed = (
        lax.psum_scatter(norm_sums[0], "dp", scatter_dimension=0, tiled=True),
        lax.psum_scatter(norm_sums[1], "dp", scatter_dimension=0, tiled=True),
        lax.psum_scatter(norm_sums[2], "dp", scatter_dimension=0, tiled=True),
        lax.psum_scatter(norm_sums[3], "dp", scatter_dimension=0, tiled=True),
        lax.psum_scatter(norm_sums[4], "dp", scatter_dimension=0, tiled=True),
        lax.psum_scatter(norm_sums[5], "dp", scatter_dimension=0, tiled=True),
        lax.psum_scatter(grad_query, "dp", scatter_dimension=0, tiled=True),
        lax.psum_scatter(grad_key, "dp", scatter_dimension=0, tiled=True),
        lax.psum_scatter(grad_value, "dp", scatter_dimension=0, tiled=True),
        lax.psum_scatter(grad_cquery, "dp", scatter_dimension=0, tiled=True),
        lax.psum_scatter(grad_ckey, "dp", scatter_dimension=0, tiled=True),
        lax.psum_scatter(grad_cvalue, "dp", scatter_dimension=0, tiled=True),
        lax.psum_scatter(grad_up, "dp", scatter_dimension=0, tiled=True),
        lax.psum_scatter(grad_wout, "dp", scatter_dimension=1, tiled=True),
        lax.psum_scatter(grad_cout, "dp", scatter_dimension=1, tiled=True),
        lax.psum_scatter(grad_down, "dp", scatter_dimension=1, tiled=True),
    )
    return (
        result.astype(jnp.bfloat16),
        grad_input,
        grad_pool,
        summed[0],
        summed[1],
        summed[2],
        summed[3],
        summed[4],
        summed[5],
        summed[6],
        summed[7],
        summed[8],
        summed[9],
        summed[10],
        summed[11],
        summed[12],
        summed[13],
        summed[14],
        summed[15],
    )


def solution(mesh):
    return jax.shard_map(
        on_device,
        mesh=mesh,
        in_specs=(
            P(("dp", "tensor"), None),
            P(("dp", "tensor"), None, None),
            P("dp", None),
            P("dp"),
            P("dp"),
            P("dp"),
            P("dp"),
            P("dp"),
            P("dp"),
            P("dp", "tensor"),
            P("dp", "tensor"),
            P("dp", "tensor"),
            P("dp", "tensor"),
            P("dp", "tensor"),
            P("dp", "tensor"),
            P("dp", "tensor"),
            P("tensor", "dp"),
            P("tensor", "dp"),
            P("tensor", "dp"),
            P(("dp", "tensor"), None),
        ),
        out_specs=(
            P(("dp", "tensor"), None),
            P(("dp", "tensor"), None),
            P(("dp", "tensor"), None, None),
            P("dp"),
            P("dp"),
            P("dp"),
            P("dp"),
            P("dp"),
            P("dp"),
            P("dp", "tensor"),
            P("dp", "tensor"),
            P("dp", "tensor"),
            P("dp", "tensor"),
            P("dp", "tensor"),
            P("dp", "tensor"),
            P("dp", "tensor"),
            P("tensor", "dp"),
            P("tensor", "dp"),
            P("tensor", "dp"),
        ),
        check_vma=False,
    )
```

profile of v0, /device:TPU:0, one launch (start us, length us, event | category | flops | bytes accessed | tf_op | source)
XLA Modules:
  0.0 2035.7 jit_solution(16744224647910826540)
XLA Ops:
  17.6 78.6 %all-reduce.14 = (bf16[768]{0:T(1024)(128)(2,1)S(1)}, bf16[768]{0:T(1024)(128)(2,1)S(1)}, bf16[768]{0:T(1024)(128)(2,1)S(1)}, bf16[768]{0:T(1024)(128)(2,1)S(1)}...) all-reduce(bf16[768]{0:T(1024)(128)(2,1)S(1)} %dynamic-update-slice.5, ...), channel_id=1, replica_groups=mesh['dp'=16,'tensor'=2] {'dp'}, use_global_device_ids=true, to_apply=%add.1 | all-reduce | flops 4608 | bytes 18432
  103.8 38.6 %all_gather.85 = bf16[384,768]{0,1:T(8,128)(2,1)S(1)} all-gather(bf16[384,48]{0,1:T(8,128)(2,1)S(1)} %convert_element_type.246), channel_id=1, replica_groups=mesh['dp'=16,'tensor'=2] {'dp'}, dimensions={1}, use_global_device_ids=true | all-gather | bytes 626688 | tf_op jit(solution)/shard_map/all_gather | solution.py:238
  142.3 41.1 %all_gather.82 = bf16[768,384]{1,0:T(8,128)(2,1)S(1)} all-gather(bf16[48,384]{1,0:T(8,128)(2,1)S(1)} %convert_element_type.239), channel_id=1, replica_groups=mesh['dp'=16,'tensor'=2] {'dp'}, dimensions={0}, use_global_device_ids=true | all-gather | bytes 626688 | tf_op jit(solution)/shard_map/all_gather | solution.py:233
  184.0 39.6 %all_gather.84 = bf16[768,384]{1,0:T(8,128)(2,1)S(1)} all-gather(bf16[48,384]{1,0:T(8,128)(2,1)S(1)} %convert_element_type.242), channel_id=1, replica_groups=mesh['dp'=16,'tensor'=2] {'dp'}, dimensions={0}, use_global_device_ids=true | all-gather | bytes 626688 | tf_op jit(solution)/shard_map/all_gather | solution.py:232
  224.0 40.5 %all_gather.83 = bf16[768,384]{1,0:T(8,128)(2,1)S(1)} all-gather(bf16[48,384]{1,0:T(8,128)(2,1)S(1)} %convert_element_type.241), channel_id=1, replica_groups=mesh['dp'=16,'tensor'=2] {'dp'}, dimensions={0}, use_global_device_ids=true | all-gather | bytes 626688 | tf_op jit(solution)/shard_map/all_gather | solution.py:231
  269.4 41.8 %all_gather.93 = bf16[384,768]{0,1:T(8,128)(2,1)} all-gather(bf16[384,48]{0,1:T(8,128)(2,1)S(1)} %convert_element_type.263), channel_id=1, replica_groups=mesh['dp'=16,'tensor'=2] {'dp'}, dimensions={1}, use_global_device_ids=true | all-gather | bytes 626688 | tf_op jit(solution)/shard_map/all_gather | solution.py:239
  311.2 40.7 %all_gather.87 = bf16[768,384]{1,0:T(8,128)(2,1)S(1)} all-gather(bf16[48,384]{1,0:T(8,128)(2,1)S(1)} %convert_element_type.249), channel_id=1, replica_groups=mesh['dp'=16,'tensor'=2] {'dp'}, dimensions={0}, use_global_device_ids=true | all-gather | bytes 626688 | tf_op jit(solution)/shard_map/all_gather | solution.py:236
  351.9 41.4 %all_gather.92 = bf16[768,384]{1,0:T(8,128)(2,1)} all-gather(bf16[48,384]{1,0:T(8,128)(2,1)S(1)} %convert_element_type.258), channel_id=1, replica_groups=mesh['dp'=16,'tensor'=2] {'dp'}, dimensions={0}, use_global_device_ids=true | all-gather | bytes 626688 | tf_op jit(solution)/shard_map/all_gather | solution.py:235
  393.3 40.4 %all_gather.91 = bf16[768,384]{1,0:T(8,128)(2,1)S(1)} all-gather(bf16[48,384]{1,0:T(8,128)(2,1)S(1)} %convert_element_type.256), channel_id=1, replica_groups=mesh['dp'=16,'tensor'=2] {'dp'}, dimensions={0}, use_global_device_ids=true | all-gather | bytes 626688 | tf_op jit(solution)/shard_map/all_gather | solution.py:234
  456.0 3.2 reshape.390
  482.3 3.7 all_gather.99
  491.1 48.2 %all-gather.8.cloned.1.call-done = bf16[1536,768]{0,1:T(8,128)(2,1)} async-done(((bf16[1536,48]{0,1:T(8,128)(2,1)}), bf16[1536,768]{0,1:T(8,128)(2,1)}) %all-gather.8.cloned.1.call-update) | async-done | bytes 2359312 | tf_op jit(solution)/shard_map/all_gather | solution.py:240
  539.3 3.8 fusion.64
  543.1 60.3 %all-gather.6.cloned.1.call-done = bf16[768,1536]{1,0:T(8,128)(2,1)} async-done(((bf16[48,1536]{1,0:T(8,128)(2,1)}), bf16[768,1536]{1,0:T(8,128)(2,1)}) %all-gather.6.cloned.1.call-update) | async-done | bytes 2359312 | tf_op jit(solution)/shard_map/all_gather | solution.py:237
  603.3 5.3 fusion.3
  611.8 4.0 convolution_convert_fusion.5
  621.0 7.5 reduce-scatter.26.cloned.1.call-done
  653.1 3.8 copy.110
  656.8 4.6 reshape.397
  664.0 3.7 copy.112
  667.8 3.4 reshape.398
  726.6 77.0 %all-reduce.12 = (f32[768]{0:T(1024)S(1)}, f32[768]{0:T(1024)S(1)}, f32[768]{0:T(1024)S(1)}, f32[768]{0:T(1024)S(1)}, f32[768]{0:T(1024)S(1)}, /*index=5*/f32[768]{0:T(1024)S(1)}) all-reduce(f32[768]{0:T(1024)S(1)} %get-tuple-element.120, f32[768]{0:T(1024)S(1)} %get-tuple-element.125, ...), channel_id=9, replica_groups=mesh['dp'=16,'tensor'=2] {'dp'}, use_global_device_ids=true, to_apply=%region_27.28.clone | all-reduce | flops 4608 | bytes 36864
  811.1 33.2 %reduce-scatter.48.cloned.1.call-done = f32[384,48]{0,1:T(8,128)} async-done(((f32[384,768]{0,1:T(8,128)}), f32[384,48]{0,1:T(8,128)}) %reduce-scatter.48.cloned.1.call-update) | async-done | bytes 73744 | tf_op jit(solution)/shard_map/reduce_scatter | solution.py:438
  844.2 128.6 %reduce-scatter.42.cloned.1.call-done = f32[48,384]{1,0:T(8,128)} async-done(((f32[768,384]{1,0:T(8,128)}), f32[48,384]{1,0:T(8,128)}) %reduce-scatter.42.cloned.1.call-update) | async-done | bytes 73744 | tf_op jit(solution)/shard_map/reduce_scatter | solution.py:433
  972.8 128.7 %reduce-scatter.52.cloned.1.call-done = f32[48,384]{1,0:T(8,128)} async-done(((f32[768,384]{1,0:T(8,128)}), f32[48,384]{1,0:T(8,128)}) %reduce-scatter.52.cloned.1.call-update) | async-done | bytes 73744
  1101.5 128.5 %reduce-scatter.54.cloned.1.call-done = f32[48,384]{1,0:T(8,128)} async-done(((f32[768,384]{1,0:T(8,128)}), f32[48,384]{1,0:T(8,128)}) %reduce-scatter.54.cloned.1.call-update) | async-done | bytes 73744
  1230.1 128.6 %reduce-scatter.46.cloned.1.call-done = f32[384,48]{0,1:T(8,128)} async-done(((f32[384,768]{0,1:T(8,128)}), f32[384,48]{0,1:T(8,128)}) %reduce-scatter.46.cloned.1.call-update) | async-done | bytes 73744 | tf_op jit(solution)/shard_map/reduce_scatter | solution.py:437
  1358.7 128.5 %reduce-scatter.40.cloned.1.call-done = f32[48,384]{1,0:T(8,128)} async-done(((f32[768,384]{1,0:T(8,128)}), f32[48,384]{1,0:T(8,128)}) %reduce-scatter.40.cloned.1.call-update) | async-done | bytes 73744 | tf_op jit(solution)/shard_map/reduce_scatter | solution.py:432
  1487.1 128.5 %reduce-scatter.38.cloned.1.call-done = f32[48,384]{1,0:T(8,128)} async-done(((f32[768,384]{1,0:T(8,128)}), f32[48,384]{1,0:T(8,128)}) %reduce-scatter.38.cloned.1.call-update) | async-done | bytes 73744 | tf_op jit(solution)/shard_map/reduce_scatter | solution.py:431
  1615.6 128.5 %reduce-scatter.36.cloned.1.call-done = f32[48,384]{1,0:T(8,128)} async-done(((f32[768,384]{1,0:T(8,128)}), f32[48,384]{1,0:T(8,128)}) %reduce-scatter.36.cloned.1.call-update) | async-done | bytes 73744 | tf_op jit(solution)/shard_map/reduce_scatter | solution.py:430
  1744.2 142.0 %reduce-scatter.44.cloned.1.call-done = f32[48,1536]{1,0:T(8,128)} async-done(((f32[768,1536]{1,0:T(8,128)}), f32[48,1536]{1,0:T(8,128)}) %reduce-scatter.44.cloned.1.call-update) | async-done | bytes 294928 | tf_op jit(solution)/shard_map/reduce_scatter | solution.py:436
  1886.1 141.9 %reduce-scatter.50.cloned.1.call-done = f32[1536,48]{0,1:T(8,128)} async-done(((f32[1536,768]{0,1:T(8,128)}), f32[1536,48]{0,1:T(8,128)}) %reduce-scatter.50.cloned.1.call-update) | async-done | bytes 294928 | tf_op jit(solution)/shard_map/reduce_scatter | solution.py:439
  (388 shorter events, 169.0 us)
Async XLA Ops:
  8.0 425.7 %reduce-scatter.22.cloned.1.call-start = ((), (), s32[]{:S(2)}) async-start(), calls=%async_computation.17 | async-start | bytes 589824 | tf_op jit(solution)/shard_map/reduce_scatter | solution.py:70
  13.1 170.4 %copy-start.73 = (f32[128]{0:T(128)}, f32[128]{0:T(128)S(1)}, u32[]{:S(2)}) copy-start(f32[128]{0:T(128)S(1)} %broadcast_multiply_fusion.3) | copy-start | bytes 1540
  14.3 169.2 %copy-start.78 = (f32[128]{0:T(128)}, f32[128]{0:T(128)S(1)}, u32[]{:S(2)}) copy-start(f32[128]{0:T(128)S(1)} %fusion.48) | copy-start | bytes 1540
  96.2 87.3 %copy-start.59 = (f32[768]{0:T(1024)}, f32[768]{0:T(1024)S(1)}, u32[]{:S(2)}) copy-start(f32[768]{0:T(1024)S(1)} %convert_element_type.235) | copy-start | bytes 9220
  100.5 164.4 %copy-start.54 = (f32[256,32]{0,1:T(8,128)}, f32[256,32]{0,1:T(8,128)S(1)}, u32[]{:S(2)}) copy-start(f32[256,32]{0,1:T(8,128)S(1)} %get-tuple-element.168) | copy-start | bytes 98308
  103.7 160.8 %copy-start.1 = (bf16[256,768]{1,0:T(8,128)(2,1)}, bf16[256,768]{1,0:T(8,128)(2,1)S(1)}, u32[]{:S(2)}) copy-start(bf16[256,768]{1,0:T(8,128)(2,1)S(1)} %all_gather.81) | copy-start | bytes 1179652
  142.3 124.7 %copy-start.9 = (bf16[384,768]{0,1:T(8,128)(2,1)}, bf16[384,768]{0,1:T(8,128)(2,1)S(1)}, u32[]{:S(2)}) copy-start(bf16[384,768]{0,1:T(8,128)(2,1)S(1)} %all_gather.85) | copy-start | bytes 1769476
  184.0 82.0 %copy-start.44 = (bf16[256,384]{0,1:T(8,128)(2,1)}, bf16[256,384]{0,1:T(8,128)(2,1)S(1)}, u32[]{:S(2)}) copy-start(bf16[256,384]{0,1:T(8,128)(2,1)S(1)} %copy.89) | copy-start | bytes 589828
  223.6 41.3 %copy-start.15 = (bf16[768,384]{1,0:T(8,128)(2,1)}, bf16[768,384]{1,0:T(8,128)(2,1)S(1)}, u32[]{:S(2)}) copy-start(bf16[768,384]{1,0:T(8,128)(2,1)S(1)} %all_gather.84) | copy-start | bytes 1769476
  268.2 175.5 %all-gather.4.cloned.1.call-start = ((), (), s32[]{:S(2)}) async-start(), calls=%async_computation.18 | async-start | bytes 1769472 | tf_op jit(solution)/shard_map/all_gather | solution.py:289
  269.0 164.7 %copy-start = (bf16[128,768]{1,0:T(8,128)(2,1)S(1)}, bf16[128,768]{1,0:T(8,128)(2,1)}, u32[]{:S(2)}) copy-start(bf16[128,768]{1,0:T(8,128)(2,1)} %param.28) | copy-start | bytes 589828
  269.0 217.0 %reduce-scatter.24.cloned.1.call-start = ((), (), s32[]{:S(2)}) async-start(), calls=%async_computation.19 | async-start | bytes 589824 | tf_op jit(solution)/shard_map/reduce_scatter | solution.py:70
  269.2 166.9 %copy-start.61 = (f32[768]{0:T(1024)}, f32[768]{0:T(1024)S(1)}, u32[]{:S(2)}) copy-start(f32[768]{0:T(1024)S(1)} %convert_element_type.252) | copy-start | bytes 9220
  351.9 96.5 %copy-start.29 = (bf16[768,384]{1,0:T(8,128)(2,1)}, bf16[768,384]{1,0:T(8,128)(2,1)S(1)}, u32[]{:S(2)}) copy-start(bf16[768,384]{1,0:T(8,128)(2,1)S(1)} %all_gather.87) | copy-start | bytes 1769476
  476.9 62.4 %all-gather.8.cloned.1.call-start = ((), (), s32[]{:S(2)}) async-start(), calls=%async_computation.21 | async-start | bytes 2506752 | tf_op jit(solution)/shard_map/all_gather | solution.py:240
  478.6 124.8 %all-gather.6.cloned.1.call-start = ((), (), s32[]{:S(2)}) async-start(), calls=%async_computation.20 | async-start | bytes 2506752 | tf_op jit(solution)/shard_map/all_gather | solution.py:237
  480.3 137.6 %reduce-scatter.28.cloned.1.call-start = ((), (), s32[]{:S(2)}) async-start(), calls=%async_computation.23 | async-start | bytes 589824 | tf_op jit(solution)/shard_map/reduce_scatter | solution.py:76
  611.2 17.4 reduce-scatter.26.cloned.1.call-start
  615.8 58.6 %reduce-scatter.30.cloned.1.call-start = ((), (), s32[]{:S(2)}) async-start(), calls=%async_computation.24 | async-start | bytes 589824 | tf_op jit(solution)/shard_map/reduce_scatter | solution.py:76
  649.9 74.3 %reduce-scatter.32.cloned.1.call-start = ((), (), s32[]{:S(2)}) async-start(), calls=%async_computation.25 | async-start | bytes 589824 | tf_op jit(solution)/shard_map/reduce_scatter | solution.py:76
  691.6 117.3 %reduce-scatter.34.cloned.1.call-start = ((), (), s32[]{:S(2)}) async-start(), calls=%async_computation.26 | async-start | bytes 1769472 | tf_op jit(solution)/shard_map/reduce_scatter | solution.py:381
  699.6 144.6 %reduce-scatter.48.cloned.1.call-start = ((), (), s32[]{:S(2)}) async-start(), calls=%async_computation.33 | async-start | bytes 1253376 | tf_op jit(solution)/shard_map/reduce_scatter | solution.py:438
  701.1 271.7 %reduce-scatter.42.cloned.1.call-start = ((), (), s32[]{:S(2)}) async-start(), calls=%async_computation.30 | async-start | bytes 1253376 | tf_op jit(solution)/shard_map/reduce_scatter | solution.py:433
  702.7 398.8 %reduce-scatter.52.cloned.1.call-start = ((), (), s32[]{:S(2)}) async-start(), calls=%async_computation.35 | async-start | bytes 1253376
  706.1 524.0 %reduce-scatter.54.cloned.1.call-start = ((), (), s32[]{:S(2)}) async-start(), calls=%async_computation.36 | async-start | bytes 1253376
  709.6 649.1 %reduce-scatter.46.cloned.1.call-start = ((), (), s32[]{:S(2)}) async-start(), calls=%async_computation.32 | async-start | bytes 1253376 | tf_op jit(solution)/shard_map/reduce_scatter | solution.py:437
  711.1 776.0 %reduce-scatter.40.cloned.1.call-start = ((), (), s32[]{:S(2)}) async-start(), calls=%async_computation.29 | async-start | bytes 1253376 | tf_op jit(solution)/shard_map/reduce_scatter | solution.py:432
  712.7 903.0 %reduce-scatter.38.cloned.1.call-start = ((), (), s32[]{:S(2)}) async-start(), calls=%async_computation.28 | async-start | bytes 1253376 | tf_op jit(solution)/shard_map/reduce_scatter | solution.py:431
  714.2 1030.0 %reduce-scatter.36.cloned.1.call-start = ((), (), s32[]{:S(2)}) async-start(), calls=%async_computation.27 | async-start | bytes 1253376 | tf_op jit(solution)/shard_map/reduce_scatter | solution.py:430
  715.7 1170.4 %reduce-scatter.44.cloned.1.call-start = ((), (), s32[]{:S(2)}) async-start(), calls=%async_computation.31 | async-start | bytes 5013504 | tf_op jit(solution)/shard_map/reduce_scatter | solution.py:436
  718.8 1309.3 %reduce-scatter.50.cloned.1.call-start = ((), (), s32[]{:S(2)}) async-start(), calls=%async_computation.34 | async-start | bytes 5013504 | tf_op jit(solution)/shard_map/reduce_scatter | solution.py:439
  723.4 83.7 %copy-start.39 = (f32[128,768]{1,0:T(8,128)S(1)}, f32[128,768]{1,0:T(8,128)}, u32[]{:S(2)}) copy-start(f32[128,768]{1,0:T(8,128)} %get-tuple-element.146) | copy-start | bytes 1179652
  (80 other events, 234.3 us)
Sparse Core Ops, SparseCore 0:
  268.3 4.3 reduce-scatter.21
  274.3 10.3 all-gather.3
  477.0 3.7 reduce-scatter.23
  611.3 6.0 reduce-scatter.27
  619.5 8.9 reduce-scatter.25
  650.0 8.9 reduce-scatter.29
  691.7 8.9 reduce-scatter.31
  703.5 9.8 reduce-scatter.33
  719.4 124.7 reduce-scatter.47
  850.1 122.6 reduce-scatter.41
  978.9 122.6 reduce-scatter.51
  1107.4 122.5 reduce-scatter.53
  1236.1 122.4 reduce-scatter.45
  1364.6 122.5 reduce-scatter.39
  1493.0 122.5 reduce-scatter.37
  1621.5 122.5 reduce-scatter.35
  1750.6 135.4 reduce-scatter.43
  1891.7 136.2 reduce-scatter.49
Sparse Core Ops, SparseCore 1:
  480.7 58.5 all-gather.7
  542.5 60.8 all-gather.5
where the time goes:
time: 2040 us
  waiting for transfers between devices  1330 us (65%)
  blocking collectives  497 us (24%)
  matrix products  70.7 us (3%)
  local copies, waits for them, and re-layouts  68.8 us (3%)
  other arithmetic  45 us (2%)
    unnamed x22, waiting for transfers between devices  258 us
    unnamed x2, blocking collectives  156 us
    reduce_scatter x1, waiting for transfers between devices, on_device(): lax.psum_scatter(grad_up, 'dp', scatter_dimension=0, tiled=True)  142 us
    reduce_scatter x1, waiting for transfers between devices, on_device(): lax.psum_scatter(grad_down, 'dp', scatter_dimension=1, tiled=True)  142 us
    reduce_scatter x1, waiting for transfers between devices, on_device(): lax.psum_scatter(grad_wout, 'dp', scatter_dimension=1, tiled=True)  129 us
    reduce_scatter x1, waiting for transfers between devices, on_device(): lax.psum_scatter(grad_cquery, 'dp', scatter_dimension=0, tiled=True)  129 us
    reduce_scatter x1, waiting for transfers between devices, on_device(): lax.psum_scatter(grad_query, 'dp', scatter_dimension=0, tiled=True)  129 us
    reduce_scatter x1, waiting for transfers between devices, on_device(): lax.psum_scatter(grad_key, 'dp', scatter_dimension=0, tiled=True)  128 us
  transfers between devices with their start and end apart: 20, of which 13 were waited for; matrix products, arithmetic and copies ran while one was open for 4% of the time, Pallas kernels for 0%

commit v1 on v0

--- a/solution.py
+++ b/solution.py
@@ -8,6 +8,7 @@
 GROUP = 64
 NBR_LEN = 128
 NBRS = 2
+LANES = 128
 
 
 HIGHEST_MODE = lax.Precision.HIGHEST
@@ -28,6 +29,14 @@
     return lax.dot_general(
         left, right, (((1,), (1,)), ((), ())), preferred_element_type=jnp.float32
     )
+
+
+def split_columns(array, widths):
+    parts, start = [], 0
+    for width in widths:
+        parts.append(array[:, start : start + width])
+        start += width
+    return parts
 
 
 def layer_norm(stream, gain, shift):
@@ -202,61 +211,19 @@
     w_down,
     cotangent,
 ):
-    masters = (
-        ln1_gain,
-        ln1_bias,
-        ln2_gain,
-        ln2_bias,
-        ln3_gain,
-        ln3_bias,
-        w_query,
-        w_key,
-        w_value,
-        c_query,
-        c_key,
-        c_value,
-        w_up,
-        w_out,
-        c_out,
-        w_down,
-    )
-    shards = tuple((master.astype(jnp.bfloat16) for master in masters))
-    fetched = (
-        lax.all_gather(shards[0], "dp", axis=0, tiled=True),
-        lax.all_gather(shards[1], "dp", axis=0, tiled=True),
-        lax.all_gather(shards[2], "dp", axis=0, tiled=True),
-        lax.all_gather(shards[3], "dp", axis=0, tiled=True),
-        lax.all_gather(shards[4], "dp", axis=0, tiled=True),
-        lax.all_gather(shards[5], "dp", axis=0, tiled=True),
-        lax.all_gather(shards[6], "dp", axis=0, tiled=True),
-        lax.all_gather(shards[7], "dp", axis=0, tiled=True),
-        lax.all_gather(shards[8], "dp", axis=0, tiled=True),
-        lax.all_gather(shards[9], "dp", axis=0, tiled=True),
-        lax.all_gather(shards[10], "dp", axis=0, tiled=True),
-        lax.all_gather(shards[11], "dp", axis=0, tiled=True),
-        lax.all_gather(shards[12], "dp", axis=0, tiled=True),
-        lax.all_gather(shards[13], "dp", axis=1, tiled=True),
-        lax.all_gather(shards[14], "dp", axis=1, tiled=True),
-        lax.all_gather(shards[15], "dp", axis=1, tiled=True),
-    )
-    (
-        gain_one,
-        shift_one,
-        gain_two,
-        shift_two,
-        gain_three,
-        shift_three,
-        query_w,
-        key_w,
-        value_w,
-        cquery_w,
-        ckey_w,
-        cvalue_w,
-        up_w,
-        out_w,
-        cout_w,
-        down_w,
-    ) = fetched
+    norms = jnp.stack([ln1_gain, ln1_bias, ln2_gain, ln2_bias, ln3_gain, ln3_bias], axis=1)
+    norms = jnp.pad(norms, ((0, 0), (0, LANES - norms.shape[1])))
+    width = w_query.shape[1]
+    hidden = w_up.shape[1]
+    columns = [norms, w_query, w_key, w_value, w_out.T, c_query, c_key, c_value, c_out.T, w_up, w_down.T]
+    widths = [LANES] + [width] * 8 + [hidden] * 2
+    first = 5
+    packed = [jnp.concatenate([col.astype(jnp.bfloat16) for col in part], axis=1) for part in (columns[:first], columns[first:])]
+    full = [lax.all_gather(part, "dp", axis=0, tiled=True) for part in packed]
+    norms_w, query_w, key_w, value_w, out_t = split_columns(full[0], widths[:first])
+    cquery_w, ckey_w, cvalue_w, cout_t, up_w, down_t = split_columns(full[1], widths[first:])
+    out_w, cout_w, down_w = out_t.T, cout_t.T, down_t.T
+    gain_one, shift_one, gain_two, shift_two, gain_three, shift_three = [norms_w[:, i] for i in range(6)]
     score_scale = HEAD_DIM ** (-0.5)
     stream = inputs.astype(jnp.float32)
     normed_one, norm_back_one = jax.vjp(
@@ -309,30 +276,9 @@
     activated, gelu_back = jax.vjp(gelu_tanh, pre_act)
     act_low = activated.astype(jnp.bfloat16)
     result = after_cross + branch_total(product(act_low, down_w))
-    refetched = (
-        lax.all_gather(shards[0], "dp", axis=0, tiled=True),
-        lax.all_gather(shards[1], "dp", axis=0, tiled=True),
-        lax.all_gather(shards[2], "dp", axis=0, tiled=True),
-        lax.all_gather(shards[3], "dp", axis=0, tiled=True),
-        lax.all_gather(shards[4], "dp", axis=0, tiled=True),
-        lax.all_gather(shards[5], "dp", axis=0, tiled=True),
-        lax.all_gather(shards[6], "dp", axis=0, tiled=True),
-        lax.all_gather(shards[7], "dp", axis=0, tiled=True),
-        lax.all_gather(shards[8], "dp", axis=0, tiled=True),
-        lax.all_gather(shards[9], "dp", axis=0, tiled=True),
-        lax.all_gather(shards[10], "dp", axis=0, tiled=True),
-        lax.all_gather(shards[11], "dp", axis=0, tiled=True),
-        lax.all_gather(shards[12], "dp", axis=0, tiled=True),
-        lax.all_gather(shards[13], "dp", axis=1, tiled=True),
-        lax.all_gather(shards[14], "dp", axis=1, tiled=True),
-        lax.all_gather(shards[15], "dp", axis=1, tiled=True),
-    )
-    query_w, key_w, value_w = (refetched[6], refetched[7], refetched[8])
-    cquery_w, ckey_w, cvalue_w = (refetched[9], refetched[10], refetched[11])
-    up_w, out_w, cout_w, down_w = (refetched[12], refetched[13], refetched[14], refetched[15])
     grad_out = cotangent.astype(jnp.float32)
     grad_full = gather_grad(grad_out)
-    grad_down = outer_sum(act_low, grad_full)
+    grad_down = outer_sum(grad_full, act_low)
     grad_act = back_product(grad_full, down_w)
     grad_pre = gelu_back(grad_act)[0].astype(jnp.bfloat16)
     grad_up = outer_sum(mlp_rows, grad_pre)
@@ -341,7 +287,7 @@
     )
     grad_cross_out = grad_out + grad_stream
     grad_full = gather_grad(grad_cross_out)
-    grad_cout = outer_sum(cmixture, grad_full)
+    grad_cout = outer_sum(grad_full, cmixture)
     grad_cmix = (
         back_product(grad_full, cout_w)
         .astype(jnp.bfloat16)
@@ -389,7 +335,7 @@
     )
     grad_self_out = grad_cross_out + grad_stream
     grad_full = gather_grad(grad_self_out)
-    grad_wout = outer_sum(mixture, grad_full)
+    grad_wout = outer_sum(grad_full, mixture)
     grad_mix = (
         back_product(grad_full, out_w).astype(jnp.bfloat16).reshape(seq_rows, heads_local, HEAD_DIM)
     )
@@ -420,24 +366,15 @@
         ),
         "tensor",
     )
-    summed = (
-        lax.psum_scatter(norm_sums[0], "dp", scatter_dimension=0, tiled=True),
-        lax.psum_scatter(norm_sums[1], "dp", scatter_dimension=0, tiled=True),
-        lax.psum_scatter(norm_sums[2], "dp", scatter_dimension=0, tiled=True),
-        lax.psum_scatter(norm_sums[3], "dp", scatter_dimension=0, tiled=True),
-        lax.psum_scatter(norm_sums[4], "dp", scatter_dimension=0, tiled=True),
-        lax.psum_scatter(norm_sums[5], "dp", scatter_dimension=0, tiled=True),
-        lax.psum_scatter(grad_query, "dp", scatter_dimension=0, tiled=True),
-        lax.psum_scatter(grad_key, "dp", scatter_dimension=0, tiled=True),
-        lax.psum_scatter(grad_value, "dp", scatter_dimension=0, tiled=True),
-        lax.psum_scatter(grad_cquery, "dp", scatter_dimension=0, tiled=True),
-        lax.psum_scatter(grad_ckey, "dp", scatter_dimension=0, tiled=True),
-        lax.psum_scatter(grad_cvalue, "dp", scatter_dimension=0, tiled=True),
-        lax.psum_scatter(grad_up, "dp", scatter_dimension=0, tiled=True),
-        lax.psum_scatter(grad_wout, "dp", scatter_dimension=1, tiled=True),
-        lax.psum_scatter(grad_cout, "dp", scatter_dimension=1, tiled=True),
-        lax.psum_scatter(grad_down, "dp", scatter_dimension=1, tiled=True),
-    )
+    norm_grads = jnp.pad(jnp.stack(norm_sums, axis=1), ((0, 0), (0, LANES - 6)))
+    grads = jnp.concatenate(
+        [grad.astype(jnp.bfloat16) for grad in (norm_grads, grad_query, grad_key, grad_value, grad_wout, grad_cquery, grad_ckey, grad_cvalue, grad_cout, grad_up, grad_down)],
+        axis=1,
+    )
+    total = lax.psum_scatter(grads, "dp", scatter_dimension=0, tiled=True).astype(jnp.float32)
+    parts = split_columns(total, widths)
+    norm_part, part_q, part_k, part_v, part_o, part_cq, part_ck, part_cv, part_co, part_up, part_down = parts
+    summed = tuple(norm_part[:, i] for i in range(6)) + (part_q, part_k, part_v, part_cq, part_ck, part_cv, part_up, part_o.T, part_co.T, part_down.T)
     return (
         result.astype(jnp.bfloat16),
         grad_input,

time: 2040 us -> 604 us (0.30)
  waiting for transfers between devices: 1330 us -> 365 us
  blocking collectives: 497 us -> 18.4 us
    reduce_scatter x8 -> x1, waiting for transfers between devices: 960 us -> 171 us  [on_device(): lax.psum_scatter(grads, 'dp', scatter_dimension=0, tiled=True)]
    all_gather x8 -> x0, blocking collectives: 324 us -> none  [the longest x1 41.8 us: on_device(): lax.all_gather(shards[14], 'dp', axis=1, tiled=True)]
    unnamed x22 -> x11, waiting for transfers between devices: 258 us -> 0.84 us
    unnamed x2 -> x0, blocking collectives: 156 us -> none
    all_gather x2, waiting for transfers between devices: 108 us -> 169 us  [on_device(): full = [lax.all_gather(part, 'dp', axis=0, tiled=True) for part in packed]]
  transfers between devices with their start and end apart: 20 -> 11, of which waited for: 13 -> 8; matrix products, arithmetic and copies ran while one was open for 4% -> 14% of each run, Pallas kernels for 0% -> 0%
where the time goes in v1:
time: 604 us; the launch traced here: 597 us
  waiting for transfers between devices  365 us (60%)
  local copies, waits for them, and re-layouts  87.1 us (14%)
  matrix products  71.7 us (12%)
  other arithmetic  38.5 us (6%)
  blocking collectives  18.4 us (3%)
  between operations  15.4 us (3%)
    reduce_scatter x1, waiting for transfers between devices, on_device(): lax.psum_scatter(grads, 'dp', scatter_dimension=0, tiled=True)  171 us
    all_gather x2, waiting for transfers between devices, on_device(): full = [lax.all_gather(part, 'dp', axis=0, tiled=True) for part in packed]  169 us
    dot_general x10, matrix products, product(): return jnp.dot(left, right, preferred_element_type=jnp.float32)  21.2 us
    unnamed x198, local copies, waits for them, and re-layouts  20.2 us
    dot_general x10, matrix products, back_product(): lax.dot_general(left, right, (((1,), (1,)), ((), ())), preferred_element_...  19.9 us
    dot_general x10, matrix products, outer_sum(): lax.dot_general(left, right, (((0,), (0,)), ((), ())), preferred_element_...  15.7 us
    reduce_scatter x3, waiting for transfers between devices, branch_total(): lax.psum_scatter(partial_out.astype(jnp.bfloat16), 'tensor', scatter_dime...  15.4 us
  transfers between devices with their start and end apart: 11, of which 8 were waited for; matrix products, arithmetic and copies ran while one was open for 14% of the time, Pallas kernels for 0%

profile of v1, /device:TPU:0, one launch (start us, length us, event | category | flops | bytes accessed | tf_op | source)
XLA Modules:
  0.0 597.3 jit_solution(15102655651125157527)
XLA Ops:
  16.9 63.1 %all-gather.4.cloned.1.call-done = bf16[768,1664]{1,0:T(8,128)(2,1)} async-done(((bf16[48,1664]{1,0:T(8,128)(2,1)}), bf16[768,1664]{1,0:T(8,128)(2,1)}) %all-gather.4.cloned.1.call-update) | async-done | bytes 2555920 | tf_op jit(solution)/shard_map/all_gather | solution.py:222
  80.0 3.1 convert_reduce_fusion.5
  97.6 4.9 reduce-scatter.9.cloned.1.call-done
  105.7 2.4 all_gather.31
  108.1 6.3 %all-gather.8.cloned.1.call-done = bf16[6,128,768]{2,1,0:T(8,128)(2,1)} async-done(((bf16[3,128,768]{2,1,0:T(8,128)(2,1)}), bf16[6,128,768]{2,1,0:T(8,128)(2,1)}) %all-gather.8.cloned.1.call-update) | async-done | bytes 1179664 | tf_op jit(solution)/shard_map/all_gather | solution.py:256
  114.5 106.1 %all-gather.6.cloned.1.call-done = bf16[768,4608]{1,0:T(8,128)(2,1)} async-done(((bf16[48,4608]{1,0:T(8,128)(2,1)}), bf16[768,4608]{1,0:T(8,128)(2,1)}) %all-gather.6.cloned.1.call-update) | async-done | bytes 7077904 | tf_op jit(solution)/shard_map/all_gather | solution.py:222
  231.6 3.3 reshape.426
  234.9 2.9 copy.126
  237.8 3.3 reshape.429
  241.1 2.8 copy.125
  253.0 2.3 convolution_convert_fusion.16
  255.4 3.7 all_gather.33
  259.1 2.3 reduce-scatter.11.cloned.1.call-done
  267.1 2.5 fusion.8
  269.6 4.0 fusion.13
  274.5 3.3 fusion.26
  278.4 4.0 fusion.29
  284.5 2.3 reduce-scatter.15.cloned.1.call-done
  289.9 8.2 %reduce-scatter.13.cloned.1.call-done = bf16[128,768]{1,0:T(8,128)(2,1)} async-done(((bf16[256,768]{1,0:T(8,128)(2,1)}), bf16[128,768]{1,0:T(8,128)(2,1)}) %reduce-scatter.13.cloned.1.call-update) | async-done | bytes 196624 | tf_op jit(solution)/shard_map/reduce_scatter | solution.py:79
  324.0 2.3 convolution_convert_fusion.15
  326.8 2.8 copy.140
  329.6 4.6 reshape.433
  334.2 3.3 convolution_convert_fusion.1
  337.5 2.9 convert_element_type.393
  340.4 2.8 copy.142
  343.2 3.4 reshape.434
  350.3 3.0 fusion.24
  359.3 2.4 all_gather.35
  376.2 2.9 add_convert_fusion
  392.5 3.4 all-reduce.2
  407.9 2.5 fusion.2
  414.6 171.1 %reduce-scatter.23.cloned.1.call-done = bf16[48,6272]{1,0:T(8,128)(2,1)} async-done(((bf16[768,6272]{1,0:T(8,128)(2,1)}), bf16[48,6272]{1,0:T(8,128)(2,1)}) %reduce-scatter.23.cloned.1.call-update) | async-done | bytes 602128 | tf_op jit(solution)/shard_map/reduce_scatter | solution.py:374
  (361 shorter events, 143.5 us)
Async XLA Ops:
  7.2 75.9 %copy-start = (bf16[128,768]{1,0:T(8,128)(2,1)S(1)}, bf16[128,768]{1,0:T(8,128)(2,1)}, u32[]{:S(2)}) copy-start(bf16[128,768]{1,0:T(8,128)(2,1)} %param.28) | copy-start | bytes 589828
  7.2 72.8 %all-gather.4.cloned.1.call-start = ((), (), s32[]{:S(2)}) async-start(), calls=%async_computation.8 | async-start | bytes 2715648 | tf_op jit(solution)/shard_map/all_gather | solution.py:222
  13.7 88.7 %reduce-scatter.9.cloned.1.call-start = ((), (), s32[]{:S(2)}) async-start(), calls=%async_computation.9 | async-start | bytes 589824 | tf_op jit(solution)/shard_map/reduce_scatter | solution.py:79
  14.9 72.1 %copy-start.69 = (f32[128]{0:T(128)}, f32[128]{0:T(128)S(1)}, u32[]{:S(2)}) copy-start(f32[128]{0:T(128)S(1)} %broadcast_multiply_fusion.3) | copy-start | bytes 1540
  16.0 70.9 %copy-start.83 = (f32[128]{0:T(128)}, f32[128]{0:T(128)S(1)}, u32[]{:S(2)}) copy-start(f32[128]{0:T(128)S(1)} %fusion.76) | copy-start | bytes 1540
  16.1 70.9 %copy-start.74 = (f32[128]{0:T(128)}, f32[128]{0:T(128)S(1)}, u32[]{:S(2)}) copy-start(f32[128]{0:T(128)S(1)} %fusion.90) | copy-start | bytes 1540
  16.9 73.3 %copy-start.48 = (f32[256,32]{0,1:T(8,128)}, f32[256,32]{0,1:T(8,128)S(1)}, u32[]{:S(2)}) copy-start(f32[256,32]{0,1:T(8,128)S(1)} %get-tuple-element.117) | copy-start | bytes 98308
  83.1 5.6 copy-start.56
  83.1 21.5 %copy-start.58 = (f32[768]{0:T(1024)}, f32[768]{0:T(1024)S(1)}, u32[]{:S(2)}) copy-start(f32[768]{0:T(1024)S(1)} %get-tuple-element.62) | copy-start | bytes 9220
  83.1 180.1 %copy-start.64 = (f32[768]{0:T(1024)}, f32[768]{0:T(1024)S(1)}, u32[]{:S(2)}) copy-start(f32[768]{0:T(1024)S(1)} %get-tuple-element.59) | copy-start | bytes 9220
  95.5 18.9 %all-gather.8.cloned.1.call-start = ((), (), s32[]{:S(2)}) async-start(), calls=%async_computation.11 | async-start | bytes 1769472 | tf_op jit(solution)/shard_map/all_gather | solution.py:256
  96.3 124.3 %all-gather.6.cloned.1.call-start = ((), (), s32[]{:S(2)}) async-start(), calls=%async_computation.10 | async-start | bytes 7520256 | tf_op jit(solution)/shard_map/all_gather | solution.py:222
  97.3 164.1 %reduce-scatter.11.cloned.1.call-start = ((), (), s32[]{:S(2)}) async-start(), calls=%async_computation.12 | async-start | bytes 589824 | tf_op jit(solution)/shard_map/reduce_scatter | solution.py:79
  103.5 117.1 %copy-start.71 = (f32[128]{0:T(128)}, f32[128]{0:T(128)S(1)}, u32[]{:S(2)}) copy-start(f32[128]{0:T(128)S(1)} %broadcast_multiply_fusion.2) | copy-start | bytes 1540
  104.6 118.1 %copy-start.85 = (f32[128]{0:T(128)}, f32[128]{0:T(128)S(1)}, u32[]{:S(2)}) copy-start(f32[128]{0:T(128)S(1)} %multiply_reduce_fusion.3) | copy-start | bytes 1540
  104.6 118.1 %copy-start.76 = (f32[128]{0:T(128)}, f32[128]{0:T(128)S(1)}, u32[]{:S(2)}) copy-start(f32[128]{0:T(128)S(1)} %fusion.91) | copy-start | bytes 1540
  250.9 10.5 %copy-start.4 = (bf16[128,768]{1,0:T(8,128)(2,1)S(1)}, bf16[128,768]{1,0:T(8,128)(2,1)}, u32[]{:S(2)}) copy-start(bf16[128,768]{1,0:T(8,128)(2,1)} %reduce-scatter.9.cloned.1.call-done) | copy-start | bytes 589828
  255.3 31.5 %reduce-scatter.15.cloned.1.call-start = ((), (), s32[]{:S(2)}) async-start(), calls=%async_computation.14 | async-start | bytes 589824 | tf_op jit(solution)/shard_map/reduce_scatter | solution.py:85
  277.8 20.4 %reduce-scatter.13.cloned.1.call-start = ((), (), s32[]{:S(2)}) async-start(), calls=%async_computation.13 | async-start | bytes 589824 | tf_op jit(solution)/shard_map/reduce_scatter | solution.py:79
  282.4 72.5 %reduce-scatter.17.cloned.1.call-start = ((), (), s32[]{:S(2)}) async-start(), calls=%async_computation.15 | async-start | bytes 589824 | tf_op jit(solution)/shard_map/reduce_scatter | solution.py:85
  298.2 6.0 %copy-start.23 = (bf16[256,384]{0,1:T(8,128)(2,1)S(1)}, bf16[256,384]{0,1:T(8,128)(2,1)}, u32[]{:S(2)}) copy-start(bf16[256,384]{0,1:T(8,128)(2,1)} %reshape.430) | copy-start | bytes 589828
  300.2 5.1 copy-start.80
  326.3 63.8 %reduce-scatter.19.cloned.1.call-start = ((), (), s32[]{:S(2)}) async-start(), calls=%async_computation.16 | async-start | bytes 589824 | tf_op jit(solution)/shard_map/reduce_scatter | solution.py:85
  334.2 6.2 %copy-start.7 = (f32[4,256,6,64]{1,3,2,0:T(8,128)S(1)}, f32[4,256,6,64]{1,3,2,0:T(8,128)}, u32[]{:S(2)}) copy-start(f32[4,256,6,64]{1,3,2,0:T(8,128)} %convolution_bitcast_fusion.1) | copy-start | bytes 4718596
  370.1 42.3 %reduce-scatter.21.cloned.1.call-start = ((), (), s32[]{:S(2)}) async-start(), calls=%async_computation.17 | async-start | bytes 1769472 | tf_op jit(solution)/shard_map/reduce_scatter | solution.py:327
  379.2 206.5 %reduce-scatter.23.cloned.1.call-start = ((), (), s32[]{:S(2)}) async-start(), calls=%async_computation.18 | async-start | bytes 10235904 | tf_op jit(solution)/shard_map/reduce_scatter | solution.py:374
  384.4 5.8 copy-start.57
  384.4 5.7 copy-start.70
  385.7 5.5 copy-start.84
  385.8 5.5 copy-start.75
  385.8 6.8 %copy-start.67 = (f32[768]{0:T(1024)S(1)}, f32[768]{0:T(1024)}, u32[]{:S(2)}) copy-start(f32[768]{0:T(1024)} %get-tuple-element.73) | copy-start | bytes 9220
  385.8 6.8 %copy-start.68 = (f32[768]{0:T(1024)S(1)}, f32[768]{0:T(1024)}, u32[]{:S(2)}) copy-start(f32[768]{0:T(1024)} %get-tuple-element.77) | copy-start | bytes 9220
  (72 other events, 156.4 us)
Sparse Core Ops, SparseCore 0:
  13.9 66.0 all-gather.3
  95.7 6.7 reduce-scatter.8
  104.1 10.3 all-gather.7
  118.1 102.4 all-gather.5
  255.4 5.9 reduce-scatter.10
  277.9 8.9 reduce-scatter.14
  289.2 8.9 reduce-scatter.12
  326.4 8.9 reduce-scatter.16
  370.2 8.9 reduce-scatter.18
  381.9 9.8 reduce-scatter.20
  410.5 175.1 reduce-scatter.22

commit v2 on v1

v2 whole, which is shorter than its diff:
```python
import functools

import jax
import jax.numpy as jnp
import numpy as np
from jax import lax
from jax.experimental import pallas as pl
from jax.experimental.pallas import tpu as pltpu
from jax.sharding import PartitionSpec as P

HEAD_DIM = 64
GROUP = 64
NBR_LEN = 128
NBRS = 2
LANES = 128
NORMS = 6
NEG_FILL = -1e30
EPSILON = 1e-05
GELU_A = 0.7978845608028654
GELU_B = 0.044715
PLANES = 4
VMEM_BYTES = 40 * 2**20

bf16 = jnp.bfloat16
f32 = jnp.float32


def mm(left, right):
    return jnp.dot(left, right, preferred_element_type=f32)


def mm_nt(left, right):
    return lax.dot_general(left, right, (((1,), (1,)), ((), ())), preferred_element_type=f32)


def mm_tn(left, right):
    return lax.dot_general(left, right, (((0,), (0,)), ((), ())), preferred_element_type=f32)


def wide(array):
    return array.astype(f32)


def grid_perms(count):
    x_swap = [(i, i ^ 1) for i in range(count)]
    y_swap = [(i, i ^ 2) for i in range(count)]
    z_pair = [(i, i ^ 4) for i in range(count)]
    z_mid = [(i, 12 - 4 * (i // 4) + i % 4) for i in range(4, 12)]
    z_out = [(i, i ^ 4) for i in range(4, 12)]
    z_in = [(i ^ 4, i) for i in range(4, 12)]
    return x_swap, y_swap, z_pair, z_mid, z_out, z_in


def block_tables(count):
    table = np.zeros((count, 2 * count), np.int32)
    for device in range(count):
        z, y, x = device // 4, device // 2 % 2, device % 2
        inner = 1 if z in (1, 2) else 0
        slot = 0
        for plane in range(PLANES):
            column = 2 * (y ^ (plane >> 1)) + (x ^ (plane & 1))
            for half in range(2):
                for j in range(2):
                    table[device, slot] = 4 * (z ^ (2 * half + (j ^ (half & inner)))) + column
                    table[device, count + slot] = 4 * (z ^ (2 * half + j)) + column
                    slot += 1
    return table


def pieces_ok(count, rows):
    return count == 16 and rows % 16 == 0


def gather_pieces(shard, count):
    if not pieces_ok(count, shard.shape[0]):
        return (lax.all_gather(shard, "dp", axis=0, tiled=True),)
    x_swap, y_swap, z_pair, z_mid, z_out, _ = grid_perms(count)
    send = functools.partial(lax.ppermute, axis_name="dp")
    buddy = send(shard, perm=z_pair)
    first = jnp.concatenate([shard, buddy], axis=0)
    middle = send(first, perm=z_mid)
    outer = send(middle, perm=z_out)
    is_inner = (lax.axis_index("dp") // 4) % 3 != 0
    second = jnp.where(is_inner, middle, outer)
    x_first, y_first = send(first, perm=x_swap), send(first, perm=y_swap)
    d_first = send(y_first, perm=x_swap)
    x_second, y_second = send(second, perm=x_swap), send(second, perm=y_swap)
    d_second = send(x_second, perm=y_swap)
    return (first, second, x_first, x_second, y_first, y_second, d_first, d_second)


def swap_blocks(array):
    half = array.shape[0] // 2
    return jnp.concatenate([array[half:], array[:half]], axis=0)


def reduce_pieces(pieces, count):
    if len(pieces) == 1:
        return wide(lax.psum_scatter(pieces[0], "dp", scatter_dimension=0, tiled=True))
    first, second, x_first, x_second, y_first, y_second, d_first, d_second = pieces
    x_swap, y_swap, z_pair, z_mid, _, z_in = grid_perms(count)
    send = functools.partial(lax.ppermute, axis_name="dp")
    from_x = send(d_first, perm=x_swap)
    from_y = send(d_second, perm=y_swap)
    got_x_first = send(x_first, perm=x_swap)
    got_y_second = send(y_second, perm=y_swap)
    got_x_second = send((wide(x_second) + wide(from_y)).astype(bf16), perm=x_swap)
    got_y_first = send((wide(y_first) + wide(from_x)).astype(bf16), perm=y_swap)
    other = (wide(second) + wide(got_x_second) + wide(got_y_second)).astype(bf16)
    own = wide(first) + wide(got_x_first) + wide(got_y_first)
    from_out = send(other, perm=z_in)
    other = (wide(other) + wide(swap_blocks(from_out))).astype(bf16)
    from_mid = send(other, perm=z_mid)
    own = own + wide(swap_blocks(from_mid))
    half = own.shape[0] // 2
    from_pair = send(own[half:].astype(bf16), perm=z_pair)
    return own[:half] + wide(from_pair)


def sum_small(array, count):
    step = 1
    while step < count:
        array = array + lax.ppermute(array, "dp", [(i, i ^ step) for i in range(count)])
        step *= 2
    return array


def swap_cores(array):
    return lax.ppermute(array, "tensor", [(0, 1), (1, 0)])


def join_cores(array):
    other = swap_cores(array)
    low = lax.axis_index("tensor") == 0
    return jnp.concatenate(
        [jnp.where(low, array, other), jnp.where(low, other, array)], axis=0
    )


def fetch(table, pieces, target, sems, columns, sem_from=0):
    start, size = columns
    copies = []
    if len(pieces) == 1:
        copies.append(
            pltpu.make_async_copy(pieces[0].at[:, pl.ds(start, size)], target, sems.at[sem_from])
        )
    else:
        rows = pieces[0].shape[0] // 2
        for slot in range(2 * len(pieces)):
            first = pl.multiple_of(table[slot] * rows, 16)
            copies.append(
                pltpu.make_async_copy(
                    pieces[slot // 2].at[pl.ds(slot % 2 * rows, rows), pl.ds(start, size)],
                    target.at[pl.ds(first, rows), :],
                    sems.at[sem_from + slot],
                )
            )
    for copy in copies:
        copy.start()
    return copies


def put(table, source, pieces, sems, columns, sem_from=0):
    start, size = columns
    copies = []
    if len(pieces) == 1:
        copies.append(
            pltpu.make_async_copy(source, pieces[0].at[:, pl.ds(start, size)], sems.at[sem_from])
        )
    else:
        rows = pieces[0].shape[0] // 2
        for slot in range(2 * len(pieces)):
            first = pl.multiple_of(table[2 * len(pieces) + slot] * rows, 16)
            copies.append(
                pltpu.make_async_copy(
                    source.at[pl.ds(first, rows), :],
                    pieces[slot // 2].at[pl.ds(slot % 2 * rows, rows), pl.ds(start, size)],
                    sems.at[sem_from + slot],
                )
            )
    for copy in copies:
        copy.start()
    return copies


def finish(copies):
    for copy in copies:
        copy.wait()


def norm_parts(stream):
    center = stream - jnp.mean(stream, axis=-1, keepdims=True)
    spread = jnp.mean(center * center, axis=-1, keepdims=True)
    scale = lax.rsqrt(spread + EPSILON)
    return center * scale, scale


def norm_back(grad, normal, scale, gain):
    inner = grad * gain
    return scale * (
        inner
        - jnp.mean(inner, axis=-1, keepdims=True)
        - normal * jnp.mean(inner * normal, axis=-1, keepdims=True)
    )


def turn(pair, cosine, sine):
    lane = lax.broadcasted_iota(jnp.int32, pair.shape, 1)
    low_half = lane % HEAD_DIM < HEAD_DIM // 2
    partner = jnp.where(
        low_half,
        pltpu.roll(pair, LANES - HEAD_DIM // 2, 1),
        pltpu.roll(pair, HEAD_DIM // 2, 1),
    )
    return pair * cosine + partner * sine


def stack_heads(pair):
    lane = lax.broadcasted_iota(jnp.int32, pair.shape, 1)
    zero = jnp.zeros_like(pair)
    return jnp.concatenate(
        [jnp.where(lane < HEAD_DIM, pair, zero), jnp.where(lane < HEAD_DIM, zero, pair)], axis=0
    )


def merge_heads(stacked):
    rows = stacked.shape[0] // 2
    lane = lax.broadcasted_iota(jnp.int32, (rows, stacked.shape[1]), 1)
    return jnp.where(lane < HEAD_DIM, stacked[:rows], stacked[rows:])


def softmax_low(scores):
    raised = jnp.exp(scores - jnp.max(scores, axis=-1, keepdims=True))
    return (raised * (1.0 / jnp.sum(raised, axis=-1, keepdims=True))).astype(bf16)


def pairs_of(width):
    return [(pair, slice(pair * LANES, (pair + 1) * LANES)) for pair in range(width // LANES)]


SCALE = HEAD_DIM ** (-0.5)


def self_forward(count, table, x_ref, cos_ref, sin_ref, *refs):
    pieces, refs = refs[:count], refs[count:]
    part, h_out, q_out, k_out, v_out, p_out, o_out, norms_out, weights, sems = refs
    width = q_out.shape[1]
    copies = fetch(table, pieces, weights, sems, (0, weights.shape[1]))
    normal, _ = norm_parts(wide(x_ref[...]))
    finish(copies)
    rows = wide(weights[:, :LANES]).T[:8]
    norms_out[...] = rows
    hidden = (normal * rows[0:1] + rows[1:2]).astype(bf16)
    h_out[...] = hidden
    mixed = mm(hidden, weights[:, LANES : LANES + 3 * width])
    cosine, sine = cos_ref[...], sin_ref[...]
    count_rows = hidden.shape[0]
    query_pos = lax.broadcasted_iota(jnp.int32, (2 * count_rows, count_rows), 0) % count_rows
    allowed = query_pos >= lax.broadcasted_iota(jnp.int32, (2 * count_rows, count_rows), 1)
    for pair, lanes in pairs_of(width):
        queries = turn(mixed[:, lanes], cosine, sine).astype(bf16)
        keys = turn(mixed[:, width + pair * LANES : width + (pair + 1) * LANES], cosine, sine).astype(bf16)
        values = mixed[:, 2 * width + pair * LANES : 2 * width + (pair + 1) * LANES].astype(bf16)
        q_out[:, lanes] = queries
        k_out[:, lanes] = keys
        v_out[:, lanes] = values
        scores = jnp.where(allowed, mm_nt(stack_heads(queries), keys) * SCALE, NEG_FILL)
        attend = softmax_low(scores)
        p_out[pair] = attend
        o_out[:, lanes] = merge_heads(mm(attend, values)).astype(bf16)
    part[...] = mm_nt(o_out[...], weights[:, LANES + 3 * width :]).astype(bf16)


def pool_forward(count, table, pool_ref, *refs):
    pieces, refs = refs[:count], refs[count:]
    k_out, v_out, weights, sems = refs
    width = k_out.shape[1]
    finish(fetch(table, pieces, weights, sems, (width, 2 * width)))
    mixed = mm(pool_ref[...], weights[...])
    k_out[...] = mixed[:, :width].astype(bf16)
    v_out[...] = mixed[:, width:].astype(bf16)


def chosen_rows(chosen, block, ref, lanes):
    return jnp.concatenate(
        [
            ref[pl.ds(pl.multiple_of(chosen[NBRS * block + j] * NBR_LEN, NBR_LEN), NBR_LEN), lanes]
            for j in range(NBRS)
        ],
        axis=0,
    )


def cross_forward(count, table, chosen, x_ref, own_ref, got_ref, norms, k_ref, v_ref, *refs):
    pieces, refs = refs[:count], refs[count:]
    part, x_out, h_out, q_out, p_out, o_out, in_w, out_w, sems, sems_out = refs
    width = q_out.shape[1]
    copies = fetch(table, pieces, in_w, sems, (0, width))
    copies_out = fetch(table, pieces, out_w, sems_out, (3 * width, width))
    stream = wide(x_ref[...]) + (wide(own_ref[...]) + wide(got_ref[...]))
    x_out[...] = stream
    normal, _ = norm_parts(stream)
    hidden = (normal * norms[2:3] + norms[3:4]).astype(bf16)
    h_out[...] = hidden
    finish(copies)
    queries = mm(hidden, in_w[...]).astype(bf16)
    q_out[...] = queries
    pair_count = width // LANES
    for block in range(queries.shape[0] // GROUP):
        rows = slice(block * GROUP, (block + 1) * GROUP)
        for pair, lanes in pairs_of(width):
            keys = chosen_rows(chosen, block, k_ref, lanes)
            values = chosen_rows(chosen, block, v_ref, lanes)
            attend = softmax_low(mm_nt(stack_heads(queries[rows, lanes]), keys) * SCALE)
            p_out[block * pair_count + pair] = attend
            o_out[rows, lanes] = merge_heads(mm(attend, values)).astype(bf16)
    finish(copies_out)
    part[...] = mm_nt(o_out[...], out_w[...]).astype(bf16)


def feed_forward(count, slices, table, x_ref, own_ref, got_ref, norms, g_ref, *refs):
    pieces, refs = refs[:count], refs[count:]
    part, x_out, dh_out = refs[:3]
    grads, refs = refs[3 : 3 + count], refs[3 + count :]
    up_w, down_w, up_g, down_g, sems, sems_out = refs
    total = up_w.shape[0] * up_w.shape[2]
    size = total // slices
    block_count = max(1, 2 * count) if count > 1 else 1
    copies = []
    for turn_of in range(slices):
        copies.append(
            fetch(table, pieces, up_w.at[turn_of], sems, (turn_of * size, size), 2 * turn_of * block_count)
            + fetch(table, pieces, down_w.at[turn_of], sems, (total + turn_of * size, size), (2 * turn_of + 1) * block_count)
        )
    stream = wide(x_ref[...]) + (wide(own_ref[...]) + wide(got_ref[...]))
    x_out[...] = stream
    normal, _ = norm_parts(stream)
    hidden = (normal * norms[4:5] + norms[5:6]).astype(bf16)
    grad = g_ref[...]
    hidden_t, grad_t = hidden.T, grad.T
    out = jnp.zeros(stream.shape, f32)
    back = jnp.zeros(stream.shape, f32)
    sent = []
    for turn_of in range(slices):
        finish(copies[turn_of])
        pre = mm(hidden, up_w[turn_of])
        grad_act = mm(grad, down_w[turn_of])
        square = pre * pre
        bend = jnp.tanh(GELU_A * (pre + GELU_B * square * pre))
        gate = 0.5 * (1.0 + bend)
        act = (pre * gate).astype(bf16)
        slope = gate + 0.5 * pre * (1.0 - bend * bend) * (GELU_A * (1.0 + 3.0 * GELU_B * square))
        grad_pre = (grad_act * slope).astype(bf16)
        up_g[turn_of] = mm(hidden_t, grad_pre).astype(bf16)
        down_g[turn_of] = mm(grad_t, act).astype(bf16)
        sent += put(table, up_g.at[turn_of], grads, sems_out, (turn_of * size, size), 2 * turn_of * block_count)
        sent += put(table, down_g.at[turn_of], grads, sems_out, (total + turn_of * size, size), (2 * turn_of + 1) * block_count)
        out = out + mm_nt(act, down_w[turn_of])
        back = back + mm_nt(grad_pre, up_w[turn_of])
    part[...] = out.astype(bf16)
    dh_out[...] = back.astype(bf16)
    finish(sent)


def attention_back(stacked_grad, outputs, attend, keys, values, stacked_queries):
    both = jnp.concatenate([outputs, outputs], axis=0)
    inner = jnp.sum(wide(stacked_grad) * wide(both), axis=-1, keepdims=True)
    grad_scores = (wide(attend) * (mm_nt(stacked_grad, values) - inner)).astype(bf16)
    grad_q = merge_heads(mm(grad_scores, keys)) * SCALE
    grad_k = mm_tn(grad_scores, stacked_queries) * SCALE
    grad_v = mm_tn(attend, stacked_grad)
    return grad_q, grad_k, grad_v


def cross_back(count, table, chosen, g_ref, x_ref, norms, own_ref, got_ref, p_ref, o_ref, q_ref, k_ref, v_ref, *refs):
    pieces, refs = refs[:count], refs[count:]
    dx_out, low_out, dh_out, dq_out, dk_out, dv_out, sums_out, in_w, out_w, dk_acc, dv_acc, sems, sems_out = refs
    width = q_ref.shape[1]
    copies = fetch(table, pieces, out_w, sems_out, (3 * width, width))
    copies_in = fetch(table, pieces, in_w, sems, (0, width))
    normal, scale = norm_parts(x_ref[...])
    grad = wide(own_ref[...]) + wide(got_ref[...])
    dx = wide(g_ref[...]) + norm_back(grad, normal, scale, norms[4:5])
    dx_out[...] = dx
    sums_out[0:1] = jnp.sum(grad * normal, axis=0, keepdims=True)
    sums_out[1:2] = jnp.sum(grad, axis=0, keepdims=True)
    low = dx.astype(bf16)
    low_out[...] = low
    dk_acc[...] = jnp.zeros_like(dk_acc)
    dv_acc[...] = jnp.zeros_like(dv_acc)
    finish(copies)
    grad_mix = mm(low, out_w[...]).astype(bf16)
    pair_count = width // LANES
    for block in range(low.shape[0] // GROUP):
        rows = slice(block * GROUP, (block + 1) * GROUP)
        for pair, lanes in pairs_of(width):
            keys = chosen_rows(chosen, block, k_ref, lanes)
            values = chosen_rows(chosen, block, v_ref, lanes)
            grad_q, grad_k, grad_v = attention_back(
                stack_heads(grad_mix[rows, lanes]),
                o_ref[rows, lanes],
                p_ref[block * pair_count + pair],
                keys,
                values,
                stack_heads(q_ref[rows, lanes]),
            )
            dq_out[rows, lanes] = grad_q.astype(bf16)
            for j in range(NBRS):
                place = pl.ds(pl.multiple_of(chosen[NBRS * block + j] * NBR_LEN, NBR_LEN), NBR_LEN)
                part = slice(j * NBR_LEN, (j + 1) * NBR_LEN)
                dk_acc[place, lanes] += grad_k[part]
                dv_acc[place, lanes] += grad_v[part]
    dk_out[...] = dk_acc[...].astype(bf16)
    dv_out[...] = dv_acc[...].astype(bf16)
    finish(copies_in)
    dh_out[...] = mm_nt(dq_out[...], in_w[...]).astype(bf16)


def cross_weights(count, table, low_ref, o_ref, h_ref, dq_ref, pool_ref, dk_ref, dv_ref, *refs):
    pieces, refs = refs[:count], refs[count:]
    pool_out = refs[0]
    grads, refs = refs[1 : 1 + count], refs[1 + count :]
    weights, made, sems, sems_out = refs
    width = dq_ref.shape[1]
    block_count = max(1, 2 * count) if count > 1 else 1
    copies = fetch(table, pieces, weights, sems, (width, 2 * width))
    made[3] = mm_tn(low_ref[...], o_ref[...]).astype(bf16)
    made[0] = mm_tn(h_ref[...], dq_ref[...]).astype(bf16)
    pool_t = pool_ref[...].T
    made[1] = mm(pool_t, dk_ref[...]).astype(bf16)
    made[2] = mm(pool_t, dv_ref[...]).astype(bf16)
    sent = []
    for part in range(4):
        sent += put(table, made.at[part], grads, sems_out, (part * width, width), part * block_count)
    finish(copies)
    pool_out[...] = (mm_nt(dk_ref[...], weights[:, :width]) + mm_nt(dv_ref[...], weights[:, width:])).astype(bf16)
    finish(sent)


def self_back(count, table, dx_ref, x_ref, norms, own_ref, got_ref, p_ref, o_ref, q_ref, k_ref, v_ref, cos_ref, sin_ref, *refs):
    pieces, refs = refs[:count], refs[count:]
    dx_out, low_out, dh_out, dq_out, dk_out, dv_out, sums_out, weights, sems = refs
    width = q_ref.shape[1]
    copies = fetch(table, pieces, weights, sems, (LANES, 4 * width))
    normal, scale = norm_parts(x_ref[...])
    grad = wide(own_ref[...]) + wide(got_ref[...])
    dx = dx_ref[...] + norm_back(grad, normal, scale, norms[2:3])
    dx_out[...] = dx
    sums_out[0:1] = jnp.sum(grad * normal, axis=0, keepdims=True)
    sums_out[1:2] = jnp.sum(grad, axis=0, keepdims=True)
    low = dx.astype(bf16)
    low_out[...] = low
    finish(copies)
    grad_mix = mm(low, weights[:, 3 * width :]).astype(bf16)
    cosine, sine = cos_ref[...], -sin_ref[...]
    for pair, lanes in pairs_of(width):
        grad_q, grad_k, grad_v = attention_back(
            stack_heads(grad_mix[:, lanes]),
            o_ref[:, lanes],
            p_ref[pair],
            k_ref[:, lanes],
            v_ref[:, lanes],
            stack_heads(q_ref[:, lanes]),
        )
        dq_out[:, lanes] = turn(grad_q, cosine, sine).astype(bf16)
        dk_out[:, lanes] = turn(grad_k, cosine, sine).astype(bf16)
        dv_out[:, lanes] = grad_v.astype(bf16)
    dh_out[...] = (
        mm_nt(dq_out[...], weights[:, :width])
        + mm_nt(dk_out[...], weights[:, width : 2 * width])
        + mm_nt(dv_out[...], weights[:, 2 * width : 3 * width])
    ).astype(bf16)


def self_weights(count, table, low_ref, o_ref, h_ref, dq_ref, dk_ref, dv_ref, *refs):
    grads, refs = refs[:count], refs[count:]
    made, sems_out = refs
    width = dq_ref.shape[1]
    block_count = max(1, 2 * count) if count > 1 else 1
    made[3] = mm_tn(low_ref[...], o_ref[...]).astype(bf16)
    hidden_t = h_ref[...].T
    made[0] = mm(hidden_t, dq_ref[...]).astype(bf16)
    made[1] = mm(hidden_t, dk_ref[...]).astype(bf16)
    made[2] = mm(hidden_t, dv_ref[...]).astype(bf16)
    sent = []
    for part in range(4):
        sent += put(table, made.at[part], grads, sems_out, (part * width, width), part * block_count)
    finish(sent)


def input_back(dx_ref, x_ref, norms, own_ref, got_ref, dx_out, sums_out):
    normal, scale = norm_parts(wide(x_ref[...]))
    grad = wide(own_ref[...]) + wide(got_ref[...])
    dx_out[...] = dx_ref[...] + norm_back(grad, normal, scale, norms[0:1])
    sums_out[0:1] = jnp.sum(grad * normal, axis=0, keepdims=True)
    sums_out[1:2] = jnp.sum(grad, axis=0, keepdims=True)


SMEM = pl.BlockSpec(memory_space=pltpu.SMEM)
VMEM = pl.BlockSpec(memory_space=pltpu.VMEM)
ANY = pl.BlockSpec(memory_space=pl.ANY)


def call(body, name, scalars, arrays, pieces, outs, grads, scratch, flops):
    shapes = [jax.ShapeDtypeStruct(shape, dtype) for shape, dtype in list(outs) + list(grads)]
    moved = sum(a.size * a.dtype.itemsize for a in list(arrays) + list(pieces))
    moved += sum(int(np.prod(s.shape)) * s.dtype.itemsize for s in shapes)
    return pl.pallas_call(
        body,
        name=name,
        out_shape=shapes,
        in_specs=[SMEM] * len(scalars) + [VMEM] * len(arrays) + [ANY] * len(pieces),
        out_specs=[VMEM] * len(outs) + [ANY] * len(grads),
        scratch_shapes=scratch,
        compiler_params=pltpu.CompilerParams(vmem_limit_bytes=VMEM_BYTES),
        cost_estimate=pl.CostEstimate(flops=int(flops), bytes_accessed=int(moved), transcendentals=0),
    )(*scalars, *arrays, *pieces)


def rope_tables(rows):
    half = HEAD_DIM // 2
    frequency = np.power(np.float32(10000.0), -np.arange(half, dtype=np.float32) / np.float32(half))
    angles = np.arange(rows, dtype=np.float32)[:, None] * frequency[None, :]
    cosine, sine = np.cos(angles), np.sin(angles)
    return (
        jnp.asarray(np.concatenate([cosine] * 4, axis=1), f32),
        jnp.asarray(np.concatenate([-sine, sine] * 2, axis=1), f32),
    )


def dma_sems(count, uses=1):
    blocks = 2 * count if count > 1 else 1
    return pltpu.SemaphoreType.DMA((blocks * uses,))


def on_device(count, inputs, neighbours, nbr_index, ln1_gain, ln1_bias, ln2_gain, ln2_bias, ln3_gain, ln3_bias,
              w_query, w_key, w_value, c_query, c_key, c_value, w_up, w_out, c_out, w_down, cotangent):
    width, hidden = w_query.shape[1], w_up.shape[1]
    shard_rows = w_query.shape[0]
    model = shard_rows * count
    rows = 2 * inputs.shape[0]
    norms = jnp.stack([ln1_gain, ln1_bias, ln2_gain, ln2_bias, ln3_gain, ln3_bias], axis=1)
    norms = jnp.pad(norms, ((0, 0), (0, LANES - NORMS)))

    def pack(*columns):
        return jnp.concatenate([column.astype(bf16) for column in columns], axis=1)

    self_w = gather_pieces(pack(norms, w_query, w_key, w_value, w_out.T), count)
    cross_w = gather_pieces(pack(c_query, c_key, c_value, c_out.T), count)
    ff_w = gather_pieces(pack(w_up, w_down.T), count)
    pieces = len(self_w)
    if pieces > 1:
        table = jnp.asarray(block_tables(count))[lax.axis_index("dp")]
    else:
        table = jnp.zeros((1,), jnp.int32)
    grad_rows = (2 * shard_rows) if pieces > 1 else model

    def bind(body, *extra):
        return functools.partial(body, pieces, *extra)

    stream = join_cores(inputs)
    cot = join_cores(cotangent)
    pool = join_cores(neighbours.reshape(-1, neighbours.shape[-1]))
    pool_rows = pool.shape[0]
    chosen = nbr_index.reshape(-1)
    cosine, sine = rope_tables(rows)
    pairs = width // LANES
    blocks = rows // GROUP
    tall, low = ((rows, model), f32), ((rows, model), bf16)
    slim = ((rows, width), bf16)
    rank8 = ((8, model), f32)
    dense = 2 * rows * model * width

    part, h_one, queries, keys, values, attend, mixture, norm_rows = call(
        bind(self_forward), "self_forward", [table], [stream, cosine, sine], self_w,
        [low, low, slim, slim, slim, ((pairs, 2 * rows, rows), bf16), slim, rank8], [],
        [pltpu.VMEM((model, LANES + 4 * width), bf16), dma_sems(pieces)], 4 * dense)
    got = swap_cores(part)
    ckeys, cvalues = call(
        bind(pool_forward), "pool_forward", [table], [pool], cross_w,
        [((pool_rows, width), bf16)] * 2, [],
        [pltpu.VMEM((model, 2 * width), bf16), dma_sems(pieces)], 4 * pool_rows * model * width)
    part, after_self, h_two, cqueries, cattend, cmixture = call(
        bind(cross_forward), "cross_forward", [table, chosen], [stream, part, got, norm_rows, ckeys, cvalues], cross_w,
        [low, tall, low, slim, ((blocks * pairs, 2 * GROUP, NBRS * NBR_LEN), bf16), slim], [],
        [pltpu.VMEM((model, width), bf16), pltpu.VMEM((model, width), bf16), dma_sems(pieces), dma_sems(pieces)], 2 * dense)
    got = swap_cores(part)
    slices = 3
    size = hidden // slices
    part, after_cross, grad_part, *ff_grads = call(
        bind(feed_forward, slices), "feed_forward", [table], [after_self, part, got, norm_rows, cot], ff_w,
        [low, tall, low], [((grad_rows, 2 * hidden), bf16)] * pieces,
        [pltpu.VMEM((slices, model, size), bf16)] * 4 + [dma_sems(pieces, 2 * slices)] * 2, 12 * rows * model * hidden)
    got = swap_cores(grad_part)
    d_ff = reduce_pieces(ff_grads, count)
    here = lax.axis_index("tensor") * inputs.shape[0]
    there = inputs.shape[0] - here

    def part_of(array, start, size):
        return lax.dynamic_slice_in_dim(array, start, size, 0)

    result = part_of(after_cross, here, inputs.shape[0]) + (
        wide(part_of(part, here, inputs.shape[0])) + wide(swap_cores(part_of(part, there, inputs.shape[0])))
    )
    acc = pltpu.VMEM((pool_rows, width), f32)
    grad_cross, low_cross, grad_part, dcq, dck, dcv, sums_three = call(
        bind(cross_back), "cross_back", [table, chosen],
        [cot, after_cross, norm_rows, grad_part, got, cattend, cmixture, cqueries, ckeys, cvalues], cross_w,
        [tall, low, low, slim, ((pool_rows, width), bf16), ((pool_rows, width), bf16), rank8], [],
        [pltpu.VMEM((model, width), bf16), pltpu.VMEM((model, width), bf16), acc, acc, dma_sems(pieces), dma_sems(pieces)], 3 * dense)
    got = swap_cores(grad_part)
    pool_part, *cross_grads = call(
        bind(cross_weights), "cross_weights", [table], [low_cross, cmixture, h_two, dcq, pool, dck, dcv], cross_w,
        [((pool_rows, model), bf16)], [((grad_rows, 4 * width), bf16)] * pieces,
        [pltpu.VMEM((model, 2 * width), bf16), pltpu.VMEM((4, model, width), bf16), dma_sems(pieces), dma_sems(pieces, 4)],
        2 * dense + 8 * pool_rows * model * width)
    d_cross = reduce_pieces(cross_grads, count)
    grad_self, low_self, grad_part, dq, dk, dv, sums_two = call(
        bind(self_back), "self_back", [table],
        [grad_cross, after_self, norm_rows, grad_part, got, attend, mixture, queries, keys, values, cosine, sine], self_w,
        [tall, low, low, slim, slim, slim, rank8], [],
        [pltpu.VMEM((model, 4 * width), bf16), dma_sems(pieces)], 5 * dense)
    got = swap_cores(grad_part)
    self_grads = call(
        bind(self_weights), "self_weights", [table], [low_self, mixture, h_one, dq, dk, dv], [],
        [], [((grad_rows, 4 * width), bf16)] * pieces,
        [pltpu.VMEM((4, model, width), bf16), dma_sems(pieces, 4)], 4 * dense)
    d_self = reduce_pieces(self_grads, count)
    grad_input, sums_one = call(
        input_back, "input_back", [], [grad_self, stream, norm_rows, grad_part, got], [], [tall, rank8], [], [], rows * model)
    grad_input = part_of(grad_input, here, inputs.shape[0])
    pool_half = pool_rows // 2
    pool_here = lax.axis_index("tensor") * pool_half
    grad_pool = wide(part_of(pool_part, pool_here, pool_half)) + wide(
        swap_cores(part_of(pool_part, pool_half - pool_here, pool_half))
    )
    sums = jnp.concatenate([sums_one[:2], sums_two[:2], sums_three[:2], jnp.zeros((2, model), f32)], axis=0)
    sums = sum_small(sums, count)
    mine = lax.dynamic_slice_in_dim(sums, lax.axis_index("dp") * shard_rows, shard_rows, 1)

    def cut(array, index, size):
        return array[:, index * size : (index + 1) * size]

    return (
        result.astype(bf16),
        grad_input,
        grad_pool.reshape(neighbours.shape),
        mine[0],
        mine[1],
        mine[2],
        mine[3],
        mine[4],
        mine[5],
        cut(d_self, 0, width),
        cut(d_self, 1, width),
        cut(d_self, 2, width),
        cut(d_cross, 0, width),
        cut(d_cross, 1, width),
        cut(d_cross, 2, width),
        cut(d_ff, 0, hidden),
        cut(d_self, 3, width).T,
        cut(d_cross, 3, width).T,
        cut(d_ff, 1, hidden).T,
    )


def solution(mesh):
    both = P(("dp", "tensor"), None)
    pool = P(("dp", "tensor"), None, None)
    norm = P("dp")
    tall, flat = P("dp", "tensor"), P("tensor", "dp")
    return jax.shard_map(
        functools.partial(on_device, mesh.shape["dp"]),
        mesh=mesh,
        in_specs=(both, pool, P("dp", None)) + (norm,) * 6 + (tall,) * 7 + (flat,) * 3 + (both,),
        out_specs=(both, both, pool) + (norm,) * 6 + (tall,) * 7 + (flat,) * 3,
        check_vma=False,
    )
```

time: 604 us -> 341 us (0.56)
  waiting for transfers between devices: 365 us -> 143 us
  starting transfers between devices: 0.86 us -> 99.1 us
  matrix products: 71.7 us -> 0 us
  local copies, waits for them, and re-layouts: 87.1 us -> 28.8 us
  Pallas kernels: 0 us -> 47.7 us
  other arithmetic: 38.5 us -> 15.2 us
  blocking collectives: 18.4 us -> 0 us
  between operations: 15.4 us -> 2.42 us
    reduce_scatter x8 -> x0, waiting for transfers between devices: 189 us -> none  [the longest x1 171 us: on_device(): lax.psum_scatter(grads, 'dp', scatter_dimension=0, tiled=True)]
    all_gather x3 -> x0, waiting for transfers between devices: 176 us -> none  [the longest x2 169 us: on_device(): full = [lax.all_gather(part, 'dp', axis=0, tiled=True) for part in packed]]
    ppermute x0 -> x68, waiting for transfers between devices: none -> 143 us  [the longest x4 30.6 us: sum_small(): lax.ppermute(array, 'dp', [(i, i ^ step) for i in range(count)])]
    ppermute x0 -> x68, starting transfers between devices: none -> 99.1 us  [the longest x3 26.8 us: reduce_pieces(): from_pair = send(own[half:].astype(bf16), perm=z_pair)]
    dot_general x44 -> x0, matrix products: 71.7 us -> none  [the longest x10 21.2 us: product(): return jnp.dot(left, right, preferred_element_type=jnp.float32)]
    pallas_call x0 -> x9, Pallas kernels: none -> 47.7 us  [call(): pl.pallas_call(body, name=name, out_shape=shapes, in_specs=[SMEM] * len(s...]
    reshape x13 -> x0, local copies, waits for them, and re-layouts: 30 us -> none  [the longest x3 7.86 us: on_device(): cvalues.reshape(pool_count, -1)[chosen]]
    convert_element_type x17 -> x0, local copies, waits for them, and re-layouts: 23.6 us -> none  [the longest x8 11.9 us: on_device(): grad.astype(jnp.bfloat16)]
  transfers between devices with their start and end apart: 11 -> 68, of which waited for: 8 -> 28; matrix products, arithmetic and copies ran while one was open for 14% -> 5% of each run, Pallas kernels for 0% -> 10%
where the time goes in v2:
time: 341 us; the launch traced here: 337 us
  waiting for transfers between devices  143 us (42%)
  starting transfers between devices  99.1 us (29%)
  Pallas kernels  47.7 us (14%)
  local copies, waits for them, and re-layouts  28.8 us (8%)
  other arithmetic  15.2 us (4%)
    pallas_call x9, Pallas kernels, call(): pl.pallas_call(body, name=name, out_shape=shapes, in_specs=[SMEM] * len(s...  47.7 us
    ppermute x4, waiting for transfers between devices, sum_small(): lax.ppermute(array, 'dp', [(i, i ^ step) for i in range(count)])  30.6 us
    ppermute x3, starting transfers between devices, reduce_pieces(): from_pair = send(own[half:].astype(bf16), perm=z_pair)  26.8 us
    ppermute x3, waiting for transfers between devices, gather_pieces(): outer = send(middle, perm=z_out)  24.6 us
    unnamed x170, local copies, waits for them, and re-layouts  22.8 us
    ppermute x3, waiting for transfers between devices, gather_pieces(): d_first = send(y_first, perm=x_swap)  15.1 us
    ppermute x3, starting transfers between devices, reduce_pieces(): from_out = send(other, perm=z_in)  13.6 us
    ppermute x3, waiting for transfers between devices, reduce_pieces(): from_y = send(d_second, perm=y_swap)  12.2 us
  transfers between devices with their start and end apart: 68, of which 28 were waited for; matrix products, arithmetic and copies ran while one was open for 5% of the time, Pallas kernels for 10%

profile of v2, /device:TPU:0, one launch (start us, length us, event | category | flops | bytes accessed | tf_op | source)
XLA Modules:
  0.0 336.6 jit_solution(10855633320915965147)
XLA Ops:
  4.5 3.1 collective-permute-start.12
  12.7 6.0 %collective-permute-done.23 = bf16[48,3072]{1,0:T(8,128)(2,1)S(1)} collective-permute-done((bf16[48,3072]{1,0:T(8,128)(2,1)S(1)}, bf16[48,3072]{1,0:T(8,128)(2,1)S(1)}, u32[]{:S(2)}, u32[]{:S(2)}) %collective-permute-start.23) | collective-permute-done | bytes 294944 | tf_op jit(solution)/shard_map/ppermute | solution.py:79
  26.4 7.7 %collective-permute-done.14 = bf16[96,1536]{1,0:T(8,128)(2,1)S(1)} collective-permute-done((bf16[96,1536]{1,0:T(8,128)(2,1)S(1)}, bf16[96,1536]{1,0:T(8,128)(2,1)S(1)}, u32[]{:S(2)}, u32[]{:S(2)}) %collective-permute-start.14) | collective-permute-done | bytes 294944 | tf_op jit(solution)/shard_map/ppermute | solution.py:82
  38.3 16.9 %collective-permute-done.3 = bf16[96,1664]{1,0:T(8,128)(2,1)S(1)} collective-permute-done((bf16[96,1664]{1,0:T(8,128)(2,1)S(1)}, bf16[96,1664]{1,0:T(8,128)(2,1)S(1)}, u32[]{:S(2)}, u32[]{:S(2)}) %collective-permute-start.3) | collective-permute-done | bytes 319520 | tf_op jit(solution)/shard_map/ppermute | solution.py:82
  57.4 4.8 %collective-permute-done.6.refs_4_ = bf16[96,1664]{1,0:T(8,128)(2,1)S(1)} collective-permute-done((bf16[96,1664]{1,0:T(8,128)(2,1)S(1)}, bf16[96,1664]{1,0:T(8,128)(2,1)S(1)}, u32[]{:S(2)}, u32[]{:S(2)}) %collective-permute-start.6) | collective-permute-done | bytes 319520 | tf_op jit(solution)/shard_map/ppermute | solution.py:85
  69.3 3.8 %collective-permute-done.8.refs_6_ = bf16[96,1664]{1,0:T(8,128)(2,1)S(1)} collective-permute-done((bf16[96,1664]{1,0:T(8,128)(2,1)S(1)}, bf16[96,1664]{1,0:T(8,128)(2,1)S(1)}, u32[]{:S(2)}, u32[]{:S(2)}) %collective-permute-start.8) | collective-permute-done | bytes 319520 | tf_op jit(solution)/shard_map/ppermute | solution.py:86
  74.6 11.6 %collective-permute-done.5.refs_3_ = bf16[96,1664]{1,0:T(8,128)(2,1)S(1)} collective-permute-done((bf16[96,1664]{1,0:T(8,128)(2,1)S(1)}, bf16[96,1664]{1,0:T(8,128)(2,1)S(1)}, u32[]{:S(2)}, u32[]{:S(2)}) %collective-permute-start.5) | collective-permute-done | bytes 319520 | tf_op jit(solution)/shard_map/ppermute | solution.py:87
  91.8 4.9 %collective-permute-done.9.refs_7_ = bf16[96,1664]{1,0:T(8,128)(2,1)S(1)} collective-permute-done((bf16[96,1664]{1,0:T(8,128)(2,1)S(1)}, bf16[96,1664]{1,0:T(8,128)(2,1)S(1)}, u32[]{:S(2)}, u32[]{:S(2)}) %collective-permute-start.9) | collective-permute-done | bytes 319520 | tf_op jit(solution)/shard_map/ppermute | solution.py:88
  98.3 7.7 %self_forward.1 = (bf16[256,768]{1,0:T(8,128)(2,1)S(1)}, bf16[256,768]{1,0:T(8,128)(2,1)S(1)}, bf16[256,384]{1,0:T(8,128)(2,1)S(1)}, bf16[256,384]{1,0:T(8,128)(...) custom-call(s32[32]{0:T(128)S(1)} %fusion.table, ...), custom_call_target="tpu_custom_call" | custom-call | flops 603979776 | bytes 5595136 | tf_op jit(solution)/shard_map/self_forward/pallas_call | solution.py:508
  113.7 4.2 %cross_forward.1 = (bf16[256,768]{1,0:T(8,128)(2,1)}, f32[256,768]{1,0:T(8,128)S(1)}, bf16[256,768]{1,0:T(8,128)(2,1)S(1)}, bf16[256,384]{1,0:T(8,128)(2,1)S(1)}...) custom-call(s32[32]{0:T(128)S(1)} %fusion.table, s32[8]{0:T(128)S(1)} %reshape.47.chosen, ...), custom_call_target="tpu_custom_call" | custom-call | flops 301989888 | bytes 7495680 | tf_op jit(solution)/shard_map/cross_forward/pallas_call | solution.py:508
  123.9 11.3 %collective-permute-done.30.refs_6_ = bf16[96,3072]{1,0:T(8,128)(2,1)} collective-permute-done((bf16[96,3072]{1,0:T(8,128)(2,1)}, bf16[96,3072]{1,0:T(8,128)(2,1)}, u32[]{:S(2)}, u32[]{:S(2)}) %collective-permute-start.30) | collective-permute-done | bytes 589856 | tf_op jit(solution)/shard_map/ppermute | solution.py:86
  137.8 12.4 %feed_forward.1 = (bf16[256,768]{1,0:T(8,128)(2,1)S(1)}, f32[256,768]{1,0:T(8,128)S(1)}, bf16[256,768]{1,0:T(8,128)(2,1)}, bf16[96,3072]{1,0:T(8,128)(2,1)S(1)},...) custom-call(s32[32]{0:T(128)S(1)} %fusion.table, ...), custom_call_target="tpu_custom_call" | custom-call | flops 3623878656 | bytes 13000704 | tf_op jit(solution)/shard_map/feed_forward/pallas_call | solution.py:508
  174.5 6.4 %cross_back.1 = (f32[256,768]{1,0:T(8,128)S(1)}, bf16[256,768]{1,0:T(8,128)(2,1)S(1)}, bf16[256,768]{1,0:T(8,128)(2,1)S(1)}, bf16[256,384]{1,0:T(8,128)(2,1)S(1)...) custom-call(s32[32]{0:T(128)S(1)} %fusion.table, s32[8]{0:T(128)S(1)} %reshape.47.chosen, ...), custom_call_target="tpu_custom_call" | custom-call | flops 452984832 | bytes 9682944 | tf_op jit(solution)/shard_map/cross_back/pallas_call | solution.py:508
  180.9 6.5 %cross_weights.1 = (bf16[768,768]{1,0:T(8,128)(2,1)S(1)}, bf16[96,1536]{1,0:T(8,128)(2,1)S(1)}, bf16[96,1536]{1,0:T(8,128)(2,1)S(1)}, bf16[96,1536]{1,0:T(8,128)...) custom-call(s32[32]{0:T(128)S(1)} %fusion.table, ...), custom_call_target="tpu_custom_call" | custom-call | flops 2113929216 | bytes 9437184 | tf_op jit(solution)/shard_map/cross_weights/pallas_call | solution.py:508
  191.6 5.8 %collective-permute-done.53 = bf16[96,1536]{1,0:T(8,128)(2,1)S(1)} collective-permute-done((bf16[96,1536]{1,0:T(8,128)(2,1)S(1)}, bf16[96,1536]{1,0:T(8,128)(2,1)S(1)}, u32[]{:S(2)}, u32[]{:S(2)}) %collective-permute-start.53) | collective-permute-done | bytes 294944 | tf_op jit(solution)/shard_map/ppermute | solution.py:104
  200.7 4.8 %self_back.1 = (f32[256,768]{1,0:T(8,128)S(1)}, bf16[256,768]{1,0:T(8,128)(2,1)S(1)}, bf16[256,768]{1,0:T(8,128)(2,1)S(1)}, bf16[256,384]{1,0:T(8,128)(2,1)S(1)}...) custom-call(s32[32]{0:T(128)S(1)} %fusion.table, ...), custom_call_target="tpu_custom_call" | custom-call | flops 754974720 | bytes 8962048 | tf_op jit(solution)/shard_map/self_back/pallas_call | solution.py:508
  205.6 2.9 self_weights.1
  212.4 6.4 %collective-permute-done.44 = bf16[96,1536]{1,0:T(8,128)(2,1)S(1)} collective-permute-done((bf16[96,1536]{1,0:T(8,128)(2,1)S(1)}, bf16[96,1536]{1,0:T(8,128)(2,1)S(1)}, u32[]{:S(2)}, u32[]{:S(2)}) %collective-permute-start.44) | collective-permute-done | bytes 294944 | tf_op jit(solution)/shard_map/ppermute | solution.py:104
  224.3 12.6 %collective-permute-done.37 = f32[8,768]{1,0:T(8,128)S(1)} collective-permute-done((f32[8,768]{1,0:T(8,128)S(1)}, f32[8,768]{1,0:T(8,128)S(1)}, u32[]{:S(2)}, u32[]{:S(2)}) %collective-permute-start.37) | collective-permute-done | bytes 24608 | tf_op jit(solution)/shard_map/ppermute | solution.py:123
  240.7 11.6 %collective-permute-done.38 = f32[8,768]{1,0:T(8,128)S(1)} collective-permute-done((f32[8,768]{1,0:T(8,128)S(1)}, f32[8,768]{1,0:T(8,128)S(1)}, u32[]{:S(2)}, u32[]{:S(2)}) %collective-permute-start.38) | collective-permute-done | bytes 24608 | tf_op jit(solution)/shard_map/ppermute | solution.py:123
  253.1 3.0 collective-permute-done.39
  258.0 3.5 %collective-permute-done.40 = f32[8,768]{1,0:T(8,128)S(1)} collective-permute-done((f32[8,768]{1,0:T(8,128)S(1)}, f32[8,768]{1,0:T(8,128)S(1)}, u32[]{:S(2)}, u32[]{:S(2)}) %collective-permute-start.40) | collective-permute-done | bytes 24608 | tf_op jit(solution)/shard_map/ppermute | solution.py:123
  264.3 4.8 %collective-permute-done.45 = bf16[96,1536]{1,0:T(8,128)(2,1)S(1)} collective-permute-done((bf16[96,1536]{1,0:T(8,128)(2,1)S(1)}, bf16[96,1536]{1,0:T(8,128)(2,1)S(1)}, u32[]{:S(2)}, u32[]{:S(2)}) %collective-permute-start.45) | collective-permute-done | bytes 294944 | tf_op jit(solution)/shard_map/ppermute | solution.py:107
  273.5 7.8 %collective-permute-start.47 = (bf16[96,1536]{1,0:T(8,128)(2,1)S(1)}, bf16[96,1536]{1,0:T(8,128)(2,1)S(1)}, u32[]{:S(2)}, u32[]{:S(2)}) collective-permute-start(bf16[96,1536]{1,0:T(8,128)(2,1)S(1)} %add_convert_fusion.9), channel_id=1, source_target_pairs={{0,8},{2,10},{4,12},{6,14},{24,16},{26,18},{28,20},{30,22},{1,9},{... | collective-permute-start | bytes 884744 | tf_op jit(solution)/shard_map/ppermute | solution.py:111
  281.4 4.0 %collective-permute-done.47 = bf16[96,1536]{1,0:T(8,128)(2,1)S(1)} collective-permute-done((bf16[96,1536]{1,0:T(8,128)(2,1)S(1)}, bf16[96,1536]{1,0:T(8,128)(2,1)S(1)}, u32[]{:S(2)}, u32[]{:S(2)}) %collective-permute-start.47) | collective-permute-done | bytes 294944 | tf_op jit(solution)/shard_map/ppermute | solution.py:111
  285.4 2.5 collective-permute-start.58
  288.0 4.2 %collective-permute-done.58 = bf16[48,1536]{1,0:T(8,128)(2,1)S(1)} collective-permute-done((bf16[48,1536]{1,0:T(8,128)(2,1)S(1)}, bf16[48,1536]{1,0:T(8,128)(2,1)S(1)}, u32[]{:S(2)}, u32[]{:S(2)}) %collective-permute-start.58) | collective-permute-done | bytes 147488 | tf_op jit(solution)/shard_map/ppermute | solution.py:116
  292.2 4.4 %collective-permute-start.65 = (bf16[96,3072]{1,0:T(8,128)(2,1)S(1)}, bf16[96,3072]{1,0:T(8,128)(2,1)S(1)}, u32[]{:S(2)}, u32[]{:S(2)}) collective-permute-start(bf16[96,3072]{1,0:T(8,128)(2,1)S(1)} %add_convert_fusion.1), channel_id=1, source_target_pairs={{0,8},{2,10},{4,12},{6,14},{24,16},{26,18},{28,20},{30,22},{1,9},{... | collective-permute-start | bytes 1769480 | tf_op jit(solution)/shard_map/ppermute | solution.py:111
  297.4 6.6 %collective-permute-done.65 = bf16[96,3072]{1,0:T(8,128)(2,1)S(1)} collective-permute-done((bf16[96,3072]{1,0:T(8,128)(2,1)S(1)}, bf16[96,3072]{1,0:T(8,128)(2,1)S(1)}, u32[]{:S(2)}, u32[]{:S(2)}) %collective-permute-start.65) | collective-permute-done | bytes 589856 | tf_op jit(solution)/shard_map/ppermute | solution.py:111
  305.8 16.1 %collective-permute-start.49 = (bf16[48,1536]{1,0:T(8,128)(2,1)S(1)}, bf16[48,1536]{1,0:T(8,128)(2,1)S(1)}, u32[]{:S(2)}, u32[]{:S(2)}) collective-permute-start(bf16[48,1536]{1,0:T(8,128)(2,1)S(1)} %slice.196), channel_id=1, source_target_pairs={{0,8},{2,10},{4,12},{6,14},{8,0},{10,2},{12,4},{14,6},{16,24},{18,... | collective-permute-start | bytes 442376 | tf_op jit(solution)/shard_map/ppermute | solution.py:116
  322.3 8.2 %collective-permute-start.67 = (bf16[48,3072]{1,0:T(8,128)(2,1)S(1)}, bf16[48,3072]{1,0:T(8,128)(2,1)S(1)}, u32[]{:S(2)}, u32[]{:S(2)}) collective-permute-start(bf16[48,3072]{1,0:T(8,128)(2,1)S(1)} %slice.194), channel_id=1, source_target_pairs={{0,8},{2,10},{4,12},{6,14},{8,0},{10,2},{12,4},{14,6},{16,24},{18,... | collective-permute-start | bytes 884744 | tf_op jit(solution)/shard_map/ppermute | solution.py:116
  331.3 3.9 %collective-permute-done.67 = bf16[48,3072]{1,0:T(8,128)(2,1)S(1)} collective-permute-done((bf16[48,3072]{1,0:T(8,128)(2,1)S(1)}, bf16[48,3072]{1,0:T(8,128)(2,1)S(1)}, u32[]{:S(2)}, u32[]{:S(2)}) %collective-permute-start.67) | collective-permute-done | bytes 294944 | tf_op jit(solution)/shard_map/ppermute | solution.py:116
  (359 shorter events, 113.9 us)
Async XLA Ops:
  19.5 15.8 %collective-permute-start.24 = (bf16[96,3072]{1,0:T(8,128)(2,1)}, bf16[96,3072]{1,0:T(8,128)(2,1)S(1)}, u32[]{:S(2)}, u32[]{:S(2)}) collective-permute-start(bf16[96,3072]{1,0:T(8,128)(2,1)} %pad_maximum_fusion.1.refs_0_), channel_id=1, source_target_pairs={{8,16},{10,18},{12,20},{14,22},{16,8},{18,10},{20,12},{22,14},{9,1... | collective-permute-start | bytes 1769480 | tf_op jit(solution)/shard_map/ppermute | solution.py:81
  23.2 13.5 %collective-permute-start = (bf16[128,768]{1,0:T(8,128)(2,1)}, bf16[128,768]{1,0:T(8,128)(2,1)S(1)}, u32[]{:S(2)}, u32[]{:S(2)}) collective-permute-start(bf16[128,768]{1,0:T(8,128)(2,1)} %param.23), channel_id=1, source_target_pairs={{0,1},{1,0},{2,3},{3,2},{4,5},{5,4},{6,7},{7,6},{8,9},{9,8},{10,11... | collective-permute-start | bytes 589832 | tf_op jit(solution)/shard_map/ppermute | solution.py:129
  23.3 32.4 %collective-permute-start.22 = (bf16[128,768]{1,0:T(8,128)(2,1)}, bf16[128,768]{1,0:T(8,128)(2,1)}, u32[]{:S(2)}, u32[]{:S(2)}) collective-permute-start(bf16[128,768]{1,0:T(8,128)(2,1)} %param.42), channel_id=1, source_target_pairs={{0,1},{1,0},{2,3},{3,2},{4,5},{5,4},{6,7},{7,6},{8,9},{9,8},{10,11... | collective-permute-start | bytes 589832 | tf_op jit(solution)/shard_map/ppermute | solution.py:129
  24.7 31.1 %collective-permute-start.17 = (bf16[96,1536]{1,0:T(8,128)(2,1)S(1)}, bf16[96,1536]{1,0:T(8,128)(2,1)S(1)}, u32[]{:S(2)}, u32[]{:S(2)}) collective-permute-start(bf16[96,1536]{1,0:T(8,128)(2,1)S(1)} %pad_maximum_fusion.5.refs_0_), channel_id=1, source_target_pairs={{0,4},{2,6},{4,0},{6,2},{8,12},{10,14},{12,8},{14,10},{16,20},{18,... | collective-permute-start | bytes 884744 | tf_op jit(solution)/shard_map/ppermute | solution.py:85
  34.1 21.1 %collective-permute-start.3 = (bf16[96,1664]{1,0:T(8,128)(2,1)S(1)}, bf16[96,1664]{1,0:T(8,128)(2,1)S(1)}, u32[]{:S(2)}, u32[]{:S(2)}) collective-permute-start(bf16[96,1664]{1,0:T(8,128)(2,1)S(1)} %collective-permute-done.2), channel_id=1, source_target_pairs={{8,0},{10,2},{12,4},{14,6},{16,24},{18,26},{20,28},{22,30},{9,1},{... | collective-permute-start | bytes 958472 | tf_op jit(solution)/shard_map/ppermute | solution.py:82
  35.4 28.8 %collective-permute-start.25 = (bf16[96,3072]{1,0:T(8,128)(2,1)S(1)}, bf16[96,3072]{1,0:T(8,128)(2,1)S(1)}, u32[]{:S(2)}, u32[]{:S(2)}) collective-permute-start(bf16[96,3072]{1,0:T(8,128)(2,1)S(1)} %collective-permute-done.24), channel_id=1, source_target_pairs={{8,0},{10,2},{12,4},{14,6},{16,24},{18,26},{20,28},{22,30},{9,1},{... | collective-permute-start | bytes 1769480 | tf_op jit(solution)/shard_map/ppermute | solution.py:82
  36.7 26.9 %collective-permute-start.15 = (bf16[96,1536]{1,0:T(8,128)(2,1)S(1)}, bf16[96,1536]{1,0:T(8,128)(2,1)S(1)}, u32[]{:S(2)}, u32[]{:S(2)}) collective-permute-start(bf16[96,1536]{1,0:T(8,128)(2,1)S(1)} %pad_maximum_fusion.5.refs_0_), channel_id=1, source_target_pairs={{0,2},{2,0},{4,6},{6,4},{8,10},{10,8},{12,14},{14,12},{16,18},{18,... | collective-permute-start | bytes 884744 | tf_op jit(solution)/shard_map/ppermute | solution.py:85
  63.7 24.1 %collective-permute-start.16 = (bf16[96,1536]{1,0:T(8,128)(2,1)S(1)}, bf16[96,1536]{1,0:T(8,128)(2,1)S(1)}, u32[]{:S(2)}, u32[]{:S(2)}) collective-permute-start(bf16[96,1536]{1,0:T(8,128)(2,1)S(1)} %broadcast_select_fusion.4.refs_1_), channel_id=1, source_target_pairs={{0,2},{2,0},{4,6},{6,4},{8,10},{10,8},{12,14},{14,12},{16,18},{18,... | collective-permute-start | bytes 884744 | tf_op jit(solution)/shard_map/ppermute | solution.py:87
  64.2 22.1 %collective-permute-start.5 = (bf16[96,1664]{1,0:T(8,128)(2,1)S(1)}, bf16[96,1664]{1,0:T(8,128)(2,1)S(1)}, u32[]{:S(2)}, u32[]{:S(2)}) collective-permute-start(bf16[96,1664]{1,0:T(8,128)(2,1)S(1)} %broadcast_select_fusion.3.refs_1_), channel_id=1, source_target_pairs={{0,2},{2,0},{4,6},{6,4},{8,10},{10,8},{12,14},{14,12},{16,18},{18,... | collective-permute-start | bytes 958472 | tf_op jit(solution)/shard_map/ppermute | solution.py:87
  66.6 40.8 %collective-permute-start.28 = (bf16[96,3072]{1,0:T(8,128)(2,1)}, bf16[96,3072]{1,0:T(8,128)(2,1)}, u32[]{:S(2)}, u32[]{:S(2)}) collective-permute-start(bf16[96,3072]{1,0:T(8,128)(2,1)} %pad_maximum_fusion.1.refs_0_), channel_id=1, source_target_pairs={{0,4},{2,6},{4,0},{6,2},{8,12},{10,14},{12,8},{14,10},{16,20},{18,... | collective-permute-start | bytes 1769480 | tf_op jit(solution)/shard_map/ppermute | solution.py:85
  67.8 38.3 %collective-permute-start.19 = (bf16[96,1536]{1,0:T(8,128)(2,1)S(1)}, bf16[96,1536]{1,0:T(8,128)(2,1)S(1)}, u32[]{:S(2)}, u32[]{:S(2)}) collective-permute-start(bf16[96,1536]{1,0:T(8,128)(2,1)S(1)} %collective-permute-done.17.refs_4_), channel_id=1, source_target_pairs={{0,2},{2,0},{4,6},{6,4},{8,10},{10,8},{12,14},{14,12},{16,18},{18,... | collective-permute-start | bytes 884744 | tf_op jit(solution)/shard_map/ppermute | solution.py:86
  73.1 18.1 %collective-permute-start.7 = (bf16[96,1664]{1,0:T(8,128)(2,1)S(1)}, bf16[96,1664]{1,0:T(8,128)(2,1)S(1)}, u32[]{:S(2)}, u32[]{:S(2)}) collective-permute-start(bf16[96,1664]{1,0:T(8,128)(2,1)S(1)} %broadcast_select_fusion.3.refs_1_), channel_id=1, source_target_pairs={{0,4},{2,6},{4,0},{6,2},{8,12},{10,14},{12,8},{14,10},{16,20},{18,... | collective-permute-start | bytes 958472 | tf_op jit(solution)/shard_map/ppermute | solution.py:87
  87.8 22.1 %collective-permute-start.27 = (bf16[96,3072]{1,0:T(8,128)(2,1)}, bf16[96,3072]{1,0:T(8,128)(2,1)}, u32[]{:S(2)}, u32[]{:S(2)}) collective-permute-start(bf16[96,3072]{1,0:T(8,128)(2,1)} %broadcast_select_fusion.refs_1_), channel_id=1, source_target_pairs={{0,2},{2,0},{4,6},{6,4},{8,10},{10,8},{12,14},{14,12},{16,18},{18,... | collective-permute-start | bytes 1769480 | tf_op jit(solution)/shard_map/ppermute | solution.py:87
  91.2 17.6 %collective-permute-start.18 = (bf16[96,1536]{1,0:T(8,128)(2,1)S(1)}, bf16[96,1536]{1,0:T(8,128)(2,1)S(1)}, u32[]{:S(2)}, u32[]{:S(2)}) collective-permute-start(bf16[96,1536]{1,0:T(8,128)(2,1)S(1)} %broadcast_select_fusion.4.refs_1_), channel_id=1, source_target_pairs={{0,4},{2,6},{4,0},{6,2},{8,12},{10,14},{12,8},{14,10},{16,20},{18,... | collective-permute-start | bytes 884744 | tf_op jit(solution)/shard_map/ppermute | solution.py:87
  107.4 16.6 %collective-permute-start.26 = (bf16[96,3072]{1,0:T(8,128)(2,1)}, bf16[96,3072]{1,0:T(8,128)(2,1)}, u32[]{:S(2)}, u32[]{:S(2)}) collective-permute-start(bf16[96,3072]{1,0:T(8,128)(2,1)} %pad_maximum_fusion.1.refs_0_), channel_id=1, source_target_pairs={{0,2},{2,0},{4,6},{6,4},{8,10},{10,8},{12,14},{14,12},{16,18},{18,... | collective-permute-start | bytes 1769480 | tf_op jit(solution)/shard_map/ppermute | solution.py:85
  108.8 26.4 %collective-permute-start.30 = (bf16[96,3072]{1,0:T(8,128)(2,1)}, bf16[96,3072]{1,0:T(8,128)(2,1)}, u32[]{:S(2)}, u32[]{:S(2)}) collective-permute-start(bf16[96,3072]{1,0:T(8,128)(2,1)} %collective-permute-done.28.refs_4_), channel_id=1, source_target_pairs={{0,2},{2,0},{4,6},{6,4},{8,10},{10,8},{12,14},{14,12},{16,18},{18,... | collective-permute-start | bytes 1769480 | tf_op jit(solution)/shard_map/ppermute | solution.py:86
  109.4 25.8 %collective-permute-start.29 = (bf16[96,3072]{1,0:T(8,128)(2,1)}, bf16[96,3072]{1,0:T(8,128)(2,1)}, u32[]{:S(2)}, u32[]{:S(2)}) collective-permute-start(bf16[96,3072]{1,0:T(8,128)(2,1)} %broadcast_select_fusion.refs_1_), channel_id=1, source_target_pairs={{0,4},{2,6},{4,0},{6,2},{8,12},{10,14},{12,8},{14,10},{16,20},{18,... | collective-permute-start | bytes 1769480 | tf_op jit(solution)/shard_map/ppermute | solution.py:87
  109.9 26.8 %collective-permute-start.31 = (bf16[96,3072]{1,0:T(8,128)(2,1)}, bf16[96,3072]{1,0:T(8,128)(2,1)}, u32[]{:S(2)}, u32[]{:S(2)}) collective-permute-start(bf16[96,3072]{1,0:T(8,128)(2,1)} %collective-permute-done.27.refs_3_), channel_id=1, source_target_pairs={{0,4},{2,6},{4,0},{6,2},{8,12},{10,14},{12,8},{14,10},{16,20},{18,... | collective-permute-start | bytes 1769480 | tf_op jit(solution)/shard_map/ppermute | solution.py:88
  121.8 13.4 %collective-permute-start.21 = (bf16[256,768]{1,0:T(8,128)(2,1)}, bf16[256,768]{1,0:T(8,128)(2,1)}, u32[]{:S(2)}, u32[]{:S(2)}) collective-permute-start(bf16[256,768]{1,0:T(8,128)(2,1)} %get-tuple-element.84.own_ref), channel_id=1, source_target_pairs={{0,1},{1,0},{2,3},{3,2},{4,5},{5,4},{6,7},{7,6},{8,9},{9,8},{10,11... | collective-permute-start | bytes 1179656 | tf_op jit(solution)/shard_map/ppermute | solution.py:129
  160.4 27.7 %collective-permute-start.62 = (bf16[96,3072]{1,0:T(8,128)(2,1)}, bf16[96,3072]{1,0:T(8,128)(2,1)S(1)}, u32[]{:S(2)}, u32[]{:S(2)}) collective-permute-start(bf16[96,3072]{1,0:T(8,128)(2,1)} %copy-done.63), channel_id=1, source_target_pairs={{0,4},{2,6},{4,0},{6,2},{8,12},{10,14},{12,8},{14,10},{16,20},{18,... | collective-permute-start | bytes 1769480 | tf_op jit(solution)/shard_map/ppermute | solution.py:104
  160.9 76.6 %collective-permute-start.64 = (bf16[96,3072]{1,0:T(8,128)(2,1)}, bf16[96,3072]{1,0:T(8,128)(2,1)S(1)}, u32[]{:S(2)}, u32[]{:S(2)}) collective-permute-start(bf16[96,3072]{1,0:T(8,128)(2,1)} %copy-done.61), channel_id=1, source_target_pairs={{0,4},{2,6},{4,0},{6,2},{8,12},{10,14},{12,8},{14,10},{16,20},{18,... | collective-permute-start | bytes 1769480 | tf_op jit(solution)/shard_map/ppermute | solution.py:106
  162.4 27.4 %collective-permute-start.60 = (bf16[96,3072]{1,0:T(8,128)(2,1)}, bf16[96,3072]{1,0:T(8,128)(2,1)S(1)}, u32[]{:S(2)}, u32[]{:S(2)}) collective-permute-start(bf16[96,3072]{1,0:T(8,128)(2,1)} %copy-done.62), channel_id=1, source_target_pairs={{0,2},{2,0},{4,6},{6,4},{8,10},{10,8},{12,14},{14,12},{16,18},{18,... | collective-permute-start | bytes 1769480 | tf_op jit(solution)/shard_map/ppermute | solution.py:103
  163.9 158.1 %collective-permute-start.59 = (bf16[96,3072]{1,0:T(8,128)(2,1)}, bf16[96,3072]{1,0:T(8,128)(2,1)S(1)}, u32[]{:S(2)}, u32[]{:S(2)}) collective-permute-start(bf16[96,3072]{1,0:T(8,128)(2,1)} %copy-done.60), channel_id=1, source_target_pairs={{0,2},{2,0},{4,6},{6,4},{8,10},{10,8},{12,14},{14,12},{16,18},{18,... | collective-permute-start | bytes 1769480 | tf_op jit(solution)/shard_map/ppermute | solution.py:105
  188.0 22.2 %collective-permute-start.55 = (bf16[96,1536]{1,0:T(8,128)(2,1)S(1)}, bf16[96,1536]{1,0:T(8,128)(2,1)S(1)}, u32[]{:S(2)}, u32[]{:S(2)}) collective-permute-start(bf16[96,1536]{1,0:T(8,128)(2,1)S(1)} %get-tuple-element.130), channel_id=1, source_target_pairs={{0,4},{2,6},{4,0},{6,2},{8,12},{10,14},{12,8},{14,10},{16,20},{18,... | collective-permute-start | bytes 884744 | tf_op jit(solution)/shard_map/ppermute | solution.py:106
  208.5 62.3 %collective-permute-start.50 = (bf16[96,1536]{1,0:T(8,128)(2,1)S(1)}, bf16[96,1536]{1,0:T(8,128)(2,1)S(1)}, u32[]{:S(2)}, u32[]{:S(2)}) collective-permute-start(bf16[96,1536]{1,0:T(8,128)(2,1)S(1)} %get-tuple-element.124), channel_id=1, source_target_pairs={{0,2},{2,0},{4,6},{6,4},{8,10},{10,8},{12,14},{14,12},{16,18},{18,... | collective-permute-start | bytes 884744 | tf_op jit(solution)/shard_map/ppermute | solution.py:105
  220.5 18.4 %collective-permute-start.63 = (bf16[96,3072]{1,0:T(8,128)(2,1)S(1)}, bf16[96,3072]{1,0:T(8,128)(2,1)S(1)}, u32[]{:S(2)}, u32[]{:S(2)}) collective-permute-start(bf16[96,3072]{1,0:T(8,128)(2,1)S(1)} %add_convert_fusion.2), channel_id=1, source_target_pairs={{0,2},{2,0},{4,6},{6,4},{8,10},{10,8},{12,14},{14,12},{16,18},{18,... | collective-permute-start | bytes 1769480 | tf_op jit(solution)/shard_map/ppermute | solution.py:107
  236.8 85.1 %collective-permute-start.61 = (bf16[96,3072]{1,0:T(8,128)(2,1)S(1)}, bf16[96,3072]{1,0:T(8,128)(2,1)S(1)}, u32[]{:S(2)}, u32[]{:S(2)}) collective-permute-start(bf16[96,3072]{1,0:T(8,128)(2,1)S(1)} %add_convert_fusion.3), channel_id=1, source_target_pairs={{0,4},{2,6},{4,0},{6,2},{8,12},{10,14},{12,8},{14,10},{16,20},{18,... | collective-permute-start | bytes 1769480 | tf_op jit(solution)/shard_map/ppermute | solution.py:108
  237.4 19.2 %collective-permute-start.56 = (bf16[96,1536]{1,0:T(8,128)(2,1)S(1)}, bf16[96,1536]{1,0:T(8,128)(2,1)S(1)}, u32[]{:S(2)}, u32[]{:S(2)}) collective-permute-start(bf16[96,1536]{1,0:T(8,128)(2,1)S(1)} %add_convert_fusion.5), channel_id=1, source_target_pairs={{0,8},{2,10},{4,12},{6,14},{24,16},{26,18},{28,20},{30,22},{1,9},{... | collective-permute-start | bytes 884744 | tf_op jit(solution)/shard_map/ppermute | solution.py:111
  269.8 35.8 %collective-permute-start.41 = (bf16[96,1536]{1,0:T(8,128)(2,1)S(1)}, bf16[96,1536]{1,0:T(8,128)(2,1)S(1)}, u32[]{:S(2)}, u32[]{:S(2)}) collective-permute-start(bf16[96,1536]{1,0:T(8,128)(2,1)S(1)} %get-tuple-element.116), channel_id=1, source_target_pairs={{0,2},{2,0},{4,6},{6,4},{8,10},{10,8},{12,14},{14,12},{16,18},{18,... | collective-permute-start | bytes 884744 | tf_op jit(solution)/shard_map/ppermute | solution.py:105
  270.9 34.8 %collective-permute-start.43 = (bf16[96,1536]{1,0:T(8,128)(2,1)S(1)}, bf16[96,1536]{1,0:T(8,128)(2,1)S(1)}, u32[]{:S(2)}, u32[]{:S(2)}) collective-permute-start(bf16[96,1536]{1,0:T(8,128)(2,1)S(1)} %add_convert_fusion.11), channel_id=1, source_target_pairs={{0,4},{2,6},{4,0},{6,2},{8,12},{10,14},{12,8},{14,10},{16,20},{18,... | collective-permute-start | bytes 884744 | tf_op jit(solution)/shard_map/ppermute | solution.py:108
  304.9 17.0 %collective-permute-start.66 = (bf16[96,3072]{1,0:T(8,128)(2,1)S(1)}, bf16[96,3072]{1,0:T(8,128)(2,1)S(1)}, u32[]{:S(2)}, u32[]{:S(2)}) collective-permute-start(bf16[96,3072]{1,0:T(8,128)(2,1)S(1)} %add_convert_fusion), channel_id=1, source_target_pairs={{8,16},{10,18},{12,20},{14,22},{16,8},{18,10},{20,12},{22,14},{9,1... | collective-permute-start | bytes 1769480 | tf_op jit(solution)/shard_map/ppermute | solution.py:113
  305.8 24.7 %collective-permute-start.49 = (bf16[48,1536]{1,0:T(8,128)(2,1)S(1)}, bf16[48,1536]{1,0:T(8,128)(2,1)S(1)}, u32[]{:S(2)}, u32[]{:S(2)}) collective-permute-start(bf16[48,1536]{1,0:T(8,128)(2,1)S(1)} %slice.196), channel_id=1, source_target_pairs={{0,8},{2,10},{4,12},{6,14},{8,0},{10,2},{12,4},{14,6},{16,24},{18,... | collective-permute-start | bytes 442376 | tf_op jit(solution)/shard_map/ppermute | solution.py:116
  (120 other events, 1005.3 us)

commit v3 on v2

--- a/solution.py
+++ b/solution.py
@@ -19,7 +19,8 @@
 GELU_A = 0.7978845608028654
 GELU_B = 0.044715
 PLANES = 4
-VMEM_BYTES = 40 * 2**20
+BLOCKS = 16
+MIB = 2**20
 
 bf16 = jnp.bfloat16
 f32 = jnp.float32
@@ -42,87 +43,249 @@
 
 
 def grid_perms(count):
-    x_swap = [(i, i ^ 1) for i in range(count)]
-    y_swap = [(i, i ^ 2) for i in range(count)]
-    z_pair = [(i, i ^ 4) for i in range(count)]
-    z_mid = [(i, 12 - 4 * (i // 4) + i % 4) for i in range(4, 12)]
-    z_out = [(i, i ^ 4) for i in range(4, 12)]
-    z_in = [(i ^ 4, i) for i in range(4, 12)]
-    return x_swap, y_swap, z_pair, z_mid, z_out, z_in
+    steps = {"x": 1, "y": 2, "near": 4, "far": 8}
+    return {name: [(i, i ^ step) for i in range(count)] for name, step in steps.items()}
 
 
 def block_tables(count):
-    table = np.zeros((count, 2 * count), np.int32)
-    for device in range(count):
-        z, y, x = device // 4, device // 2 % 2, device % 2
-        inner = 1 if z in (1, 2) else 0
-        slot = 0
-        for plane in range(PLANES):
-            column = 2 * (y ^ (plane >> 1)) + (x ^ (plane & 1))
-            for half in range(2):
-                for j in range(2):
-                    table[device, slot] = 4 * (z ^ (2 * half + (j ^ (half & inner)))) + column
-                    table[device, count + slot] = 4 * (z ^ (2 * half + j)) + column
-                    slot += 1
-    return table
+    orders = [
+        [4 * z + plane for plane in range(PLANES) for z in (0, 2, 1, 3)],
+        [4 * z + plane for z in (0, 2, 1, 3) for plane in range(PLANES)],
+    ]
+    return np.array([[[device ^ step for step in order] for device in range(count)] for order in orders], np.int32)
 
 
 def pieces_ok(count, rows):
-    return count == 16 and rows % 16 == 0
-
-
-def gather_pieces(shard, count):
-    if not pieces_ok(count, shard.shape[0]):
-        return (lax.all_gather(shard, "dp", axis=0, tiled=True),)
-    x_swap, y_swap, z_pair, z_mid, z_out, _ = grid_perms(count)
-    send = functools.partial(lax.ppermute, axis_name="dp")
-    buddy = send(shard, perm=z_pair)
-    first = jnp.concatenate([shard, buddy], axis=0)
-    middle = send(first, perm=z_mid)
-    outer = send(middle, perm=z_out)
-    is_inner = (lax.axis_index("dp") // 4) % 3 != 0
-    second = jnp.where(is_inner, middle, outer)
-    x_first, y_first = send(first, perm=x_swap), send(first, perm=y_swap)
-    d_first = send(y_first, perm=x_swap)
-    x_second, y_second = send(second, perm=x_swap), send(second, perm=y_swap)
-    d_second = send(x_second, perm=y_swap)
-    return (first, second, x_first, x_second, y_first, y_second, d_first, d_second)
-
-
-def swap_blocks(array):
-    half = array.shape[0] // 2
-    return jnp.concatenate([array[half:], array[:half]], axis=0)
-
-
-def reduce_pieces(pieces, count):
-    if len(pieces) == 1:
-        return wide(lax.psum_scatter(pieces[0], "dp", scatter_dimension=0, tiled=True))
-    first, second, x_first, x_second, y_first, y_second, d_first, d_second = pieces
-    x_swap, y_swap, z_pair, z_mid, _, z_in = grid_perms(count)
-    send = functools.partial(lax.ppermute, axis_name="dp")
-    from_x = send(d_first, perm=x_swap)
-    from_y = send(d_second, perm=y_swap)
-    got_x_first = send(x_first, perm=x_swap)
-    got_y_second = send(y_second, perm=y_swap)
-    got_x_second = send((wide(x_second) + wide(from_y)).astype(bf16), perm=x_swap)
-    got_y_first = send((wide(y_first) + wide(from_x)).astype(bf16), perm=y_swap)
-    other = (wide(second) + wide(got_x_second) + wide(got_y_second)).astype(bf16)
-    own = wide(first) + wide(got_x_first) + wide(got_y_first)
-    from_out = send(other, perm=z_in)
-    other = (wide(other) + wide(swap_blocks(from_out))).astype(bf16)
-    from_mid = send(other, perm=z_mid)
-    own = own + wide(swap_blocks(from_mid))
-    half = own.shape[0] // 2
-    from_pair = send(own[half:].astype(bf16), perm=z_pair)
-    return own[:half] + wide(from_pair)
-
-
-def sum_small(array, count):
-    step = 1
-    while step < count:
-        array = array + lax.ppermute(array, "dp", [(i, i ^ step) for i in range(count)])
-        step *= 2
-    return array
+    return count == BLOCKS and rows % 16 == 0
+
+
+def tie(arrays, gate=()):
+    arrays = tuple(arrays)
+    if len(arrays) + len(gate) < 2:
+        return arrays
+    return lax.optimization_barrier(arrays + tuple(gate))[: len(arrays)]
+
+
+def stack(*arrays):
+    return jnp.concatenate(arrays, axis=0)
+
+
+class Rounds:
+    def __init__(self, count):
+        self.perms = grid_perms(count)
+
+    def go(self, gate, *sends):
+        out = []
+        for array, name in sends:
+            (array,) = tie([array], gate)
+            out.append(lax.ppermute(array, "dp", self.perms[name]))
+        return out
+
+
+def gather_all(a, b, c, d, count, early):
+    if not pieces_ok(count, a.shape[0]):
+        gathered = [(lax.all_gather(shard, "dp", axis=0, tiled=True),) for shard in (a, b, c, d)]
+        return gathered + [(), (), ()]
+    go = Rounds(count).go
+    (a_far,) = go((), (a, "far"))
+    d_x, d_y = go((), (d, "x"), (d, "y"))
+    a1 = stack(a, a_far)
+    r0 = (d_x, d_y)
+    r1 = ax1, ay1, a2, d_d = go((), (a1, "x"), (a1, "y"), (a1, "near"), (d_y, "x"))
+    (b_far,) = go((a_far,), (b, "far"))
+    b1, column = stack(b, b_far), stack(d, d_x, d_y, d_d)
+    r2 = bx1, by1, b2, c_far = go(r0, (b1, "x"), (b1, "y"), (b1, "near"), (c, "far"))
+    c1 = stack(c, c_far)
+    r3 = ax2, ay2 = go(r1 + list(early), (a2, "x"), (a2, "y"))
+    (column_far,) = go(r1, (column, "far"))
+    r4 = bx2, by2 = go(r2, (b2, "x"), (b2, "y"))
+    (column_near,) = go(r2, (column, "near"))
+    r5 = ad1, ad2 = go(r3, (ay1, "x"), (ax2, "y"))
+    r6 = bd1, bd2, c2 = go(r4, (by1, "x"), (bx2, "y"), (c1, "near"))
+    r7 = cx1, cy1 = go(r5 + [column_far], (c1, "x"), (c1, "y"))
+    (column_both,) = go(r5, (column_far, "near"))
+    r8 = cx2, cy2 = go(r6 + [column_near], (c2, "x"), (c2, "y"))
+    cd1, cd2 = go(r7, (cy1, "x"), (cx2, "y"))
+    return [
+        (a1, a2, ax1, ax2, ay1, ay2, ad1, ad2),
+        (b1, b2, bx1, bx2, by1, by2, bd1, bd2),
+        (c1, c2, cx1, cx2, cy1, cy2, cd1, cd2),
+        (column, column_far, column_near, column_both),
+        tuple(r4),
+        tuple(r6),
+        tuple(r7),
+    ]
+
+
+def add_half(own, got):
+    return (wide(own) + wide(got)).astype(bf16)
+
+
+def add_diagonal(x_in, y_in, from_x, from_y, x_out, y_out, x_buf, y_buf, sems):
+    half = from_x.shape[0]
+    loads = [
+        pltpu.make_async_copy(x_in.at[pl.ds(half, half), :], x_buf, sems.at[0]),
+        pltpu.make_async_copy(y_in.at[pl.ds(0, half), :], y_buf, sems.at[1]),
+    ]
+    for load in loads:
+        load.start()
+    finish(loads)
+    x_buf[...] = add_half(x_buf[...], from_y[...])
+    y_buf[...] = add_half(y_buf[...], from_x[...])
+    stores = [
+        pltpu.make_async_copy(x_buf, x_out.at[pl.ds(half, half), :], sems.at[2]),
+        pltpu.make_async_copy(y_buf, y_out.at[pl.ds(0, half), :], sems.at[3]),
+    ]
+    for store in stores:
+        store.start()
+    finish(stores)
+
+
+def add_plane(own, got_x, got_y, kept, other):
+    half = kept.shape[0]
+    total = wide(own[...]) + wide(got_x[...]) + wide(got_y[...])
+    kept[...] = total[:half]
+    other[...] = total[half:].astype(bf16)
+
+
+def add_near(kept, got, mine, other):
+    rows = mine.shape[0]
+    total = kept[...] + wide(got[...])
+    mine[...] = total[:rows]
+    other[...] = total[rows:].astype(bf16)
+
+
+def write_outs(turned, total, outs):
+    start = 0
+    for out, flip in zip(outs, turned):
+        if flip:
+            columns = max(out.shape[0], LANES)
+            out[...] = total[:, start : start + columns].T[: out.shape[0]]
+            start += columns
+        else:
+            out[...] = total[:, start : start + out.shape[1]]
+            start += out.shape[1]
+
+
+def add_far(turned, mine, got, *outs):
+    write_outs(turned, mine[...] + wide(got[...]), outs)
+
+
+class Reduction:
+    def __init__(self, pieces, count, widths, turned):
+        self.pieces, self.widths, self.turned = pieces, widths, turned
+        self.perms = grid_perms(count)
+        self.ended = ()
+        self.outs = None
+        if len(pieces) == 1:
+            total = wide(lax.psum_scatter(pieces[0], "dp", scatter_dimension=0, tiled=True))
+            self.outs, start = [], 0
+            for width, flip in zip(widths, turned):
+                part = total[:, start : start + width]
+                self.outs.append(part.T if flip else part)
+                start += max(width, LANES)
+
+    def out_shapes(self, rows):
+        return [((width, rows) if flip else (rows, width), f32) for width, flip in zip(self.widths, self.turned)]
+
+    def send(self, arrays, names, gate):
+        out = []
+        for array, name in zip(arrays, names):
+            (array,) = tie([array], gate)
+            out.append(lax.ppermute(array, "dp", self.perms[name]))
+        self.ended = tie(out)
+        return self.ended
+
+    def diagonal(self, gate=()):
+        if self.outs is not None:
+            return
+        own, x_col, y_col, d_first, d_second = self.pieces
+        half, columns = d_first.shape
+        from_x, from_y = self.send([d_first, d_second], ["x", "y"], gate)
+        buffer = pltpu.VMEM((half, columns), bf16)
+        self.sides = pl.pallas_call(
+            add_diagonal, name="add_diagonal", out_shape=[pltpu.HBM(x_col.shape, bf16)] * 2,
+            in_specs=[HBM, HBM, VMEM, VMEM], out_specs=[HBM, HBM], input_output_aliases={0: 0, 1: 1},
+            scratch_shapes=[buffer, buffer, pltpu.SemaphoreType.DMA((4,))],
+            compiler_params=pltpu.CompilerParams(vmem_limit_bytes=60 * MIB), cost_estimate=cost(2),
+        )(x_col, y_col, from_x, from_y)
+
+    def plane(self, gate=()):
+        if self.outs is not None:
+            return
+        half, columns = self.pieces[3].shape
+        got_x, got_y = self.send(self.sides, ["x", "y"], gate)
+        self.kept, self.other = call(
+            add_plane, "add_plane", [], [self.pieces[0], got_x, got_y], [],
+            [((half, columns), f32), ((half, columns), bf16)], [], [], 2, mib=60)
+
+    def near(self, gate=()):
+        if self.outs is not None:
+            return
+        half, columns = self.pieces[3].shape
+        (got,) = self.send([self.other], ["near"], gate)
+        self.mine, self.other = call(
+            add_near, "add_near", [], [self.kept, got], [],
+            [((half // 2, columns), f32), ((half // 2, columns), bf16)], [], [], 1, mib=60)
+
+    def far(self, gate=()):
+        if self.outs is not None:
+            return
+        (got,) = self.send([self.other], ["far"], gate)
+        shapes = self.out_shapes(self.pieces[3].shape[0] // 2)
+        self.outs = call(
+            functools.partial(add_far, self.turned), "add_far", [], [self.mine, got], [], shapes, [], [], 1, mib=60)
+
+
+def add_two(left, right, out):
+    out[...] = add_half(left[...], right[...])
+
+
+def add_column(own, got_near, got_far, mine, x_out, y_out, d_out):
+    rows = mine.shape[0]
+    total = wide(own[...]) + wide(got_near[...]) + wide(got_far[...])
+    mine[...] = total[:rows]
+    for place, out in enumerate((x_out, y_out, d_out)):
+        out[...] = total[(place + 1) * rows : (place + 2) * rows].astype(bf16)
+
+
+def add_sides(turned, mine, got_x, got_y, *outs):
+    write_outs(turned, mine[...] + wide(got_x[...]) + wide(got_y[...]), outs)
+
+
+class FlatReduction(Reduction):
+    def near(self, gate=()):
+        if self.outs is not None:
+            return
+        own, across, beside, corner = self.pieces
+        (got_across,) = self.send([corner], ["near"], gate)
+        self.got_across = got_across
+        (self.got_own,) = self.send([beside], ["near"], gate)
+        (self.across,) = call(add_two, "add_two", [], [across, got_across], [], [(across.shape, bf16)], [], [], 1, mib=60)
+
+    def far(self, gate=()):
+        if self.outs is not None:
+            return
+        own = self.pieces[0]
+        (got,) = self.send([self.across], ["far"], gate)
+        self.rows = own.shape[0] // PLANES
+        block = (self.rows, own.shape[1])
+        self.mine, *self.sides = call(
+            add_column, "add_column", [], [own, self.got_own, got], [], [(block, f32)] + [(block, bf16)] * 3, [], [], 2, mib=60)
+
+    def diagonal(self, gate=()):
+        if self.outs is not None:
+            return
+        (got,) = self.send([self.sides[2]], ["x"], gate)
+        (self.y_side,) = call(add_two, "add_two", [], [self.sides[1], got], [], [(got.shape, bf16)], [], [], 1, mib=60)
+
+    def plane(self, gate=()):
+        if self.outs is not None:
+            return
+        got_x, got_y = self.send([self.sides[0], self.y_side], ["x", "y"], gate)
+        self.outs = call(
+            functools.partial(add_sides, self.turned), "add_sides", [], [self.mine, got_x, got_y], [],
+            self.out_shapes(self.rows), [], [], 1, mib=60)
 
 
 def swap_cores(array):
@@ -145,16 +308,19 @@
             pltpu.make_async_copy(pieces[0].at[:, pl.ds(start, size)], target, sems.at[sem_from])
         )
     else:
-        rows = pieces[0].shape[0] // 2
-        for slot in range(2 * len(pieces)):
-            first = pl.multiple_of(table[slot] * rows, 16)
-            copies.append(
-                pltpu.make_async_copy(
-                    pieces[slot // 2].at[pl.ds(slot % 2 * rows, rows), pl.ds(start, size)],
-                    target.at[pl.ds(first, rows), :],
-                    sems.at[sem_from + slot],
+        rows = target.shape[0] // table.shape[0]
+        slot = 0
+        for piece in pieces:
+            for j in range(piece.shape[0] // rows):
+                first = pl.multiple_of(table[slot] * rows, 16)
+                copies.append(
+                    pltpu.make_async_copy(
+                        piece.at[pl.ds(j * rows, rows), pl.ds(start, size)],
+                        target.at[pl.ds(first, rows), :],
+                        sems.at[sem_from + slot],
+                    )
                 )
-            )
+                slot += 1
     for copy in copies:
         copy.start()
     return copies
@@ -168,16 +334,19 @@
             pltpu.make_async_copy(source, pieces[0].at[:, pl.ds(start, size)], sems.at[sem_from])
         )
     else:
-        rows = pieces[0].shape[0] // 2
-        for slot in range(2 * len(pieces)):
-            first = pl.multiple_of(table[2 * len(pieces) + slot] * rows, 16)
-            copies.append(
-                pltpu.make_async_copy(
-                    source.at[pl.ds(first, rows), :],
-                    pieces[slot // 2].at[pl.ds(slot % 2 * rows, rows), pl.ds(start, size)],
-                    sems.at[sem_from + slot],
+        rows = source.shape[0] // table.shape[0]
+        slot = 0
+        for piece in pieces:
+            for j in range(piece.shape[0] // rows):
+                first = pl.multiple_of(table[slot] * rows, 16)
+                copies.append(
+                    pltpu.make_async_copy(
+                        source.at[pl.ds(first, rows), :],
+                        piece.at[pl.ds(j * rows, rows), pl.ds(start, size)],
+                        sems.at[sem_from + slot],
+                    )
                 )
-            )
+                slot += 1
     for copy in copies:
         copy.start()
     return copies
@@ -318,14 +487,17 @@
     part[...] = mm_nt(o_out[...], out_w[...]).astype(bf16)
 
 
-def feed_forward(count, slices, table, x_ref, own_ref, got_ref, norms, g_ref, *refs):
+def feed_forward(count, grad_count, slices, table, grad_table, side, x_ref, own_ref, got_ref, norms, g_ref, out_ref, back_ref, *refs):
     pieces, refs = refs[:count], refs[count:]
-    part, x_out, dh_out = refs[:3]
-    grads, refs = refs[3 : 3 + count], refs[3 + count :]
+    part, x_out, dh_out, mine, other = refs[:5]
+    grads, refs = refs[5 : 5 + grad_count], refs[5 + grad_count :]
     up_w, down_w, up_g, down_g, sems, sems_out = refs
+    half = mine.shape[0]
+    here = pl.ds(pl.multiple_of(side[0] * half, half), half)
+    there = pl.ds(pl.multiple_of((1 - side[0]) * half, half), half)
     total = up_w.shape[0] * up_w.shape[2]
     size = total // slices
-    block_count = max(1, 2 * count) if count > 1 else 1
+    block_count = table.shape[0] if count > 1 else 1
     copies = []
     for turn_of in range(slices):
         copies.append(
@@ -338,8 +510,8 @@
     hidden = (normal * norms[4:5] + norms[5:6]).astype(bf16)
     grad = g_ref[...]
     hidden_t, grad_t = hidden.T, grad.T
-    out = jnp.zeros(stream.shape, f32)
-    back = jnp.zeros(stream.shape, f32)
+    out = out_ref[...]
+    back = back_ref[...]
     sent = []
     for turn_of in range(slices):
         finish(copies[turn_of])
@@ -353,12 +525,14 @@
         grad_pre = (grad_act * slope).astype(bf16)
         up_g[turn_of] = mm(hidden_t, grad_pre).astype(bf16)
         down_g[turn_of] = mm(grad_t, act).astype(bf16)
-        sent += put(table, up_g.at[turn_of], grads, sems_out, (turn_of * size, size), 2 * turn_of * block_count)
-        sent += put(table, down_g.at[turn_of], grads, sems_out, (total + turn_of * size, size), (2 * turn_of + 1) * block_count)
+        sent += put(grad_table, up_g.at[turn_of], grads, sems_out, (turn_of * size, size), 2 * turn_of * block_count)
+        sent += put(grad_table, down_g.at[turn_of], grads, sems_out, (total + turn_of * size, size), (2 * turn_of + 1) * block_count)
         out = out + mm_nt(act, down_w[turn_of])
         back = back + mm_nt(grad_pre, up_w[turn_of])
-    part[...] = out.astype(bf16)
-    dh_out[...] = back.astype(bf16)
+    part[...] = out
+    mine[...] = x_out[here, :] + part[here, :]
+    other[...] = part[there, :].astype(bf16)
+    dh_out[...] = back.astype(dh_out.dtype)
     finish(sent)
 
 
@@ -416,13 +590,13 @@
     dh_out[...] = mm_nt(dq_out[...], in_w[...]).astype(bf16)
 
 
-def cross_weights(count, table, low_ref, o_ref, h_ref, dq_ref, pool_ref, dk_ref, dv_ref, *refs):
+def cross_weights(count, grad_count, table, side, low_ref, o_ref, h_ref, dq_ref, pool_ref, dk_ref, dv_ref, *refs):
     pieces, refs = refs[:count], refs[count:]
-    pool_out = refs[0]
-    grads, refs = refs[1 : 1 + count], refs[1 + count :]
-    weights, made, sems, sems_out = refs
+    pool_out, pool_other = refs[:2]
+    grads, refs = refs[2 : 2 + grad_count], refs[2 + grad_count :]
+    weights, made, full, sems, sems_out = refs
     width = dq_ref.shape[1]
-    block_count = max(1, 2 * count) if count > 1 else 1
+    block_count = table.shape[0] if count > 1 else 1
     copies = fetch(table, pieces, weights, sems, (width, 2 * width))
     made[3] = mm_tn(low_ref[...], o_ref[...]).astype(bf16)
     made[0] = mm_tn(h_ref[...], dq_ref[...]).astype(bf16)
@@ -433,7 +607,10 @@
     for part in range(4):
         sent += put(table, made.at[part], grads, sems_out, (part * width, width), part * block_count)
     finish(copies)
-    pool_out[...] = (mm_nt(dk_ref[...], weights[:, :width]) + mm_nt(dv_ref[...], weights[:, width:])).astype(bf16)
+    full[...] = mm_nt(dk_ref[...], weights[:, :width]) + mm_nt(dv_ref[...], weights[:, width:])
+    half = pool_out.shape[0]
+    pool_out[...] = full[pl.ds(pl.multiple_of(side[0] * half, half), half), :].astype(bf16)
+    pool_other[...] = full[pl.ds(pl.multiple_of((1 - side[0]) * half, half), half), :].astype(bf16)
     finish(sent)
 
 
@@ -472,11 +649,11 @@
     ).astype(bf16)
 
 
-def self_weights(count, table, low_ref, o_ref, h_ref, dq_ref, dk_ref, dv_ref, *refs):
-    grads, refs = refs[:count], refs[count:]
-    made, sems_out = refs
+def self_weights(count, grad_count, table, low_ref, o_ref, h_ref, dq_ref, dk_ref, dv_ref, one_ref, two_ref, three_ref, *refs):
+    grads, refs = refs[:grad_count], refs[grad_count:]
+    made, norms, sems_out, sems_norm = refs
     width = dq_ref.shape[1]
-    block_count = max(1, 2 * count) if count > 1 else 1
+    block_count = table.shape[0] if grad_count > 1 else 1
     made[3] = mm_tn(low_ref[...], o_ref[...]).astype(bf16)
     hidden_t = h_ref[...].T
     made[0] = mm(hidden_t, dq_ref[...]).astype(bf16)
@@ -485,13 +662,18 @@
     sent = []
     for part in range(4):
         sent += put(table, made.at[part], grads, sems_out, (part * width, width), part * block_count)
+    sums = [one_ref[:2], two_ref[:2], three_ref[:2], jnp.zeros((LANES - NORMS, one_ref.shape[1]), f32)]
+    norms[...] = jnp.concatenate(sums, axis=0).T.astype(bf16)
+    sent += put(table, norms, grads, sems_norm, (4 * width, LANES))
     finish(sent)
 
 
-def input_back(dx_ref, x_ref, norms, own_ref, got_ref, dx_out, sums_out):
+def input_back(side, dx_ref, x_ref, norms, own_ref, got_ref, dx_out, sums_out, full):
     normal, scale = norm_parts(wide(x_ref[...]))
     grad = wide(own_ref[...]) + wide(got_ref[...])
-    dx_out[...] = dx_ref[...] + norm_back(grad, normal, scale, norms[0:1])
+    full[...] = dx_ref[...] + norm_back(grad, normal, scale, norms[0:1])
+    half = dx_out.shape[0]
+    dx_out[...] = full[pl.ds(pl.multiple_of(side[0] * half, half), half), :]
     sums_out[0:1] = jnp.sum(grad * normal, axis=0, keepdims=True)
     sums_out[1:2] = jnp.sum(grad, axis=0, keepdims=True)
 
@@ -499,21 +681,27 @@
 SMEM = pl.BlockSpec(memory_space=pltpu.SMEM)
 VMEM = pl.BlockSpec(memory_space=pltpu.VMEM)
 ANY = pl.BlockSpec(memory_space=pl.ANY)
-
-
-def call(body, name, scalars, arrays, pieces, outs, grads, scratch, flops):
-    shapes = [jax.ShapeDtypeStruct(shape, dtype) for shape, dtype in list(outs) + list(grads)]
-    moved = sum(a.size * a.dtype.itemsize for a in list(arrays) + list(pieces))
-    moved += sum(int(np.prod(s.shape)) * s.dtype.itemsize for s in shapes)
+HBM = pl.BlockSpec(memory_space=pltpu.HBM)
+
+
+def cost(microseconds):
+    return pl.CostEstimate(flops=int(microseconds * 3.85e+08), bytes_accessed=0, transcendentals=0)
+
+
+def call(body, name, scalars, arrays, pieces, outs, grads, scratch, microseconds, mib=60, gate=()):
+    if gate:
+        arrays = list(tie(arrays, gate))
+    shapes = [pltpu.VMEM(*out[:2]) if len(out) > 2 else jax.ShapeDtypeStruct(*out) for out in outs]
+    shapes += [pltpu.HBM(shape, dtype) for shape, dtype in grads]
     return pl.pallas_call(
         body,
         name=name,
         out_shape=shapes,
         in_specs=[SMEM] * len(scalars) + [VMEM] * len(arrays) + [ANY] * len(pieces),
-        out_specs=[VMEM] * len(outs) + [ANY] * len(grads),
+        out_specs=[VMEM] * len(outs) + [HBM] * len(grads),
         scratch_shapes=scratch,
-        compiler_params=pltpu.CompilerParams(vmem_limit_bytes=VMEM_BYTES),
-        cost_estimate=pl.CostEstimate(flops=int(flops), bytes_accessed=int(moved), transcendentals=0),
+        compiler_params=pltpu.CompilerParams(vmem_limit_bytes=mib * MIB),
+        cost_estimate=cost(microseconds),
     )(*scalars, *arrays, *pieces)
 
 
@@ -529,8 +717,31 @@
 
 
 def dma_sems(count, uses=1):
-    blocks = 2 * count if count > 1 else 1
+    blocks = BLOCKS if count > 1 else 1
     return pltpu.SemaphoreType.DMA((blocks * uses,))
+
+
+def pack(*columns):
+    return jnp.concatenate([column.astype(bf16) for column in columns], axis=1)
+
+
+def pack_kernel(*refs):
+    norms, (query, key, value, out_w, packed) = refs[:NORMS], refs[NORMS:]
+    rows, width = query.shape
+    lines = [norm[...] for norm in norms] + [jnp.zeros((LANES - NORMS, rows), f32)]
+    packed[:, :LANES] = jnp.concatenate(lines, axis=0).T.astype(bf16)
+    for place, ref in enumerate((query, key, value)):
+        packed[:, LANES + place * width : LANES + (place + 1) * width] = ref[...].astype(bf16)
+    packed[:, LANES + 3 * width :] = out_w[...].T.astype(bf16)
+
+
+def pack_self(norms, query, key, value, out_w, fast):
+    if not fast:
+        lines = jnp.pad(jnp.stack(norms, axis=1), ((0, 0), (0, LANES - NORMS)))
+        return pack(lines, query, key, value, out_w.T)
+    lines = [norm.reshape(1, -1) for norm in norms]
+    shape = (query.shape[0], LANES + 4 * query.shape[1])
+    return call(pack_kernel, "pack_self", [], lines + [query, key, value, out_w], [], [(shape, bf16)], [], [], 2, mib=60)[0]
 
 
 def on_device(count, inputs, neighbours, nbr_index, ln1_gain, ln1_bias, ln2_gain, ln2_bias, ln3_gain, ln3_bias,
@@ -539,28 +750,38 @@
     shard_rows = w_query.shape[0]
     model = shard_rows * count
     rows = 2 * inputs.shape[0]
-    norms = jnp.stack([ln1_gain, ln1_bias, ln2_gain, ln2_bias, ln3_gain, ln3_bias], axis=1)
-    norms = jnp.pad(norms, ((0, 0), (0, LANES - NORMS)))
-
-    def pack(*columns):
-        return jnp.concatenate([column.astype(bf16) for column in columns], axis=1)
-
-    self_w = gather_pieces(pack(norms, w_query, w_key, w_value, w_out.T), count)
-    cross_w = gather_pieces(pack(c_query, c_key, c_value, c_out.T), count)
-    ff_w = gather_pieces(pack(w_up, w_down.T), count)
-    pieces = len(self_w)
-    if pieces > 1:
-        table = jnp.asarray(block_tables(count))[lax.axis_index("dp")]
-    else:
-        table = jnp.zeros((1,), jnp.int32)
-    grad_rows = (2 * shard_rows) if pieces > 1 else model
-
-    def bind(body, *extra):
-        return functools.partial(body, pieces, *extra)
+    norms = [ln1_gain, ln1_bias, ln2_gain, ln2_bias, ln3_gain, ln3_bias]
 
     stream = join_cores(inputs)
     cot = join_cores(cotangent)
     pool = join_cores(neighbours.reshape(-1, neighbours.shape[-1]))
+    down_t = w_down.T
+    part_hidden = hidden // 2
+    cuts = [slice(0, part_hidden), slice(part_hidden, hidden)]
+    self_w, cross_w, *ff_w, gate_self, gate_pool, gate_cross = gather_all(
+        pack_self(norms, w_query, w_key, w_value, w_out, pieces_ok(count, shard_rows)),
+        pack(c_query, c_key, c_value, c_out.T),
+        pack(w_up[:, cuts[0]], down_t[:, cuts[0]]),
+        pack(w_up[:, cuts[1]], down_t[:, cuts[1]]),
+        count,
+        (stream, cot, pool),
+    )
+    ff_w = ff_w[::-1]
+    side = lax.axis_index("tensor").astype(jnp.int32).reshape(1)
+    pieces = len(self_w)
+    if pieces > 1:
+        tables = jnp.asarray(block_tables(count))
+        table, flat_table = (tables[i][lax.axis_index("dp")] for i in range(2))
+        grad_rows = [shard_rows * blocks for blocks in (4, 4, 4, 2, 2)]
+        flat_rows = [shard_rows * PLANES] * 4
+    else:
+        table = flat_table = jnp.zeros((1,), jnp.int32)
+        grad_rows = flat_rows = [model]
+    grad_count = len(grad_rows)
+
+    def bind(body, *extra):
+        return functools.partial(body, pieces, *extra)
+
     pool_rows = pool.shape[0]
     chosen = nbr_index.reshape(-1)
     cosine, sine = rope_tables(rows)
@@ -569,80 +790,95 @@
     tall, low = ((rows, model), f32), ((rows, model), bf16)
     slim = ((rows, width), bf16)
     rank8 = ((8, model), f32)
-    dense = 2 * rows * model * width
+    half_tall, half_low = ((rows // 2, model), f32), ((rows // 2, model), bf16)
+
+    def kept(out):
+        return out
+
 
     part, h_one, queries, keys, values, attend, mixture, norm_rows = call(
         bind(self_forward), "self_forward", [table], [stream, cosine, sine], self_w,
-        [low, low, slim, slim, slim, ((pairs, 2 * rows, rows), bf16), slim, rank8], [],
-        [pltpu.VMEM((model, LANES + 4 * width), bf16), dma_sems(pieces)], 4 * dense)
+        [low, kept(low), kept(slim), kept(slim), kept(slim), kept(((pairs, 2 * rows, rows), bf16)), kept(slim), rank8], [],
+        [pltpu.VMEM((model, LANES + 4 * width), bf16), dma_sems(pieces)], 8, mib=60, gate=gate_self)
     got = swap_cores(part)
     ckeys, cvalues = call(
         bind(pool_forward), "pool_forward", [table], [pool], cross_w,
-        [((pool_rows, width), bf16)] * 2, [],
-        [pltpu.VMEM((model, 2 * width), bf16), dma_sems(pieces)], 4 * pool_rows * model * width)
+        [kept(((pool_rows, width), bf16))] * 2, [],
+        [pltpu.VMEM((model, 2 * width), bf16), dma_sems(pieces)], 3, mib=60, gate=gate_pool)
     part, after_self, h_two, cqueries, cattend, cmixture = call(
         bind(cross_forward), "cross_forward", [table, chosen], [stream, part, got, norm_rows, ckeys, cvalues], cross_w,
-        [low, tall, low, slim, ((blocks * pairs, 2 * GROUP, NBRS * NBR_LEN), bf16), slim], [],
-        [pltpu.VMEM((model, width), bf16), pltpu.VMEM((model, width), bf16), dma_sems(pieces), dma_sems(pieces)], 2 * dense)
+        [low, kept(tall), kept(low), kept(slim), kept(((blocks * pairs, 2 * GROUP, NBRS * NBR_LEN), bf16)), kept(slim)], [],
+        [pltpu.VMEM((model, width), bf16), pltpu.VMEM((model, width), bf16), dma_sems(pieces), dma_sems(pieces)], 6, mib=60, gate=gate_cross)
     got = swap_cores(part)
-    slices = 3
-    size = hidden // slices
-    part, after_cross, grad_part, *ff_grads = call(
-        bind(feed_forward, slices), "feed_forward", [table], [after_self, part, got, norm_rows, cot], ff_w,
-        [low, tall, low], [((grad_rows, 2 * hidden), bf16)] * pieces,
-        [pltpu.VMEM((slices, model, size), bf16)] * 4 + [dma_sems(pieces, 2 * slices)] * 2, 12 * rows * model * hidden)
+    slices = 2
+    size = part_hidden // slices
+    out, back = jnp.zeros((rows, model), f32), jnp.zeros((rows, model), f32)
+    ff_grads = []
+    forms = [(flat_table, flat_table, flat_rows, tall, ()), (table, table, grad_rows, low, ())]
+    for ff_pieces, (from_table, to_table, to_rows, form, gate) in zip(ff_w, forms):
+        out, after_cross, back, result, result_other, *grads = call(
+            functools.partial(feed_forward, len(ff_pieces), len(to_rows), slices), "feed_forward", [from_table, to_table, side],
+            [after_self, part, got, norm_rows, cot, out, back], ff_pieces,
+            [tall, kept(tall), form, half_tall, half_low], [((count_of, 2 * part_hidden), bf16) for count_of in to_rows],
+            [pltpu.VMEM((slices, model, size), bf16)] * 4 + [dma_sems(pieces, 2 * slices)] * 2, 10, mib=60, gate=gate)
+        ff_grads.append(grads)
+    grad_part = back
     got = swap_cores(grad_part)
-    d_ff = reduce_pieces(ff_grads, count)
-    here = lax.axis_index("tensor") * inputs.shape[0]
-    there = inputs.shape[0] - here
-
-    def part_of(array, start, size):
-        return lax.dynamic_slice_in_dim(array, start, size, 0)
-
-    result = part_of(after_cross, here, inputs.shape[0]) + (
-        wide(part_of(part, here, inputs.shape[0])) + wide(swap_cores(part_of(part, there, inputs.shape[0])))
-    )
+    ff_widths, ff_turned = [part_hidden] * 2, [False, True]
+    one = FlatReduction(ff_grads[0], count, ff_widths, ff_turned)
+    two = Reduction(ff_grads[1], count, ff_widths, ff_turned)
+    one.near()
+    two.diagonal()
+    two.plane()
+    one.far()
     acc = pltpu.VMEM((pool_rows, width), f32)
     grad_cross, low_cross, grad_part, dcq, dck, dcv, sums_three = call(
         bind(cross_back), "cross_back", [table, chosen],
         [cot, after_cross, norm_rows, grad_part, got, cattend, cmixture, cqueries, ckeys, cvalues], cross_w,
         [tall, low, low, slim, ((pool_rows, width), bf16), ((pool_rows, width), bf16), rank8], [],
-        [pltpu.VMEM((model, width), bf16), pltpu.VMEM((model, width), bf16), acc, acc, dma_sems(pieces), dma_sems(pieces)], 3 * dense)
+        [pltpu.VMEM((model, width), bf16), pltpu.VMEM((model, width), bf16), acc, acc, dma_sems(pieces), dma_sems(pieces)], 8, mib=60, gate=(one.got_across,) if pieces > 1 else ())
     got = swap_cores(grad_part)
-    pool_part, *cross_grads = call(
-        bind(cross_weights), "cross_weights", [table], [low_cross, cmixture, h_two, dcq, pool, dck, dcv], cross_w,
-        [((pool_rows, model), bf16)], [((grad_rows, 4 * width), bf16)] * pieces,
-        [pltpu.VMEM((model, 2 * width), bf16), pltpu.VMEM((4, model, width), bf16), dma_sems(pieces), dma_sems(pieces, 4)],
-        2 * dense + 8 * pool_rows * model * width)
-    d_cross = reduce_pieces(cross_grads, count)
+    pool_part, pool_other, *cross_grads = call(
+        bind(cross_weights, grad_count), "cross_weights", [table, side], [low_cross, cmixture, h_two, dcq, pool, dck, dcv], cross_w,
+        [((pool_rows // 2, model), bf16)] * 2, [((count_of, 4 * width), bf16) for count_of in grad_rows],
+        [pltpu.VMEM((model, 2 * width), bf16), pltpu.VMEM((4, model, width), bf16), pltpu.VMEM((pool_rows, model), f32), dma_sems(pieces), dma_sems(pieces, 4)],
+        8, mib=60, gate=(one.got_own,) if pieces > 1 else ())
     grad_self, low_self, grad_part, dq, dk, dv, sums_two = call(
         bind(self_back), "self_back", [table],
         [grad_cross, after_self, norm_rows, grad_part, got, attend, mixture, queries, keys, values, cosine, sine], self_w,
         [tall, low, low, slim, slim, slim, rank8], [],
-        [pltpu.VMEM((model, 4 * width), bf16), dma_sems(pieces)], 5 * dense)
+        [pltpu.VMEM((model, 4 * width), bf16), dma_sems(pieces)], 7, mib=60, gate=tuple(two.sides) + (one.across,) if pieces > 1 else ())
     got = swap_cores(grad_part)
+    three = Reduction(cross_grads, count, [width] * 4, [False] * 3 + [True])
+    three.diagonal()
+    grad_input, sums_one = call(
+        input_back, "input_back", [side], [grad_self, stream, norm_rows, grad_part, got], [], [half_tall, rank8], [],
+        [pltpu.VMEM((rows, model), f32)], 2, mib=60)
     self_grads = call(
-        bind(self_weights), "self_weights", [table], [low_self, mixture, h_one, dq, dk, dv], [],
-        [], [((grad_rows, 4 * width), bf16)] * pieces,
-        [pltpu.VMEM((4, model, width), bf16), dma_sems(pieces, 4)], 4 * dense)
-    d_self = reduce_pieces(self_grads, count)
-    grad_input, sums_one = call(
-        input_back, "input_back", [], [grad_self, stream, norm_rows, grad_part, got], [], [tall, rank8], [], [], rows * model)
-    grad_input = part_of(grad_input, here, inputs.shape[0])
-    pool_half = pool_rows // 2
-    pool_here = lax.axis_index("tensor") * pool_half
-    grad_pool = wide(part_of(pool_part, pool_here, pool_half)) + wide(
-        swap_cores(part_of(pool_part, pool_half - pool_here, pool_half))
-    )
-    sums = jnp.concatenate([sums_one[:2], sums_two[:2], sums_three[:2], jnp.zeros((2, model), f32)], axis=0)
-    sums = sum_small(sums, count)
-    mine = lax.dynamic_slice_in_dim(sums, lax.axis_index("dp") * shard_rows, shard_rows, 1)
-
-    def cut(array, index, size):
-        return array[:, index * size : (index + 1) * size]
-
+        functools.partial(self_weights, pieces, grad_count), "self_weights", [table],
+        [low_self, mixture, h_one, dq, dk, dv, sums_one, sums_two, sums_three], [],
+        [], [((count_of, 4 * width + LANES), bf16) for count_of in grad_rows],
+        [pltpu.VMEM((4, model, width), bf16), pltpu.VMEM((model, LANES), bf16), dma_sems(pieces, 4), dma_sems(pieces)], 4,
+        mib=60, gate=two.ended)
+    four = Reduction(self_grads, count, [width] * 4 + [8], [False] * 3 + [True] * 2)
+    two.near()
+    four.diagonal()
+    three.plane()
+    four.plane(one.ended + two.ended)
+    one.diagonal()
+    three.near()
+    two.far(three.ended[:0])
+    one.plane(three.ended)
+    four.near()
+    three.far(one.ended)
+    four.far()
+    d_ff, d_cross, d_self = [one.outs, two.outs], three.outs, four.outs
+    d_up = jnp.concatenate([part_of_ff[0] for part_of_ff in d_ff[::-1]], axis=1)
+    d_down = jnp.concatenate([part_of_ff[1] for part_of_ff in d_ff[::-1]], axis=0)
+    grad_pool = wide(pool_part) + wide(swap_cores(pool_other))
+    mine = d_self[4]
     return (
-        result.astype(bf16),
+        (result + wide(swap_cores(result_other))).astype(bf16),
         grad_input,
         grad_pool.reshape(neighbours.shape),
         mine[0],
@@ -651,16 +887,12 @@
         mine[3],
         mine[4],
         mine[5],
-        cut(d_self, 0, width),
-        cut(d_self, 1, width),
-        cut(d_self, 2, width),
-        cut(d_cross, 0, width),
-        cut(d_cross, 1, width),
-        cut(d_cross, 2, width),
-        cut(d_ff, 0, hidden),
-        cut(d_self, 3, width).T,
-        cut(d_cross, 3, width).T,
-        cut(d_ff, 1, hidden).T,
+        *d_self[:3],
+        *d_cross[:3],
+        d_up,
+        d_self[3],
+        d_cross[3],
+        d_down,
     )
 
 

time: 341 us -> 272 us (0.80)
  waiting for transfers between devices: 143 us -> 62.6 us
  Pallas kernels: 47.7 us -> 111 us
  starting transfers between devices: 99.1 us -> 63 us
  local copies, waits for them, and re-layouts: 28.8 us -> 22.5 us
  other arithmetic: 15.2 us -> 10.1 us
    ppermute x58 -> x54, waiting for transfers between devices: 141 us -> 62.6 us  [the longest x30 41.5 us: go(): out.append(lax.ppermute(array, 'dp', self.perms[name]))]
    pallas_call x9 -> x24, Pallas kernels: 47.7 us -> 101 us  [call(): pl.pallas_call(body, name=name, out_shape=shapes, in_specs=[SMEM] * len(s...]
    ppermute x58 -> x54, starting transfers between devices: 97.3 us -> 61.9 us  [the longest x30 34.5 us: go(): out.append(lax.ppermute(array, 'dp', self.perms[name]))]
    pallas_call x0 -> x3, Pallas kernels: none -> 9.17 us  [diagonal(): pl.pallas_call(add_diagonal, name='add_diagonal', out_shape=[pltpu.HBM(x_...]
    unnamed x170 -> x134, local copies, waits for them, and re-layouts: 22.8 us -> 14.8 us
    convert_element_type x6 -> x4, other arithmetic: 4.76 us -> 0.03 us  [pack(): return jnp.concatenate([column.astype(bf16) for column in columns], axis=1)]
  transfers between devices with their start and end apart: 68 -> 64, of which waited for: 28 -> 21; matrix products, arithmetic and copies ran while one was open for 5% -> 6% of each run, Pallas kernels for 10% -> 40%
where the time goes in v3:
time: 272 us; the launch traced here: 270 us
  Pallas kernels  111 us (41%)
  starting transfers between devices  63 us (23%)
  waiting for transfers between devices  62.6 us (23%)
  local copies, waits for them, and re-layouts  22.5 us (8%)
  other arithmetic  10.1 us (4%)
    pallas_call x24, Pallas kernels, call(): pl.pallas_call(body, name=name, out_shape=shapes, in_specs=[SMEM] * len(s...  101 us
    ppermute x30, waiting for transfers between devices, go(): out.append(lax.ppermute(array, 'dp', self.perms[name]))  41.5 us
    ppermute x30, starting transfers between devices, go(): out.append(lax.ppermute(array, 'dp', self.perms[name]))  34.5 us
    ppermute x24, starting transfers between devices, send(): out.append(lax.ppermute(array, 'dp', self.perms[name]))  27.5 us
    ppermute x24, waiting for transfers between devices, send(): out.append(lax.ppermute(array, 'dp', self.perms[name]))  21.1 us
    unnamed x134, local copies, waits for them, and re-layouts  14.8 us
    pallas_call x3, Pallas kernels, diagonal(): pl.pallas_call(add_diagonal, name='add_diagonal', out_shape=[pltpu.HBM(x_...  9.17 us
  transfers between devices with their start and end apart: 64, of which 21 were waited for; matrix products, arithmetic and copies ran while one was open for 6% of the time, Pallas kernels for 40%

profile of v3, /device:TPU:0, one launch (start us, length us, event | category | flops | bytes accessed | tf_op | source)
XLA Modules:
  0.0 270.3 jit_solution(13702253892006035387)
XLA Ops:
  2.7 3.0 %collective-permute-start.4 = (bf16[48,1536]{1,0:T(8,128)(2,1)S(1)}, bf16[48,1536]{1,0:T(8,128)(2,1)S(1)}, u32[]{:S(2)}, u32[]{:S(2)}) collective-permute-start(bf16[48,1536]{1,0:T(8,128)(2,1)S(1)} %pad_maximum_fusion.10), channel_id=1, source_target_pairs={{0,4},{2,6},{4,0},{6,2},{8,12},{10,14},{12,8},{14,10},{16,20},{18,... | collective-permute-start | bytes 442376 | tf_op jit(solution)/shard_map/ppermute | solution.py:81
  10.0 2.6 collective-permute-start.1
  14.0 5.9 %collective-permute-done.1 = bf16[48,1664]{1,0:T(8,128)(2,1)S(1)} collective-permute-done((bf16[48,1664]{1,0:T(8,128)(2,1)}, bf16[48,1664]{1,0:T(8,128)(2,1)S(1)}, u32[]{:S(2)}, u32[]{:S(2)}) %collective-permute-start.1) | collective-permute-done | bytes 159776 | tf_op jit(solution)/shard_map/ppermute | solution.py:81
  24.3 3.3 %collective-permute-start.2 = (bf16[48,1536]{1,0:T(8,128)(2,1)S(1)}, bf16[48,1536]{1,0:T(8,128)(2,1)S(1)}, u32[]{:S(2)}, u32[]{:S(2)}) collective-permute-start(bf16[48,1536]{1,0:T(8,128)(2,1)S(1)} %pad_maximum_fusion.9), channel_id=1, source_target_pairs={{0,16},{2,18},{4,20},{6,22},{8,24},{10,26},{12,28},{14,30},{16,0},... | collective-permute-start | bytes 442376 | tf_op jit(solution)/shard_map/ppermute | solution.py:81
  29.5 5.0 %collective-permute-done.11.refs_1_ = bf16[96,1664]{1,0:T(8,128)(2,1)S(1)} collective-permute-done((bf16[96,1664]{1,0:T(8,128)(2,1)S(1)}, bf16[96,1664]{1,0:T(8,128)(2,1)S(1)}, u32[]{:S(2)}, u32[]{:S(2)}) %collective-permute-start.11) | collective-permute-done | bytes 319520 | tf_op jit(solution)/shard_map/ppermute | solution.py:81
  46.2 2.5 collective-permute-done.5.refs_1_
  52.8 2.9 %collective-permute-start.25 = (bf16[192,1536]{1,0:T(8,128)(2,1)S(1)}, bf16[192,1536]{1,0:T(8,128)(2,1)S(1)}, u32[]{:S(2)}, u32[]{:S(2)}) collective-permute-start(bf16[192,1536]{1,0:T(8,128)(2,1)S(1)} %pad_maximum_fusion.1.refs_0_), channel_id=1, source_target_pairs={{0,16},{2,18},{4,20},{6,22},{8,24},{10,26},{12,28},{14,30},{16,0},... | collective-permute-start | bytes 1769480 | tf_op jit(solution)/shard_map/ppermute | solution.py:81
  55.8 3.0 %collective-permute-done.10.refs_5_ = bf16[96,1536]{1,0:T(8,128)(2,1)S(1)} collective-permute-done((bf16[96,1536]{1,0:T(8,128)(2,1)}, bf16[96,1536]{1,0:T(8,128)(2,1)S(1)}, u32[]{:S(2)}, u32[]{:S(2)}) %collective-permute-start.10) | collective-permute-done | bytes 294944 | tf_op jit(solution)/shard_map/ppermute | solution.py:81
  62.4 4.6 %collective-permute-done.19.refs_6_ = bf16[96,1664]{1,0:T(8,128)(2,1)S(1)} collective-permute-done((bf16[96,1664]{1,0:T(8,128)(2,1)S(1)}, bf16[96,1664]{1,0:T(8,128)(2,1)S(1)}, u32[]{:S(2)}, u32[]{:S(2)}) %collective-permute-start.19) | collective-permute-done | bytes 319520 | tf_op jit(solution)/shard_map/ppermute | solution.py:81
  67.7 6.4 %self_forward.1 = (bf16[256,768]{1,0:T(8,128)(2,1)}, bf16[256,768]{1,0:T(8,128)(2,1)}, bf16[256,384]{1,0:T(8,128)(2,1)}, bf16[256,384]{1,0:T(8,128)(2,1)}, bf16[...) custom-call(s32[16]{0:T(128)} %dynamic-slice_bitcast_fusion.1.table.grad_table,, ...), custom_call_target="tpu_custom_call" | custom-call | flops 3080000000 | tf_op jit(solution)/shard_map/self_forward/pallas_call | solution.py:696
  74.3 4.6 %collective-permute-done.25.refs_1_ = bf16[192,1536]{1,0:T(8,128)(2,1)S(1)} collective-permute-done((bf16[192,1536]{1,0:T(8,128)(2,1)S(1)}, bf16[192,1536]{1,0:T(8,128)(2,1)S(1)}, u32[]{:S(2)}, u32[]{:S(2)}) %collective-permute-start.25) | collective-permute-done | bytes 589856 | tf_op jit(solution)/shard_map/ppermute | solution.py:81
  82.5 5.0 %pool_forward.1 = (bf16[768,384]{1,0:T(8,128)(2,1)}, bf16[768,384]{1,0:T(8,128)(2,1)}) custom-call(s32[16]{0:T(128)} %dynamic-slice_bitcast_fusion.1.table.grad_table, bf16[768,768]{1,0:T(8,128)(2,1)} %pad_maximum_fusion.pool_ref, bf16[96,1536]{1,0:T(8,128)(2,1)} %copy-done.7, bf16[96,1536]{1,0:T(8,128)(2,1)} %collective-permute-done.5.refs_1_, ...), custom_call_target="tpu_custom_call" | custom-call | flops 1155000064 | tf_op jit(solution)/shard_map/pool_forward/pallas_call | solution.py:696
  90.5 6.2 %cross_forward.1 = (bf16[256,768]{1,0:T(8,128)(2,1)}, f32[256,768]{1,0:T(8,128)}, bf16[256,768]{1,0:T(8,128)(2,1)}, bf16[256,384]{1,0:T(8,128)(2,1)}, bf16[12,12...) custom-call(s32[16]{0:T(128)} %dynamic-slice_bitcast_fusion.1.table.grad_table, s32[8]{0:T(128)} %reshape.73.chosen, ...), custom_call_target="tpu_custom_call" | custom-call | flops 2310000128 | tf_op jit(solution)/shard_map/cross_forward/pallas_call | solution.py:696
  100.5 5.7 %collective-permute-done.31.refs_3_ = bf16[96,1536]{1,0:T(8,128)(2,1)S(1)} collective-permute-done((bf16[96,1536]{1,0:T(8,128)(2,1)S(1)}, bf16[96,1536]{1,0:T(8,128)(2,1)S(1)}, u32[]{:S(2)}, u32[]{:S(2)}) %collective-permute-start.31) | collective-permute-done | bytes 294944 | tf_op jit(solution)/shard_map/ppermute | solution.py:81
  109.6 10.3 %feed_forward.2 = (f32[256,768]{1,0:T(8,128)}, f32[256,768]{1,0:T(8,128)}, f32[256,768]{1,0:T(8,128)}, f32[128,768]{1,0:T(8,128)}, bf16[128,768]{1,0:T(8,128)(2,...) custom-call(s32[16]{0:T(128)} %dynamic-slice_bitcast_fusion.table.gr, ...), custom_call_target="tpu_custom_call" | custom-call | flops 3849999872 | tf_op jit(solution)/shard_map/feed_forward/pallas_call | solution.py:696
  121.3 10.1 %feed_forward.3 = (f32[256,768]{1,0:T(8,128)}, f32[256,768]{1,0:T(8,128)}, bf16[256,768]{1,0:T(8,128)(2,1)}, f32[128,768]{1,0:T(8,128)}, bf16[128,768]{1,0:T(8,1...) custom-call(s32[16]{0:T(128)} %dynamic-slice_bitcast_fusion.1.table., ...), custom_call_target="tpu_custom_call" | custom-call | flops 3849999872 | tf_op jit(solution)/shard_map/feed_forward/pallas_call | solution.py:696
  135.0 6.1 %collective-permute-done.39.from_x = bf16[96,1536]{1,0:T(8,128)(2,1)S(1)} collective-permute-done((bf16[96,1536]{1,0:T(8,128)(2,1)}, bf16[96,1536]{1,0:T(8,128)(2,1)S(1)}, u32[]{:S(2)}, u32[]{:S(2)}) %collective-permute-start.39) | collective-permute-done | bytes 294944 | tf_op jit(solution)/shard_map/ppermute | solution.py:195
  142.4 8.6 %cross_back.1 = (f32[256,768]{1,0:T(8,128)}, bf16[256,768]{1,0:T(8,128)(2,1)}, bf16[256,768]{1,0:T(8,128)(2,1)}, bf16[256,384]{1,0:T(8,128)(2,1)}, bf16[768,384]...) custom-call(s32[16]{0:T(128)} %dynamic-slice_bitcast_fusion.1.table.grad_table, s32[8]{0:T(128)} %reshape.73.chosen, ...), custom_call_target="tpu_custom_call" | custom-call | flops 3080000000 | tf_op jit(solution)/shard_map/cross_back/pallas_call | solution.py:696
  151.1 3.0 %add_diagonal.3 = (bf16[192,1536]{1,0:T(8,128)(2,1)}, bf16[192,1536]{1,0:T(8,128)(2,1)}) custom-call(bf16[192,1536]{1,0:T(8,128)(2,1)} %get-tuple-element.257.x_in, bf16[192,1536]{1,0:T(8,128)(2,1)} %get-tuple-element.258.y_in, bf16[96,1536]{1,0:T(8,128)(2,1)} %copy-done.55, bf16[96,1536]{1,0:T(8,128)(2,1)} %copy-done.56), custom_call_target="tpu_custom_call", output_to_operand_aliasing={{0}: (0, {}), {1}: (1, {})} | custom-call | flops 770000000 | tf_op jit(solution)/shard_map/add_diagonal/pallas_call | solution.py:206
  156.6 10.6 %cross_weights.1 = (bf16[384,768]{1,0:T(8,128)(2,1)}, bf16[384,768]{1,0:T(8,128)(2,1)}, bf16[192,1536]{1,0:T(8,128)(2,1)}, bf16[192,1536]{1,0:T(8,128)(2,1)}, bf...) custom-call(s32[16]{0:T(128)} %dynamic-slice_bitcast_fusion.1.table.grad_table, ...), custom_call_target="tpu_custom_call" | custom-call | flops 3080000000 | tf_op jit(solution)/shard_map/cross_weights/pallas_call | solution.py:696
  172.0 7.3 %self_back.1 = (f32[256,768]{1,0:T(8,128)}, bf16[256,768]{1,0:T(8,128)(2,1)}, bf16[256,768]{1,0:T(8,128)(2,1)}, bf16[256,384]{1,0:T(8,128)(2,1)}, bf16[256,384]{...) custom-call(s32[16]{0:T(128)} %dynamic-slice_bitcast_fusion.1.table.grad_table, ...), custom_call_target="tpu_custom_call" | custom-call | flops 2695000064 | tf_op jit(solution)/shard_map/self_back/pallas_call | solution.py:696
  179.4 3.2 %collective-permute-start.48 = (bf16[192,1536]{1,0:T(8,128)(2,1)S(1)}, bf16[192,1536]{1,0:T(8,128)(2,1)}, u32[]{:S(2)}, u32[]{:S(2)}) collective-permute-start(bf16[192,1536]{1,0:T(8,128)(2,1)S(1)} %copy-done.2), channel_id=1, source_target_pairs={{0,16},{2,18},{4,20},{6,22},{8,24},{10,26},{12,28},{14,30},{16,0},... | collective-permute-start | bytes 1769480 | tf_op jit(solution)/shard_map/ppermute | solution.py:195
  183.4 3.0 %add_diagonal.5 = (bf16[192,1536]{1,0:T(8,128)(2,1)}, bf16[192,1536]{1,0:T(8,128)(2,1)}) custom-call(bf16[192,1536]{1,0:T(8,128)(2,1)} %get-tuple-element.339.x_in, bf16[192,1536]{1,0:T(8,128)(2,1)} %get-tuple-element.340.y_in, bf16[96,1536]{1,0:T(8,128)(2,1)} %copy-done.53, bf16[96,1536]{1,0:T(8,128)(2,1)} %copy-done.54), custom_call_target="tpu_custom_call", output_to_operand_aliasing={{0}: (0, {}), {1}: (1, {})} | custom-call | flops 770000000 | tf_op jit(solution)/shard_map/add_diagonal/pallas_call | solution.py:206
  189.9 2.9 %input_back.1 = (f32[128,768]{1,0:T(8,128)}, f32[8,768]{1,0:T(8,128)}) custom-call(s32[1]{0:T(128)} %bitcast.1.side, f32[256,768]{1,0:T(8,128)} %get-tuple-element.278.dx_ref, bf16[256,768]{1,0:T(8,128)(2,1)} %pad_maximum_fusion.2.x_ref, f32[8,768]{1,0:T(8,128)} %get-tuple-element.268.norms, bf16[256,768]{1,0:T(8,128)(2,1)} %get-tuple-element.279.own_ref, ...), custom_call_target="tpu_custom_call" | custom-call | flops 770000000 | tf_op jit(solution)/shard_map/input_back/pallas_call | solution.py:696
  192.8 4.8 %self_weights.1 = (bf16[192,1664]{1,0:T(8,128)(2,1)}, bf16[192,1664]{1,0:T(8,128)(2,1)}, bf16[192,1664]{1,0:T(8,128)(2,1)}, bf16[96,1664]{1,0:T(8,128)(2,1)}, bf16[96,1664]{1,0:T(8,128)(2,1)}) custom-call(s32[16]{0:T(128)} %dynamic-slice_bitcast_fusion.1.table.grad_table, bf16[256,768]{1,0:T(8,128)(2,1)} %get-tuple-element.306.low_ref, ...), custom_call_target="tpu_custom_call" | custom-call | flops 1540000000 | tf_op jit(solution)/shard_map/self_weights/pallas_call | solution.py:696
  199.2 2.5 add_plane.3
  201.6 7.7 %collective-permute-done.48.got_far = bf16[192,1536]{1,0:T(8,128)(2,1)} collective-permute-done((bf16[192,1536]{1,0:T(8,128)(2,1)S(1)}, bf16[192,1536]{1,0:T(8,128)(2,1)}, u32[]{:S(2)}, u32[]{:S(2)}) %collective-permute-start.48) | collective-permute-done | bytes 589856 | tf_op jit(solution)/shard_map/ppermute | solution.py:195
  210.2 2.3 add_column.1
  214.5 3.1 %add_diagonal.4 = (bf16[192,1664]{1,0:T(8,128)(2,1)}, bf16[192,1664]{1,0:T(8,128)(2,1)}) custom-call(bf16[192,1664]{1,0:T(8,128)(2,1)} %get-tuple-element.316.x_in, bf16[192,1664]{1,0:T(8,128)(2,1)} %get-tuple-element.317.y_in, bf16[96,1664]{1,0:T(8,128)(2,1)} %copy-done.39, bf16[96,1664]{1,0:T(8,128)(2,1)} %copy-done.40), custom_call_target="tpu_custom_call", output_to_operand_aliasing={{0}: (0, {}), {1}: (1, {})} | custom-call | flops 770000000 | tf_op jit(solution)/shard_map/add_diagonal/pallas_call | solution.py:206
  220.9 2.5 add_plane.5
  230.6 3.9 %collective-permute-done.58.got = bf16[96,1536]{1,0:T(8,128)(2,1)S(1)} collective-permute-done((bf16[96,1536]{1,0:T(8,128)(2,1)}, bf16[96,1536]{1,0:T(8,128)(2,1)S(1)}, u32[]{:S(2)}, u32[]{:S(2)}) %collective-permute-start.58) | collective-permute-done | bytes 294944 | tf_op jit(solution)/shard_map/ppermute | solution.py:195
  238.6 2.5 add_plane.4
  (287 shorter events, 113.6 us)
Async XLA Ops:
  13.4 15.4 %collective-permute-start.14 = (bf16[48,1536]{1,0:T(8,128)(2,1)S(1)}, bf16[48,1536]{1,0:T(8,128)(2,1)S(1)}, u32[]{:S(2)}, u32[]{:S(2)}) collective-permute-start(bf16[48,1536]{1,0:T(8,128)(2,1)S(1)} %collective-permute-done.4), channel_id=1, source_target_pairs={{0,2},{2,0},{4,6},{6,4},{8,10},{10,8},{12,14},{14,12},{16,18},{18,... | collective-permute-start | bytes 442376 | tf_op jit(solution)/shard_map/ppermute | solution.py:81
  24.3 13.2 %collective-permute-start.2 = (bf16[48,1536]{1,0:T(8,128)(2,1)S(1)}, bf16[48,1536]{1,0:T(8,128)(2,1)S(1)}, u32[]{:S(2)}, u32[]{:S(2)}) collective-permute-start(bf16[48,1536]{1,0:T(8,128)(2,1)S(1)} %pad_maximum_fusion.9), channel_id=1, source_target_pairs={{0,16},{2,18},{4,20},{6,22},{8,24},{10,26},{12,28},{14,30},{16,0},... | collective-permute-start | bytes 442376 | tf_op jit(solution)/shard_map/ppermute | solution.py:81
  34.5 17.1 %collective-permute-start.18 = (bf16[96,1664]{1,0:T(8,128)(2,1)S(1)}, bf16[96,1664]{1,0:T(8,128)(2,1)S(1)}, u32[]{:S(2)}, u32[]{:S(2)}) collective-permute-start(bf16[96,1664]{1,0:T(8,128)(2,1)S(1)} %collective-permute-done.11.refs_1_), channel_id=1, source_target_pairs={{0,4},{2,6},{4,0},{6,2},{8,12},{10,14},{12,8},{14,10},{16,20},{18,... | collective-permute-start | bytes 958472 | tf_op jit(solution)/shard_map/ppermute | solution.py:81
  36.0 15.6 %collective-permute-start.17 = (bf16[96,1664]{1,0:T(8,128)(2,1)S(1)}, bf16[96,1664]{1,0:T(8,128)(2,1)}, u32[]{:S(2)}, u32[]{:S(2)}) collective-permute-start(bf16[96,1664]{1,0:T(8,128)(2,1)S(1)} %collective-permute-done.11.refs_1_), channel_id=1, source_target_pairs={{0,2},{2,0},{4,6},{6,4},{8,10},{10,8},{12,14},{14,12},{16,18},{18,... | collective-permute-start | bytes 958472 | tf_op jit(solution)/shard_map/ppermute | solution.py:81
  51.6 15.4 %collective-permute-start.19 = (bf16[96,1664]{1,0:T(8,128)(2,1)S(1)}, bf16[96,1664]{1,0:T(8,128)(2,1)S(1)}, u32[]{:S(2)}, u32[]{:S(2)}) collective-permute-start(bf16[96,1664]{1,0:T(8,128)(2,1)S(1)} %collective-permute-done.13.refs_4_), channel_id=1, source_target_pairs={{0,2},{2,0},{4,6},{6,4},{8,10},{10,8},{12,14},{14,12},{16,18},{18,... | collective-permute-start | bytes 958472 | tf_op jit(solution)/shard_map/ppermute | solution.py:81
  52.2 15.2 %collective-permute-start.20 = (bf16[96,1664]{1,0:T(8,128)(2,1)}, bf16[96,1664]{1,0:T(8,128)(2,1)}, u32[]{:S(2)}, u32[]{:S(2)}) collective-permute-start(bf16[96,1664]{1,0:T(8,128)(2,1)} %collective-permute-done.17.refs_3_), channel_id=1, source_target_pairs={{0,4},{2,6},{4,0},{6,2},{8,12},{10,14},{12,8},{14,10},{16,20},{18,... | collective-permute-start | bytes 958472 | tf_op jit(solution)/shard_map/ppermute | solution.py:81
  52.8 26.0 %collective-permute-start.25 = (bf16[192,1536]{1,0:T(8,128)(2,1)S(1)}, bf16[192,1536]{1,0:T(8,128)(2,1)S(1)}, u32[]{:S(2)}, u32[]{:S(2)}) collective-permute-start(bf16[192,1536]{1,0:T(8,128)(2,1)S(1)} %pad_maximum_fusion.1.refs_0_), channel_id=1, source_target_pairs={{0,16},{2,18},{4,20},{6,22},{8,24},{10,26},{12,28},{14,30},{16,0},... | collective-permute-start | bytes 1769480 | tf_op jit(solution)/shard_map/ppermute | solution.py:81
  60.4 19.8 %collective-permute-start.22 = (bf16[96,1536]{1,0:T(8,128)(2,1)}, bf16[96,1536]{1,0:T(8,128)(2,1)S(1)}, u32[]{:S(2)}, u32[]{:S(2)}) collective-permute-start(bf16[96,1536]{1,0:T(8,128)(2,1)} %collective-permute-done.7.refs_4_), channel_id=1, source_target_pairs={{0,2},{2,0},{4,6},{6,4},{8,10},{10,8},{12,14},{14,12},{16,18},{18,... | collective-permute-start | bytes 884744 | tf_op jit(solution)/shard_map/ppermute | solution.py:81
  61.9 19.8 %collective-permute-start.23 = (bf16[96,1536]{1,0:T(8,128)(2,1)}, bf16[96,1536]{1,0:T(8,128)(2,1)}, u32[]{:S(2)}, u32[]{:S(2)}) collective-permute-start(bf16[96,1536]{1,0:T(8,128)(2,1)} %collective-permute-done.9.refs_3_), channel_id=1, source_target_pairs={{0,4},{2,6},{4,0},{6,2},{8,12},{10,14},{12,8},{14,10},{16,20},{18,... | collective-permute-start | bytes 884744 | tf_op jit(solution)/shard_map/ppermute | solution.py:81
  67.0 15.5 %collective-permute-start.24 = (bf16[96,1536]{1,0:T(8,128)(2,1)S(1)}, bf16[96,1536]{1,0:T(8,128)(2,1)S(1)}, u32[]{:S(2)}, u32[]{:S(2)}) collective-permute-start(bf16[96,1536]{1,0:T(8,128)(2,1)S(1)} %pad_maximum_fusion.6.refs_0_), channel_id=1, source_target_pairs={{0,8},{2,10},{4,12},{6,14},{8,0},{10,2},{12,4},{14,6},{16,24},{18,... | collective-permute-start | bytes 884744 | tf_op jit(solution)/shard_map/ppermute | solution.py:81
  74.2 15.5 %collective-permute-start.21 = (bf16[256,768]{1,0:T(8,128)(2,1)}, bf16[256,768]{1,0:T(8,128)(2,1)S(1)}, u32[]{:S(2)}, u32[]{:S(2)}) collective-permute-start(bf16[256,768]{1,0:T(8,128)(2,1)} %get-tuple-element.218.own_ref), channel_id=1, source_target_pairs={{0,1},{1,0},{2,3},{3,2},{4,5},{5,4},{6,7},{7,6},{8,9},{9,8},{10,11... | collective-permute-start | bytes 1179656 | tf_op jit(solution)/shard_map/ppermute | solution.py:292
  81.8 16.3 %collective-permute-start.29 = (bf16[192,1536]{1,0:T(8,128)(2,1)S(1)}, bf16[192,1536]{1,0:T(8,128)(2,1)S(1)}, u32[]{:S(2)}, u32[]{:S(2)}) collective-permute-start(bf16[192,1536]{1,0:T(8,128)(2,1)S(1)} %pad_maximum_fusion.1.refs_0_), channel_id=1, source_target_pairs={{0,8},{2,10},{4,12},{6,14},{8,0},{10,2},{12,4},{14,6},{16,24},{18,... | collective-permute-start | bytes 1769480 | tf_op jit(solution)/shard_map/ppermute | solution.py:81
  87.6 20.9 %collective-permute-start.30 = (bf16[192,1536]{1,0:T(8,128)(2,1)S(1)}, bf16[192,1536]{1,0:T(8,128)(2,1)S(1)}, u32[]{:S(2)}, u32[]{:S(2)}) collective-permute-start(bf16[192,1536]{1,0:T(8,128)(2,1)S(1)} %collective-permute-done.25.refs_1_), channel_id=1, source_target_pairs={{0,8},{2,10},{4,12},{6,14},{8,0},{10,2},{12,4},{14,6},{16,24},{18,... | collective-permute-start | bytes 1769480 | tf_op jit(solution)/shard_map/ppermute | solution.py:81
  99.9 20.5 %collective-permute-start.32 = (bf16[96,1536]{1,0:T(8,128)(2,1)S(1)}, bf16[96,1536]{1,0:T(8,128)(2,1)S(1)}, u32[]{:S(2)}, u32[]{:S(2)}) collective-permute-start(bf16[96,1536]{1,0:T(8,128)(2,1)S(1)} %collective-permute-done.24.refs_1_), channel_id=1, source_target_pairs={{0,4},{2,6},{4,0},{6,2},{8,12},{10,14},{12,8},{14,10},{16,20},{18,... | collective-permute-start | bytes 884744 | tf_op jit(solution)/shard_map/ppermute | solution.py:81
  106.2 14.2 %collective-permute-start.33 = (bf16[96,1536]{1,0:T(8,128)(2,1)}, bf16[96,1536]{1,0:T(8,128)(2,1)S(1)}, u32[]{:S(2)}, u32[]{:S(2)}) collective-permute-start(bf16[96,1536]{1,0:T(8,128)(2,1)} %collective-permute-done.27.refs_4_), channel_id=1, source_target_pairs={{0,2},{2,0},{4,6},{6,4},{8,10},{10,8},{12,14},{14,12},{16,18},{18,... | collective-permute-start | bytes 884744 | tf_op jit(solution)/shard_map/ppermute | solution.py:81
  106.8 13.6 %collective-permute-start.34 = (bf16[96,1536]{1,0:T(8,128)(2,1)S(1)}, bf16[96,1536]{1,0:T(8,128)(2,1)S(1)}, u32[]{:S(2)}, u32[]{:S(2)}) collective-permute-start(bf16[96,1536]{1,0:T(8,128)(2,1)S(1)} %collective-permute-done.31.refs_3_), channel_id=1, source_target_pairs={{0,4},{2,6},{4,0},{6,2},{8,12},{10,14},{12,8},{14,10},{16,20},{18,... | collective-permute-start | bytes 884744 | tf_op jit(solution)/shard_map/ppermute | solution.py:81
  119.9 21.6 %collective-permute-start.37 = (bf16[192,1536]{1,0:T(8,128)(2,1)}, bf16[192,1536]{1,0:T(8,128)(2,1)S(1)}, u32[]{:S(2)}, u32[]{:S(2)}) collective-permute-start(bf16[192,1536]{1,0:T(8,128)(2,1)} %get-tuple-element.239), channel_id=1, source_target_pairs={{0,8},{2,10},{4,12},{6,14},{8,0},{10,2},{12,4},{14,6},{16,24},{18,... | collective-permute-start | bytes 1769480 | tf_op jit(solution)/shard_map/ppermute | solution.py:195
  133.5 23.1 %collective-permute-start.42 = (bf16[192,1536]{1,0:T(8,128)(2,1)S(1)}, bf16[192,1536]{1,0:T(8,128)(2,1)S(1)}, u32[]{:S(2)}, u32[]{:S(2)}) collective-permute-start(bf16[192,1536]{1,0:T(8,128)(2,1)S(1)} %copy-done.26), channel_id=1, source_target_pairs={{0,8},{2,10},{4,12},{6,14},{8,0},{10,2},{12,4},{14,6},{16,24},{18,... | collective-permute-start | bytes 1769480 | tf_op jit(solution)/shard_map/ppermute | solution.py:195
  151.0 20.2 %collective-permute-start.38 = (bf16[256,768]{1,0:T(8,128)(2,1)}, bf16[256,768]{1,0:T(8,128)(2,1)S(1)}, u32[]{:S(2)}, u32[]{:S(2)}) collective-permute-start(bf16[256,768]{1,0:T(8,128)(2,1)} %get-tuple-element.269.own_ref), channel_id=1, source_target_pairs={{0,1},{1,0},{2,3},{3,2},{4,5},{5,4},{6,7},{7,6},{8,9},{9,8},{10,11... | collective-permute-start | bytes 1179656 | tf_op jit(solution)/shard_map/ppermute | solution.py:292
  154.2 33.5 %collective-permute-start.44 = (bf16[192,1536]{1,0:T(8,128)(2,1)}, bf16[192,1536]{1,0:T(8,128)(2,1)S(1)}, u32[]{:S(2)}, u32[]{:S(2)}) collective-permute-start(bf16[192,1536]{1,0:T(8,128)(2,1)} %get-tuple-element.263), channel_id=1, source_target_pairs={{0,2},{2,0},{4,6},{6,4},{8,10},{10,8},{12,14},{14,12},{16,18},{18,... | collective-permute-start | bytes 1769480 | tf_op jit(solution)/shard_map/ppermute | solution.py:195
  155.5 33.6 %collective-permute-start.45 = (bf16[192,1536]{1,0:T(8,128)(2,1)}, bf16[192,1536]{1,0:T(8,128)(2,1)S(1)}, u32[]{:S(2)}, u32[]{:S(2)}) collective-permute-start(bf16[192,1536]{1,0:T(8,128)(2,1)} %get-tuple-element.264), channel_id=1, source_target_pairs={{0,4},{2,6},{4,0},{6,2},{8,12},{10,14},{12,8},{14,10},{16,20},{18,... | collective-permute-start | bytes 1769480 | tf_op jit(solution)/shard_map/ppermute | solution.py:195
  168.2 14.5 %collective-permute-start.55 = (bf16[96,1536]{1,0:T(8,128)(2,1)}, bf16[96,1536]{1,0:T(8,128)(2,1)S(1)}, u32[]{:S(2)}, u32[]{:S(2)}) collective-permute-start(bf16[96,1536]{1,0:T(8,128)(2,1)} %get-tuple-element.342), channel_id=1, source_target_pairs={{0,4},{2,6},{4,0},{6,2},{8,12},{10,14},{12,8},{14,10},{16,20},{18,... | collective-permute-start | bytes 884744 | tf_op jit(solution)/shard_map/ppermute | solution.py:195
  179.4 29.9 %collective-permute-start.48 = (bf16[192,1536]{1,0:T(8,128)(2,1)S(1)}, bf16[192,1536]{1,0:T(8,128)(2,1)}, u32[]{:S(2)}, u32[]{:S(2)}) collective-permute-start(bf16[192,1536]{1,0:T(8,128)(2,1)S(1)} %copy-done.2), channel_id=1, source_target_pairs={{0,16},{2,18},{4,20},{6,22},{8,24},{10,26},{12,28},{14,30},{16,0},... | collective-permute-start | bytes 1769480 | tf_op jit(solution)/shard_map/ppermute | solution.py:195
  186.4 23.0 %collective-permute-start.56 = (bf16[192,1536]{1,0:T(8,128)(2,1)}, bf16[192,1536]{1,0:T(8,128)(2,1)S(1)}, u32[]{:S(2)}, u32[]{:S(2)}) collective-permute-start(bf16[192,1536]{1,0:T(8,128)(2,1)} %get-tuple-element.345), channel_id=1, source_target_pairs={{0,2},{2,0},{4,6},{6,4},{8,10},{10,8},{12,14},{14,12},{16,18},{18,... | collective-permute-start | bytes 1769480 | tf_op jit(solution)/shard_map/ppermute | solution.py:195
  187.7 21.8 %collective-permute-start.57 = (bf16[192,1536]{1,0:T(8,128)(2,1)}, bf16[192,1536]{1,0:T(8,128)(2,1)}, u32[]{:S(2)}, u32[]{:S(2)}) collective-permute-start(bf16[192,1536]{1,0:T(8,128)(2,1)} %get-tuple-element.346), channel_id=1, source_target_pairs={{0,4},{2,6},{4,0},{6,2},{8,12},{10,14},{12,8},{14,10},{16,20},{18,... | collective-permute-start | bytes 1769480 | tf_op jit(solution)/shard_map/ppermute | solution.py:195
  197.6 14.9 %collective-permute-start.46 = (bf16[96,1664]{1,0:T(8,128)(2,1)}, bf16[96,1664]{1,0:T(8,128)(2,1)S(1)}, u32[]{:S(2)}, u32[]{:S(2)}) collective-permute-start(bf16[96,1664]{1,0:T(8,128)(2,1)} %get-tuple-element.318), channel_id=1, source_target_pairs={{0,2},{2,0},{4,6},{6,4},{8,10},{10,8},{12,14},{14,12},{16,18},{18,... | collective-permute-start | bytes 958472 | tf_op jit(solution)/shard_map/ppermute | solution.py:195
  198.5 15.2 %collective-permute-start.47 = (bf16[96,1664]{1,0:T(8,128)(2,1)}, bf16[96,1664]{1,0:T(8,128)(2,1)S(1)}, u32[]{:S(2)}, u32[]{:S(2)}) collective-permute-start(bf16[96,1664]{1,0:T(8,128)(2,1)} %get-tuple-element.319), channel_id=1, source_target_pairs={{0,4},{2,6},{4,0},{6,2},{8,12},{10,14},{12,8},{14,10},{16,20},{18,... | collective-permute-start | bytes 958472 | tf_op jit(solution)/shard_map/ppermute | solution.py:195
  209.4 26.2 %collective-permute-start.43 = (bf16[384,768]{1,0:T(8,128)(2,1)S(1)}, bf16[384,768]{1,0:T(8,128)(2,1)S(1)}, u32[]{:S(2)}, u32[]{:S(2)}) collective-permute-start(bf16[384,768]{1,0:T(8,128)(2,1)S(1)} %copy-done.20), channel_id=1, source_target_pairs={{0,1},{1,0},{2,3},{3,2},{4,5},{5,4},{6,7},{7,6},{8,9},{9,8},{10,11... | collective-permute-start | bytes 1769480 | tf_op jit(solution)/shard_map/ppermute | solution.py:292
  212.5 14.7 %collective-permute-start.60 = (bf16[48,1536]{1,0:T(8,128)(2,1)}, bf16[48,1536]{1,0:T(8,128)(2,1)S(1)}, u32[]{:S(2)}, u32[]{:S(2)}) collective-permute-start(bf16[48,1536]{1,0:T(8,128)(2,1)} %get-tuple-element.357), channel_id=1, source_target_pairs={{0,2},{2,0},{4,6},{6,4},{8,10},{10,8},{12,14},{14,12},{16,18},{18,... | collective-permute-start | bytes 442376 | tf_op jit(solution)/shard_map/ppermute | solution.py:195
  218.4 19.1 %collective-permute-start.51 = (bf16[192,1664]{1,0:T(8,128)(2,1)}, bf16[192,1664]{1,0:T(8,128)(2,1)S(1)}, u32[]{:S(2)}, u32[]{:S(2)}) collective-permute-start(bf16[192,1664]{1,0:T(8,128)(2,1)} %get-tuple-element.327), channel_id=1, source_target_pairs={{0,4},{2,6},{4,0},{6,2},{8,12},{10,14},{12,8},{14,10},{16,20},{18,... | collective-permute-start | bytes 1916936 | tf_op jit(solution)/shard_map/ppermute | solution.py:195
  219.8 17.7 %collective-permute-start.50 = (bf16[192,1664]{1,0:T(8,128)(2,1)}, bf16[192,1664]{1,0:T(8,128)(2,1)S(1)}, u32[]{:S(2)}, u32[]{:S(2)}) collective-permute-start(bf16[192,1664]{1,0:T(8,128)(2,1)} %get-tuple-element.325), channel_id=1, source_target_pairs={{0,2},{2,0},{4,6},{6,4},{8,10},{10,8},{12,14},{14,12},{16,18},{18,... | collective-permute-start | bytes 1916936 | tf_op jit(solution)/shard_map/ppermute | solution.py:195
  227.2 14.4 %collective-permute-start.63 = (bf16[48,1536]{1,0:T(8,128)(2,1)}, bf16[48,1536]{1,0:T(8,128)(2,1)S(1)}, u32[]{:S(2)}, u32[]{:S(2)}) collective-permute-start(bf16[48,1536]{1,0:T(8,128)(2,1)} %get-tuple-element.367), channel_id=1, source_target_pairs={{0,16},{2,18},{4,20},{6,22},{8,24},{10,26},{12,28},{14,30},{16,0},... | collective-permute-start | bytes 442376 | tf_op jit(solution)/shard_map/ppermute | solution.py:195
  (97 other events, 784.4 us)
